TPU v7x, 32 devices: a whole 2x2x4 slice. The times are simulated.
32 devices in a mesh: tok: 8 (over z, y), voc: 4 (over x, core).
Axes of the slice: x: 2, y: 2, z: 4, core: 2. Of those that a mesh axis runs over, the one named last changes fastest.
Arguments:
- teacher_logits: bfloat16 [1024, 76032], P('tok', 'voc'), may hold values from -1000 to 1000
- student_logits: bfloat16 [1024, 76032], P('tok', 'voc'), may hold values from -1000 to 1000
- target_ids: int32 [1024], P('tok'), may hold values from -1 to 76031, as said below
- vocab_used: int32 [76032], replicated, may hold values from 0 to 1
Outputs:
- logit_grad: bfloat16 [1024, 76032], P('tok', 'voc')
- token_loss: float32 [1024], P('tok')
Inputs may be any that keep to these rules, and one draw needn't show every extreme that they name: `target_ids`: every entry that is not -1 names a vocabulary entry v with vocab_used[v] == 1; the first token of every 128 is never -1.
All inputs are finite; a program needn't handle non-finite values.
Results may differ from a plain program's by a relative error of at most 0.0004.
Values may be sent and summed in bfloat16 or wider, within the bound.
No kernel may reach another device: no remote copies, remote signals or barrier semaphores. Data moves between devices by JAX's collectives and lax.ppermute only.
A program may use at most 64 MiB of HBM per device.

v0:
```python
import jax
import jax.numpy as jnp
from jax import lax
from jax.sharding import PartitionSpec as P

SENTINEL = -1e30


def combined_all(value, axis, join):
    pieces = jax.tree.map(lambda part: lax.all_gather(part, axis), value)
    head = jax.tree.map(lambda part: part[0], pieces)
    tail = jax.tree.map(lambda part: part[1:], pieces)
    subtotal, _ = lax.scan(lambda subtotal, slab: (join(subtotal, slab), None), head, tail)
    return subtotal


def local_totals(values, used):
    top_value = jnp.max(jnp.where(used, values, SENTINEL), axis=1)
    total = jnp.sum(jnp.where(used, jnp.exp(values - top_value[:, None]), 0.0), axis=1)
    return (top_value, total)


def merge_pair(first, second):
    top_value = jnp.maximum(first[0], second[0])
    total = first[1] * jnp.exp(first[0] - top_value) + second[1] * jnp.exp(second[0] - top_value)
    return (top_value, total)


def merge_joint(first, second):
    teacher_top = jnp.maximum(first[0], second[0])
    scale_one = jnp.exp(first[0] - teacher_top)
    scale_two = jnp.exp(second[0] - teacher_top)
    student_top, student_sum = merge_pair((first[3], first[4]), (second[3], second[4]))
    return (
        teacher_top,
        first[1] * scale_one + second[1] * scale_two,
        first[2] * scale_one + second[2] * scale_two,
        student_top,
        student_sum,
        first[5] + second[5],
    )


def body(teacher_logits, student_logits, target_ids, vocab_used):
    tok_rows, vocab_cols = teacher_logits.shape
    voc_count = lax.axis_size("voc")
    voc_index = lax.axis_index("voc")
    block_cols = vocab_cols // voc_count
    total_tokens = tok_rows * lax.axis_size("tok")
    kept = target_ids >= 0
    kept_count = lax.psum(jnp.sum(kept.astype(jnp.float32)), "tok")
    hard_weight = jnp.where(kept, 0.5 * total_tokens / kept_count, 0.0)
    position = jnp.arange(vocab_cols, dtype=jnp.int32)
    student_cols = (
        position // block_cols * voc_count + voc_index
    ) * block_cols + position % block_cols
    teacher_here = lax.all_to_all(
        teacher_logits.reshape(tok_rows, voc_count, block_cols),
        "voc",
        split_axis=1,
        concat_axis=1,
        tiled=True,
    ).reshape(tok_rows, vocab_cols)
    used = (vocab_used[student_cols] == 1)[None, :]
    onehot = student_cols[None, :] == target_ids[:, None]
    teacher = teacher_here.astype(jnp.float32)
    student = student_logits.astype(jnp.float32)
    student_top, student_sum = local_totals(student, used)
    target_part = jnp.sum(jnp.where(onehot, student, 0.0), axis=1)
    teacher_top, teacher_sum = local_totals(teacher, used)
    weighted = jnp.sum(
        jnp.where(used, jnp.exp(teacher - teacher_top[:, None]) * (teacher - student), 0.0), axis=1
    )
    teacher_top, teacher_sum, weighted, student_top, student_sum, target_logit = combined_all(
        (teacher_top, teacher_sum, weighted, student_top, student_sum, target_part),
        "voc",
        merge_joint,
    )
    teacher_lse = teacher_top + jnp.log(teacher_sum)
    student_lse = student_top + jnp.log(student_sum)
    teacher_prob = jnp.where(used, jnp.exp(teacher - teacher_lse[:, None]), 0.0)
    divergence = weighted / teacher_sum - teacher_lse + student_lse
    student_prob = jnp.where(used, jnp.exp(student - student_lse[:, None]), 0.0)
    gradient = 0.5 * (student_prob - teacher_prob) + hard_weight[:, None] * (
        student_prob - onehot.astype(jnp.float32)
    )
    gradient = jnp.where(used, gradient, 0.0).astype(jnp.bfloat16)
    token_loss = 0.5 * divergence + hard_weight * (student_lse - target_logit)
    return (gradient, token_loss)


def solution(mesh):
    placed = (P("tok", "voc"), P("tok", "voc"), P("tok"), P())
    return jax.shard_map(
        body, mesh=mesh, in_specs=placed, out_specs=(P("tok", "voc"), P("tok")), check_vma=False
    )
```

profile of v0, /device:TPU:0, one launch (start us, length us, event | category | flops | bytes accessed | tf_op | source)
XLA Modules:
  0.0 223.0 jit_solution(9439695803364014107)
XLA Ops:
  0.6 0.0 copy-start
  0.6 0.0 copy-start.1
  0.7 5.1 %all-to-all-start = ((bf16[128,4,4752]{0,2,1:T(8,128)(2,1)}), bf16[128,4,4752]{0,2,1:T(8,128)(2,1)}, u32[]{:S(2)}, u32[]{:S(2)}) async-start(bf16[128,4,4752]{0,2,1:T(8,128)(2,1)} %bitcast.95), calls=%async_computation | async-start | bytes 9732096 | tf_op jit(solution)/shard_map/all_to_all | solution.py:57
  5.8 0.0 copy-done.1
  5.8 0.6 fusion.55
  6.4 23.8 %psum.7 = f32[]{:T(128)} all-reduce(f32[]{:T(128)} %fusion.55), channel_id=1, replica_groups=mesh['tok'=8,'voc'=4] {'tok'}, use_global_device_ids=true, to_apply=%region_9.10 | all-reduce | flops 1 | bytes 8 | tf_op jit(solution)/shard_map/psum | solution.py:51
  30.1 0.6 fusion.51
  30.7 0.0 copy-done
  30.8 97.7 %gather_fusion = s32[19008]{0:T(1024)S(1)} fusion(s32[76032]{0:T(1024)S(1)} %copy-done, s32[19456]{0:T(1024)S(1)} %pad_clamp_fusion), kind=kCustom, calls=%fused_computation | custom fusion | bytes 228096 | tf_op jit(solution)/shard_map/gather | solution.py:64
  128.5 0.1 eq.28
  128.7 13.7 %fusion.27 = (f32[128]{0:T(128)S(1)}, f32[128]{0:T(128)S(1)}) fusion(bf16[128,19008]{0,1:T(8,128)(2,1)} %param.7, s32[128]{0:T(128)S(1)} %copy-done.1, s32[19008]{0:T(1024)S(1)} %fusion.48, pred[19008]{0:T(1024)(128)(4,1)S(1)} %broadcast_compare_fusion), kind=kLoop, calls=%fused_computation.42 | loop fusion | flops 14597888 | bytes 4962624 | tf_op jit(solution)/shard_map/reduce_sum | solution.py:69
  142.4 5.1 %all-gather.11 = f32[4,1,128]{2,1,0:T(1,128)S(1)} all-gather(f32[1,1,128]{2,1,0:T(1,128)S(1)} %bitcast.106), channel_id=7, replica_groups=mesh['tok'=8,'voc'=4] {'voc'}, dimensions={0}, use_global_device_ids=true | all-gather | bytes 2560 | tf_op jit(solution)/shard_map/all_gather | solution.py:10
  147.5 5.3 %all-gather.9 = f32[4,1,128]{2,1,0:T(1,128)S(1)} all-gather(f32[1,1,128]{2,1,0:T(1,128)S(1)} %bitcast.103), channel_id=5, replica_groups=mesh['tok'=8,'voc'=4] {'voc'}, dimensions={0}, use_global_device_ids=true | all-gather | bytes 2560 | tf_op jit(solution)/shard_map/all_gather | solution.py:10
  153.5 0.0 all-to-all-done
  153.5 10.4 %fusion.32 = f32[128]{0:T(128)S(1)} fusion(bf16[128,4,4752]{0,2,1:T(8,128)(2,1)} %all-to-all-done, pred[4,4752]{1,0:T(4,128)(4,1)S(1)} %eq.28), kind=kLoop, calls=%fused_computation.51 | loop fusion | flops 7298944 | bytes 4885568 | tf_op jit(solution)/shard_map/reduce_max | solution.py:18
  163.9 12.6 %fusion.26 = (f32[128]{0:T(128)S(1)}, f32[128]{0:T(128)S(1)}) fusion(bf16[128,19008]{0,1:T(8,128)(2,1)} %param.7, f32[128]{0:T(128)S(1)} %get-tuple-element.83, pred[19008]{0:T(1024)(128)(4,1)S(1)} %broadcast_compare_fusion, f32[128]{0:T(128)S(1)} %fusion.32, bf16[128,4,4752]{0,2,1:T(8,128)(2,1)} %all-to-all-done), kind=kLoop, calls=%fused_computation.41 | loop fusion | flops 24329984 | bytes 9753152 | tf_op jit(solution)/shard_map/reduce_sum | solution.py:19
  176.6 5.1 %all-gather.8 = f32[4,1,128]{2,1,0:T(1,128)S(1)} all-gather(f32[1,1,128]{2,1,0:T(1,128)S(1)} %bitcast.105), channel_id=4, replica_groups=mesh['tok'=8,'voc'=4] {'voc'}, dimensions={0}, use_global_device_ids=true | all-gather | bytes 2560 | tf_op jit(solution)/shard_map/all_gather | solution.py:10
  181.6 5.0 %all-gather.10 = f32[4,1,128]{2,1,0:T(1,128)S(1)} all-gather(f32[1,1,128]{2,1,0:T(1,128)S(1)} %bitcast.104), channel_id=6, replica_groups=mesh['tok'=8,'voc'=4] {'voc'}, dimensions={0}, use_global_device_ids=true | all-gather | bytes 2560 | tf_op jit(solution)/shard_map/all_gather | solution.py:10
  186.7 10.4 %fusion.35 = f32[128]{0:T(128)S(1)} fusion(bf16[128,4,4752]{0,2,1:T(8,128)(2,1)} %all-to-all-done, f32[128]{0:T(128)S(1)} %fusion.32, pred[4,4752]{1,0:T(4,128)(4,1)S(1)} %eq.28), kind=kLoop, calls=%fused_computation.54 | loop fusion | flops 9731968 | bytes 4886080 | tf_op jit(solution)/shard_map/reduce_sum | solution.py:19
  197.0 5.1 %all-gather.7 = f32[4,1,128]{2,1,0:T(1,128)S(1)} all-gather(f32[1,1,128]{2,1,0:T(1,128)S(1)} %bitcast.107), channel_id=3, replica_groups=mesh['tok'=8,'voc'=4] {'voc'}, dimensions={0}, use_global_device_ids=true | all-gather | bytes 2560 | tf_op jit(solution)/shard_map/all_gather | solution.py:10
  202.1 5.0 %all-gather.6 = f32[4,1,128]{2,1,0:T(1,128)S(1)} all-gather(f32[1,1,128]{2,1,0:T(1,128)S(1)} %bitcast.102), channel_id=2, replica_groups=mesh['tok'=8,'voc'=4] {'voc'}, dimensions={0}, use_global_device_ids=true | all-gather | bytes 2560 | tf_op jit(solution)/shard_map/all_gather | solution.py:10
  207.2 0.3 while.20
  207.5 0.5 multiply_add_fusion
  208.0 15.0 %fusion.19 = bf16[128,19008]{0,1:T(8,128)(2,1)} fusion(bf16[128,19008]{0,1:T(8,128)(2,1)} %param.7, bf16[128,4,4752]{0,2,1:T(8,128)(2,1)} %all-to-all-done, f32[128]{0:T(128)S(1)} %get-tuple-element.116, f32[128]{0:T(128)S(1)} %get-tuple-element.118, f32[128]{0:T(128)S(1)} %get-tuple-element.115, s32[128]{0:T(128)S(1)} %copy-done.1, s32[19008]{0:T(1024)S(1)} %fusion.48, ...), kind=kLoop, calls=%fused_computation.34 | loop fusion | flops 36495360 | bytes 14695232 | tf_op jit(solution)/shard_map/convert_element_type | solution.py:87
  (33 shorter events, 0.3 us)
Async XLA Ops:
  0.6 30.1 %copy-start = (s32[76032]{0:T(1024)S(1)}, s32[76032]{0:T(1024)}, u32[]{:S(2)}) copy-start(s32[76032]{0:T(1024)} %param.9) | copy-start | bytes 912388
  0.6 5.1 %copy-start.1 = (s32[128]{0:T(128)S(1)}, s32[128]{0:T(128)}, u32[]{:S(2)}) copy-start(s32[128]{0:T(128)} %param.8) | copy-start | bytes 1540
  0.7 152.9 %all-to-all-start = ((bf16[128,4,4752]{0,2,1:T(8,128)(2,1)}), bf16[128,4,4752]{0,2,1:T(8,128)(2,1)}, u32[]{:S(2)}, u32[]{:S(2)}) async-start(bf16[128,4,4752]{0,2,1:T(8,128)(2,1)} %bitcast.95), calls=%async_computation | async-start | bytes 9732096 | tf_op jit(solution)/shard_map/all_to_all | solution.py:57
where the time goes:
time: 224 us; the launch traced here: 223 us
  local copies, waits for them, and re-layouts  97.9 us (44%)
  other arithmetic  64.1 us (29%)
  blocking collectives  54.4 us (24%)
  starting transfers between devices  5.11 us (2%)
    gather x1, local copies, waits for them, and re-layouts, body(): used = (vocab_used[student_cols] == 1)[None, :]  97.7 us
    all_gather x6, blocking collectives, combined_all(): pieces = jax.tree.map(lambda part: lax.all_gather(part, axis), value)  30.6 us
    psum x1, blocking collectives, body(): kept_count = lax.psum(jnp.sum(kept.astype(jnp.float32)), 'tok')  23.8 us
    reduce_sum x2, other arithmetic, local_totals(): jnp.sum(jnp.where(used, jnp.exp(values - top_value[:, None]), 0.0), axis=1)  23 us
    convert_element_type x1, other arithmetic, body(): gradient = jnp.where(used, gradient, 0.0).astype(jnp.bfloat16)  15 us
    reduce_sum x1, other arithmetic, body(): target_part = jnp.sum(jnp.where(onehot, student, 0.0), axis=1)  13.7 us
    reduce_max x1, other arithmetic, local_totals(): top_value = jnp.max(jnp.where(used, values, SENTINEL), axis=1)  10.4 us
    all_to_all x1, starting transfers between devices, body(): lax.all_to_all(teacher_logits.reshape(tok_rows, voc_count, block_cols), '...  5.11 us
  transfers between devices with their start and end apart: 1, of which 0 were waited for; matrix products, arithmetic and copies ran while one was open for 51% of the time, Pallas kernels for 0%

commit v1 on v0

v1 whole, which is shorter than its diff:
```python
import functools

import jax
import jax.numpy as jnp
import numpy as np
from jax import lax
from jax.experimental import pallas as pl
from jax.experimental.pallas import tpu as pltpu
from jax.sharding import PartitionSpec as P

NEG = -1e30
LOW = -3e38
ROWS = 16
LINES = 8
LN2 = 0.6931471805599453
F32 = jnp.float32
BF16 = jnp.bfloat16


def largest_part(total, limit):
    best = ROWS
    for size in range(ROWS, limit + 1, ROWS):
        if total % size == 0:
            best = size
    return best


def fold(op, value, height=8):
    return op(value.reshape(-1, height, value.shape[-1]), axis=0)


def mask_bias(mask_ref, n):
    lines = mask_ref[n]
    ones = jnp.ones((lines.shape[0], 128), BF16)
    spread = lax.dot_general(lines, ones, (((0,), (0,)), ((), ())), preferred_element_type=F32)
    return spread.astype(BF16)


def wide_rows(line, height):
    return jnp.broadcast_to(line, (height, line.shape[-1]))


def stats_kernel(t_ref, tb_ref, s_ref, sb_ref, *rest, step, counts):
    ids, (o_ref, mt, ms, lt, ls, t_held, s_held) = rest[:-7], rest[-7:]
    g = pl.program_id(0)
    rows, lanes = t_ref.shape

    @pl.when(g == 0)
    def _():
        mt[...] = jnp.full(mt.shape, LOW, F32)
        ms[...] = jnp.full(ms.shape, LOW, F32)
        lt[...] = jnp.zeros(lt.shape, F32)
        ls[...] = jnp.zeros(ls.shape, F32)

    def part(n):
        return pl.ds(pl.multiple_of(n * step, step), step)

    def first(n, carry):
        t = t_ref[part(n), :] + mask_bias(tb_ref, n)
        s = s_ref[part(n), :] + mask_bias(sb_ref, n)
        t_held[part(n), :] = t
        s_held[part(n), :] = s
        return (
            jnp.maximum(carry[0], fold(jnp.max, t, 16)),
            jnp.maximum(carry[1], fold(jnp.max, s, 16)),
        )

    low = jnp.full((16, lanes), LOW, BF16)
    t_high, s_high = lax.fori_loop(0, rows // step, first, (low, low))
    a = jnp.maximum(mt[...], fold(jnp.max, t_high.astype(F32)))
    b = jnp.maximum(ms[...], fold(jnp.max, s_high.astype(F32)))

    def spread(top):
        return jnp.broadcast_to(top[None], (step // 8, 8, lanes)).reshape(step, lanes)

    def second(n, carry):
        return (
            carry[0] + fold(jnp.sum, jnp.exp(t_held[part(n), :].astype(F32) - spread(a))),
            carry[1] + fold(jnp.sum, jnp.exp(s_held[part(n), :].astype(F32) - spread(b))),
        )

    start = (lt[...] * jnp.exp(mt[...] - a), ls[...] * jnp.exp(ms[...] - b))
    p, q = lax.fori_loop(0, rows // step, second, start)
    mt[...] = a
    ms[...] = b
    lt[...] = p
    ls[...] = q

    @pl.when(g == pl.num_programs(0) - 1)
    def _():
        def close(m, l):
            top = jnp.max(m, axis=0, keepdims=True)
            return top, jnp.sum(l * jnp.exp(m - top), axis=0, keepdims=True)

        t_top, t_sum = close(a, p)
        s_top, s_sum = close(b, q)
        kept = jnp.zeros((1, lanes), F32)
        for ref, counted in zip(ids, counts):
            share = jnp.where(ref[...] >= 0, 1.0, 0.0)
            if counted is not None:
                share = jnp.where(lax.axis_index("voc") < counted, share, 0.0)
            kept = kept + share
        o_ref[...] = jnp.concatenate(
            [t_top, t_sum, s_top, s_sum, kept, jnp.zeros((3, lanes), F32)], axis=0)


def run_stats(teacher, student, bias, ids, counts, limit):
    total, lanes = teacher.shape
    rows = largest_part(total, limit)
    count = total // rows
    near = pl.BlockSpec((rows, lanes), lambda g: (g, 0))
    step = bias.shape[-1]
    lines = (rows // step,) + bias.shape[1:]
    t_mask = pl.BlockSpec(lines, lambda g: (g, 0, 0))
    s_mask = pl.BlockSpec(lines, lambda g: (g + count, 0, 0))
    one = pl.BlockSpec((1, lanes), lambda g: (0, 0))

    def kernel(*refs):
        stats_kernel(*refs, step=step, counts=counts)

    return pl.pallas_call(
        kernel,
        out_shape=jax.ShapeDtypeStruct((8, lanes), F32),
        grid=(count,),
        in_specs=[near, t_mask, near, s_mask] + [one] * len(ids),
        out_specs=pl.BlockSpec((8, lanes), lambda g: (0, 0)),
        scratch_shapes=[pltpu.VMEM((8, lanes), F32)] * 4 + [pltpu.VMEM((rows, lanes), BF16)] * 2,
        compiler_params=pltpu.CompilerParams(dimension_semantics=("arbitrary",)),
        name="stats",
    )(teacher, bias, student, bias, *ids)


def join_stats(refs, target, tokens):
    parts = [ref[...] for ref in refs]
    t_top = parts[0][0:1]
    s_top = parts[0][2:3]
    kept = parts[0][4:5]
    for part in parts[1:]:
        t_top = jnp.maximum(t_top, part[0:1])
        s_top = jnp.maximum(s_top, part[2:3])
        kept = kept + part[4:5]
    t_sum = jnp.zeros_like(t_top)
    s_sum = jnp.zeros_like(t_top)
    for part in parts:
        t_sum = t_sum + part[1:2] * jnp.exp(part[0:1] - t_top)
        s_sum = s_sum + part[3:4] * jnp.exp(part[2:3] - s_top)
    t_lse = t_top + jnp.log(t_sum)
    s_lse = s_top + jnp.log(s_sum)
    count = jnp.sum(kept, axis=1, keepdims=True)
    weight = jnp.where(target >= 0, (0.5 * tokens) / count, 0.0)
    base = (0.5 * (s_lse - t_lse) + weight * s_lse) * (1.0 / len(parts))
    blank = jnp.zeros((4, target.shape[1]), F32)
    return jnp.concatenate([t_lse + LN2, s_lse - jnp.log(0.5 + weight), weight, base, blank], axis=0)


def chunk_kernel(spots, *refs, spans, slot, step, cols, shares, tokens, last):
    pieces, refs = refs[:len(spans)], refs[len(spans):]
    s_ref, b_ref, tgt_ref = refs[:3]
    refs = refs[3:]
    g = pl.program_id(0)
    rows, lanes = s_ref.shape
    if shares:
        share_refs, (g_ref, d_out, vec_ref) = refs[:shares], refs[shares:]

        @pl.when(g == 0)
        def _():
            vec_ref[...] = join_stats(share_refs, tgt_ref[...], tokens)
            d_out[...] = jnp.zeros(d_out.shape, F32)
    else:
        vec_ref, d_in, _, g_ref, d_out = refs[:5]
        if last:
            d_sum = refs[5]
        else:
            d_sum = d_out

            @pl.when(g == 0)
            def _():
                d_out[...] = d_in[...]
    if shares:
        d_sum = d_out
    if last:
        @pl.when(g == 0)
        def _():
            d_sum[...] = d_in[...]

    at = 3 * (slot + g)
    base = spots[at + 1]
    target = wide_rows(tgt_ref[...], 8)
    iota = lax.broadcasted_iota(jnp.int32, (step, lanes), 0)
    t_lse = wide_rows(vec_ref[0:1, :], step)
    s_lse = wide_rows(vec_ref[1:2, :], step)
    weight = wide_rows(vec_ref[2:3, :], step)

    def run(t_ref, first=0):
        def body(n, carry):
            div, picked = carry
            r = pl.multiple_of(n * step, step)
            bias = mask_bias(b_ref, n)
            t = (t_ref[pl.ds(first + r, step), :] + bias).astype(F32)
            s = (s_ref[pl.ds(r, step), :] + bias).astype(F32)
            tp = jnp.exp(t - t_lse)
            sp = jnp.exp(s - s_lse)
            away = target - (base + r)
            hit = iota == jnp.broadcast_to(away[None], (step // 8, 8, lanes)).reshape(step, lanes)
            if cols is not None:
                hit = hit & (iota + (spots[at + 2] + r) < cols)
            grad = (sp - tp) - jnp.where(hit, weight, 0.0)
            g_ref[pl.ds(r, step), :] = grad.astype(BF16)
            div = div + fold(jnp.sum, tp * (t - s))
            picked = picked + fold(jnp.sum, jnp.where(hit, s, 0.0))
            return (div, picked)

        div, picked = lax.fori_loop(0, rows // step, body, (d_sum[0:8, :], d_sum[8:16, :]))
        d_sum[0:8, :] = div
        d_sum[8:16, :] = picked

    done = 0
    for ref, length in zip(pieces, spans):
        if len(pieces) == 1:
            run(ref, pl.multiple_of(g * rows, rows))
        else:
            pl.when((g >= done) & (g < done + length))(functools.partial(run, ref))
        done += length
    if last:
        @pl.when(g == pl.num_programs(0) - 1)
        def _():
            mixed = d_sum[0:8, :] - wide_rows(vec_ref[2:3, :], 8) * d_sum[8:16, :]
            d_out[...] = jnp.sum(mixed, axis=0, keepdims=True) + vec_ref[3:4, :]


def run_chunk(spots, slot, rows, pieces, student, bias, target, cols, stats=(), tokens=0, state=None, last=False):
    total, lanes = student.shape
    step = bias.shape[-1]
    lines = (rows // step,) + bias.shape[1:]
    spans = [length for _, length, _ in pieces]
    moved = pl.BlockSpec((rows, lanes), lambda g, pref: (pref[3 * (slot + g)], 0))
    after = pl.BlockSpec(lines, lambda g, pref: (pref[3 * (slot + g)] + total // rows, 0, 0))

    def fixed(height):
        return pl.BlockSpec((height, lanes), lambda g, pref: (0, 0))

    in_specs, operands = [], [spots]
    done = 0
    for array, length, local in pieces:
        def where(g, pref, done=done, length=length, local=local):
            mine = jnp.clip(g - done, 0, length - 1)
            return ((pref[3 * (slot + done + mine)] if local else mine), 0)

        held = pl.BlockSpec(memory_space=pltpu.VMEM)
        in_specs.append(held if len(pieces) == 1 else pl.BlockSpec((rows, lanes), where))
        operands.append(array)
        done += length
    in_specs += [moved, after, fixed(1)]
    operands += [student, bias, target]
    out_shape = [jax.ShapeDtypeStruct(student.shape, BF16)]
    out_specs = [moved]
    aliases = {}
    scratch = []
    if stats:
        in_specs += [fixed(8)] * len(stats)
        operands += list(stats)
        out_shape += [jax.ShapeDtypeStruct((16, lanes), F32), jax.ShapeDtypeStruct((8, lanes), F32)]
        out_specs += [fixed(16), fixed(8)]
    else:
        vec, div, grad = state
        in_specs += [fixed(8), fixed(16), pl.BlockSpec(memory_space=pl.ANY)]
        operands += [vec, div, grad]
        aliases = {len(operands) - 1: 0}
        height = 1 if last else 16
        out_shape.append(jax.ShapeDtypeStruct((height, lanes), F32))
        out_specs.append(fixed(height))
        if last:
            scratch = [pltpu.VMEM((16, lanes), F32)]

    def kernel(*refs):
        chunk_kernel(*refs, spans=spans, slot=slot, step=step, cols=cols, shares=len(stats), tokens=tokens, last=last)

    return pl.pallas_call(
        kernel,
        out_shape=tuple(out_shape),
        grid_spec=pltpu.PrefetchScalarGridSpec(
            num_scalar_prefetch=1,
            grid=(sum(spans),),
            in_specs=in_specs,
            out_specs=tuple(out_specs),
            scratch_shapes=scratch,
        ),
        input_output_aliases=aliases,
        compiler_params=pltpu.CompilerParams(dimension_semantics=("arbitrary",)),
        name="chunk",
    )(*operands)


def cut_kernel(where, t_ref, *rest, parts, held):
    outs, rest = rest[:len(parts)], rest[len(parts):]
    stops = outs if held else rest[:len(parts)]
    sems = rest[-1]
    reads, writes = [], []
    for k, (slot, start, size) in enumerate(parts):
        reads.append(pltpu.make_async_copy(t_ref.at[where[slot], pl.ds(start, size), :], stops[k], sems.at[k]))
        reads[-1].start()
    for k in range(len(parts)):
        reads[k].wait()
        if not held:
            writes.append(pltpu.make_async_copy(stops[k], outs[k], sems.at[len(parts) + k]))
            writes[-1].start()
    for copy in writes:
        copy.wait()


def cut(where, teacher, parts, held):
    lanes = teacher.shape[-1]
    space = pltpu.VMEM if held else pl.ANY
    scratch = [] if held else [pltpu.VMEM((size, lanes), BF16) for _, _, size in parts]

    def kernel(*refs):
        cut_kernel(*refs, parts=parts, held=held)

    return pl.pallas_call(
        kernel,
        out_shape=tuple(jax.ShapeDtypeStruct((size, lanes), BF16) for _, _, size in parts),
        grid_spec=pltpu.PrefetchScalarGridSpec(
            num_scalar_prefetch=1,
            grid=(1,),
            in_specs=[pl.BlockSpec(memory_space=pl.ANY)],
            out_specs=tuple(pl.BlockSpec(memory_space=space) for _ in parts),
            scratch_shapes=scratch + [pltpu.SemaphoreType.DMA((2 * len(parts),))],
        ),
        name="cut",
    )(where, teacher)


def plan(padded, voc_count):
    shifts = list(range(voc_count - 1, 0, -1))
    far = shifts[:-1] if len(shifts) > 1 else shifts
    near = shifts[len(far):]
    big = largest_part(padded, 1600)
    small = largest_part(padded, 544)
    chunked = padded == 3 * big and big == 3 * small
    pieces = []
    for index, shift in enumerate(far):
        if chunked and index == 0:
            pieces += [(shift, 0, big, big), (shift, big, 2 * big, big)]
        elif chunked and index == len(far) - 1:
            pieces += [(shift, 0, 2 * big, big), (shift, 2 * big, 2 * small, small),
                       (shift, 2 * big + 2 * small, small, small)]
        else:
            pieces.append((shift, 0, padded, big))
    late = [k for k, piece in enumerate(pieces) if len(far) > 1 and piece[0] == far[-1]]
    pieces += [(shift, 0, padded, big) for shift in near]
    early = [k for k in range(len(pieces)) if k not in late]
    return pieces, early, late, big


def body(teacher_logits, student_logits, target_ids, vocab_used):
    tok_rows, vocab_cols = teacher_logits.shape
    voc_count = lax.axis_size("voc")
    voc_index = lax.axis_index("voc")
    tok_count = lax.axis_size("tok")
    block_cols = vocab_cols // voc_count
    padded = -(-block_cols // ROWS) * ROWS
    split = padded != block_cols
    paired = voc_count & (voc_count - 1) == 0

    def partner(index, shift):
        return index ^ shift if paired else (index + shift) % voc_count

    def source(index, shift):
        return index ^ shift if paired else (index - shift) % voc_count

    def swap(value, shift):
        return lax.ppermute(value, "voc", [(i, partner(i, shift)) for i in range(voc_count)])

    def blocked(matrix):
        shaped = matrix.T.reshape(voc_count, block_cols, tok_rows)
        if split:
            shaped = jnp.pad(shaped, ((0, 0), (0, padded - block_cols), (0, 0)))
        return shaped

    teacher = blocked(teacher_logits)
    flat = teacher.reshape(voc_count * padded, tok_rows)
    student = blocked(student_logits).reshape(voc_count * padded, tok_rows)
    pieces, early, late, big = plan(padded, voc_count)

    blocks = partner(voc_index, np.array([piece[0] for piece in pieces], np.int32)).astype(jnp.int32)
    cuts = [(k, piece[1], piece[2]) for k, piece in enumerate(pieces)]
    parts = list(cut(blocks, teacher, cuts[:1], True))
    parts += list(cut(blocks, teacher, cuts[1:], False))
    arrived = []
    for k, piece in enumerate(pieces):
        arrived.append(swap(parts[k], piece[0]))

    target = target_ids.reshape(1, tok_rows)
    ids, counts = [], []
    for j in range(-(-tok_count // voc_count)):
        pairs = []
        for t in range(tok_count):
            for v in range(voc_count):
                shift = j * voc_count + v
                if shift < tok_count:
                    pairs.append((t * voc_count + v, (t + shift) % tok_count * voc_count + v))
        ids.append(lax.ppermute(target, ("tok", "voc"), pairs))
        counts.append(None if (j + 1) * voc_count <= tok_count else tok_count - j * voc_count)

    flags = vocab_used.reshape(voc_count, voc_count, block_cols)
    flags = jnp.stack([
        lax.dynamic_index_in_dim(flags, voc_index, 0, keepdims=False),
        lax.dynamic_index_in_dim(flags, voc_index, 1, keepdims=False),
    ])
    line = jnp.where(flags == 1, 0.0, NEG / LINES).astype(BF16).reshape(2 * voc_count, block_cols)
    if split:
        line = jnp.pad(line, ((0, 0), (0, padded - block_cols)), constant_values=NEG / LINES)
    step = largest_part(padded, 544)
    line = line.reshape(2 * voc_count * padded // step, 1, step)
    bias = jnp.broadcast_to(line, (line.shape[0], LINES, step))

    stats = run_stats(flat, student, bias, ids, counts, 1600)
    gathered = [stats]
    for shift in range(1, voc_count):
        gathered.append(swap(stats, shift))

    shift_of, scale, own, fixed = [], [], [], []

    def note(shift, start, size, rows):
        for at in range(start, start + size, rows):
            shift_of.extend([shift] * 3)
            scale.extend([padded // rows, voc_count * block_cols, 0])
            own.extend([0, block_cols, 0])
            fixed.extend([at // rows, at, at])
        return size // rows

    groups = []
    first = [(flat, note(0, 0, padded, big), True)]
    for k in sorted(early, key=lambda k: k < len(pieces) - 1):
        first.append((arrived[k], note(*pieces[k]), False))
    used = sum(length for _, length, _ in first)
    for k in late:
        length = note(*pieces[k])
        groups.append((used, pieces[k][3], [(arrived[k], length, False)]))
        used += length
    blocks = source(voc_index, np.array(shift_of, np.int32))
    spots = blocks * np.array(scale, np.int32) + voc_index * np.array(own, np.int32) + np.array(fixed, np.int32)
    spots = spots.astype(jnp.int32)

    cols = block_cols if split else None
    grad, div, vec = run_chunk(
        spots, 0, big, first, student, bias, target, cols, stats=gathered, tokens=tok_rows * tok_count)
    for n, (slot, rows, piece) in enumerate(groups):
        grad, div = run_chunk(
            spots, slot, rows, piece, student, bias, target, cols, state=(vec, div, grad),
            last=n == len(groups) - 1)
    if not groups:
        div = jnp.sum(div[:8] - vec[2:3] * div[8:], axis=0, keepdims=True) + vec[3:4]
    loss = div
    for shift in range(1, voc_count):
        loss = loss + swap(div, shift)
    gradient = grad.reshape(voc_count, padded, tok_rows)[:, :block_cols].reshape(vocab_cols, tok_rows).T
    return (gradient, loss.reshape(tok_rows))


def solution(mesh):
    placed = (P("tok", "voc"), P("tok", "voc"), P("tok"), P())

    step = jax.shard_map(body, mesh=mesh, in_specs=placed, out_specs=(P("tok", "voc"), P("tok")), check_vma=False)

    def whole(teacher_logits, student_logits, target_ids, vocab_used):
        run = step
        return run(teacher_logits, student_logits, target_ids, vocab_used)

    return whole
```

time: 224 us -> 101 us (0.45)
  local copies, waits for them, and re-layouts: 97.9 us -> 5.06 us
  other arithmetic: 64.1 us -> 2.91 us
  blocking collectives: 54.4 us -> 0 us
  Pallas kernels: 0 us -> 51.1 us
  waiting for transfers between devices: 0.01 us -> 23.6 us
  starting transfers between devices: 5.11 us -> 16.7 us
    gather x1 -> x0, local copies, waits for them, and re-layouts: 97.7 us -> none  [body(): used = (vocab_used[student_cols] == 1)[None, :]]
    pallas_call x0 -> x7, Pallas kernels: none -> 51.1 us  [the longest x4 25.8 us: run_chunk(): pl.pallas_call(kernel, out_shape=tuple(out_shape), grid_spec=pltpu.Prefet...]
    reduce_sum x4 -> x0, other arithmetic: 37.4 us -> none  [the longest x2 23 us: local_totals(): jnp.sum(jnp.where(used, jnp.exp(values - top_value[:, None]), 0.0), axis=1)]
    all_gather x6 -> x0, blocking collectives: 30.6 us -> none  [combined_all(): pieces = jax.tree.map(lambda part: lax.all_gather(part, axis), value)]
    psum x1 -> x0, blocking collectives: 23.8 us -> none  [body(): kept_count = lax.psum(jnp.sum(kept.astype(jnp.float32)), 'tok')]
    ppermute x0 -> x14, waiting for transfers between devices: none -> 23.6 us  [the longest x12 23.6 us: swap(): lax.ppermute(value, 'voc', [(i, partner(i, shift)) for i in range(voc_cou...]
    ppermute x0 -> x14, starting transfers between devices: none -> 16.7 us  [the longest x12 11.3 us: swap(): lax.ppermute(value, 'voc', [(i, partner(i, shift)) for i in range(voc_cou...]
    convert_element_type x1, other arithmetic: 15 us -> 0.04 us  [body(): jnp.where(flags == 1, 0.0, NEG / LINES).astype(BF16)]
  transfers between devices with their start and end apart: 1 -> 14, of which waited for: 0 -> 5; matrix products, arithmetic and copies ran while one was open for 51% -> 3% of each run, Pallas kernels for 0% -> 48%
where the time goes in v1:
time: 101 us; the launch traced here: 100 us
  Pallas kernels  51.1 us (51%)
  waiting for transfers between devices  23.6 us (23%)
  starting transfers between devices  16.7 us (17%)
  local copies, waits for them, and re-layouts  5.06 us (5%)
  other arithmetic  2.91 us (3%)
    pallas_call x4, Pallas kernels, run_chunk(): pl.pallas_call(kernel, out_shape=tuple(out_shape), grid_spec=pltpu.Prefet...  25.8 us
    ppermute x12, waiting for transfers between devices, swap(): lax.ppermute(value, 'voc', [(i, partner(i, shift)) for i in range(voc_cou...  23.6 us
    pallas_call x1, Pallas kernels, run_stats(): pl.pallas_call(kernel, out_shape=jax.ShapeDtypeStruct((8, lanes), F32), g...  19 us
    ppermute x12, starting transfers between devices, swap(): lax.ppermute(value, 'voc', [(i, partner(i, shift)) for i in range(voc_cou...  11.3 us
    pallas_call x2, Pallas kernels, cut(): pl.pallas_call(kernel, out_shape=tuple((jax.ShapeDtypeStruct((size, lanes...  6.26 us
    ppermute x2, starting transfers between devices, body(): ids.append(lax.ppermute(target, ('tok', 'voc'), pairs))  5.42 us
    unnamed x31, local copies, waits for them, and re-layouts  3.56 us
  transfers between devices with their start and end apart: 14, of which 5 were waited for; matrix products, arithmetic and copies ran while one was open for 3% of the time, Pallas kernels for 48%

profile of v1, /device:TPU:0, one launch (start us, length us, event | category | flops | bytes accessed | tf_op | source)
XLA Modules:
  0.0 100.2 jit_solution(7181356336958322142)
XLA Ops:
  0.6 4.1 %collective-permute-start.5 = (s32[1,128]{1,0:T(1,128)}, s32[1,128]{1,0:T(1,128)S(1)}, u32[]{:S(2)}, u32[]{:S(2)}) collective-permute-start(s32[1,128]{1,0:T(1,128)} %bitcast.22), channel_id=1, source_target_pairs={{0,16},{1,21},{2,26},{3,31},{4,20},{5,25},{6,30},{7,3},{8,24},{9,2... | collective-permute-start | bytes 1544 | tf_op jit(solution)/shard_map/ppermute | solution.py:402
  4.7 1.3 %collective-permute-start.4 = (s32[1,128]{1,0:T(1,128)}, s32[1,128]{1,0:T(1,128)S(1)}, u32[]{:S(2)}, u32[]{:S(2)}) collective-permute-start(s32[1,128]{1,0:T(1,128)} %bitcast.23), channel_id=1, source_target_pairs={{0,0},{1,5},{2,10},{3,15},{4,4},{5,9},{6,14},{7,19},{8,8},{9,13},{... | collective-permute-start | bytes 1544 | tf_op jit(solution)/shard_map/ppermute | solution.py:402
  6.0 1.2 %broadcast_xor_fusion.refs_0_ = s32[6]{0:T(128)} fusion(s32[6]{0:T(128)} %constant.30.clone, s32[]{:T(128)S(6)} %axis_index.12), kind=kLoop, calls=%fused_computation.7 | loop fusion | flops 6 | bytes 52 | tf_op jit(solution)/shard_map/xor | solution.py:366
  7.2 0.0 copy-start.4
  7.2 2.6 %cut.3 = bf16[1584,128]{1,0:T(8,128)(2,1)} custom-call(s32[6]{0:T(128)} %broadcast_xor_fusion.refs_0_, bf16[4,4752,128]{2,1,0:T(8,128)(2,1)} %bitcast.16), custom_call_target="tpu_custom_call" | custom-call | tf_op jit(solution)/shard_map/cut/pallas_call | solution.py:319
  9.8 3.3 %collective-permute-start.2 = (bf16[1584,128]{1,0:T(8,128)(2,1)}, bf16[1584,128]{1,0:T(8,128)(2,1)S(1)}, u32[]{:S(2)}, u32[]{:S(2)}) collective-permute-start(bf16[1584,128]{1,0:T(8,128)(2,1)} %cut.3), channel_id=1, source_target_pairs={{0,3},{1,2},{2,1},{3,0},{4,7},{5,6},{6,5},{7,4},{8,11},{9,10},{10,... | collective-permute-start | bytes 1216520 | tf_op jit(solution)/shard_map/ppermute | solution.py:372
  13.1 3.7 %cut.2 = (bf16[3168,128]{1,0:T(8,128)(2,1)}, bf16[3168,128]{1,0:T(8,128)(2,1)}, bf16[1056,128]{1,0:T(8,128)(2,1)}, bf16[528,128]{1,0:T(8,128)(2,1)}, bf16[4752,128]{1,0:T(8,128)(2,1)}) custom-call(s32[6]{0:T(128)} %broadcast_xor_fusion.refs_0_, bf16[4,4752,128]{2,1,0:T(8,128)(2,1)} %bitcast.17), custom_call_target="tpu_custom_call" | custom-call | tf_op jit(solution)/shard_map/cut/pallas_call | solution.py:319
  16.8 0.1 collective-permute-start.3
  16.9 0.8 collective-permute-start.1
  17.7 0.0 copy-done.4
  17.7 0.3 reshape.31
  18.0 0.1 constant_dynamic-slice_fusion
  18.1 0.0 collective-permute-done.5.refs_5_
  18.2 0.0 copy-start.9
  18.2 1.3 %collective-permute-start.10 = (bf16[3168,128]{1,0:T(8,128)(2,1)}, bf16[3168,128]{1,0:T(8,128)(2,1)S(1)}, u32[]{:S(2)}, u32[]{:S(2)}) collective-permute-start(bf16[3168,128]{1,0:T(8,128)(2,1)} %get-tuple-element.21), channel_id=1, source_target_pairs={{0,2},{1,3},{2,0},{3,1},{4,6},{5,7},{6,4},{7,5},{8,10},{9,11},{10,... | collective-permute-start | bytes 2433032 | tf_op jit(solution)/shard_map/ppermute | solution.py:372
  19.6 0.2 convert_element_type.11
  19.7 0.0 collective-permute-done.4.refs_4_
  19.7 0.0 copy-start.10
  19.7 1.0 broadcast_in_dim.15.refs_1_.refs_3_.refs_6_
  20.7 0.0 copy-done.9
  20.7 0.0 copy-done.10
  20.7 0.0 copy-start.11
  20.7 0.0 copy-start.13
  20.7 0.0 copy-start.14
  20.8 19.0 %stats.1.refs_8_ = f32[8,128]{1,0:T(8,128)} custom-call(bf16[19008,128]{1,0:T(8,128)(2,1)} %bitcast.18, bf16[72,8,528]{2,1,0:T(8,128)(2,1)} %broadcast_in_dim.15.refs_1_.refs_3_.refs_6_, bf16[19008,128]{1,0:T(8,128)(2,1)} %bitcast.11, bf16[72,8,528]{2,1,0:T(8,128)(2,1)} %broadcast_in_dim.15.refs_1_.refs_3_.refs_6_, s32[1,128]{1,0:T(1,128)} %copy-done.10, ...), custom_call_target="tpu_custom_call" | custom-call | tf_op jit(solution)/shard_map/stats/pallas_call | solution.py:121
  39.8 0.1 collective-permute-start.8
  39.9 17.5 %collective-permute-done.8.refs_11_ = f32[8,128]{1,0:T(8,128)S(1)} collective-permute-done((f32[8,128]{1,0:T(8,128)}, f32[8,128]{1,0:T(8,128)S(1)}, u32[]{:S(2)}, u32[]{:S(2)}) %collective-permute-start.8) | collective-permute-done | bytes 4128 | tf_op jit(solution)/shard_map/ppermute | solution.py:372
  57.3 1.7 %collective-permute-start.7 = (f32[8,128]{1,0:T(8,128)}, f32[8,128]{1,0:T(8,128)S(1)}, u32[]{:S(2)}, u32[]{:S(2)}) collective-permute-start(f32[8,128]{1,0:T(8,128)} %stats.1.refs_8_), channel_id=1, source_target_pairs={{0,2},{1,3},{2,0},{3,1},{4,6},{5,7},{6,4},{7,5},{8,10},{9,11},{10,... | collective-permute-start | bytes 12296 | tf_op jit(solution)/shard_map/ppermute | solution.py:372
  59.0 2.1 %collective-permute-done.7.refs_10_ = f32[8,128]{1,0:T(8,128)S(1)} collective-permute-done((f32[8,128]{1,0:T(8,128)}, f32[8,128]{1,0:T(8,128)S(1)}, u32[]{:S(2)}, u32[]{:S(2)}) %collective-permute-start.7) | collective-permute-done | bytes 4128 | tf_op jit(solution)/shard_map/ppermute | solution.py:372
  61.1 0.0 collective-permute-start.6
  61.1 1.4 %collective-permute-done.6.refs_9_ = f32[8,128]{1,0:T(8,128)S(1)} collective-permute-done((f32[8,128]{1,0:T(8,128)}, f32[8,128]{1,0:T(8,128)S(1)}, u32[]{:S(2)}, u32[]{:S(2)}) %collective-permute-start.6) | collective-permute-done | bytes 4128 | tf_op jit(solution)/shard_map/ppermute | solution.py:372
  62.5 1.7 %collective-permute-start.9 = (bf16[1056,128]{1,0:T(8,128)(2,1)}, bf16[1056,128]{1,0:T(8,128)(2,1)S(1)}, u32[]{:S(2)}, u32[]{:S(2)}) collective-permute-start(bf16[1056,128]{1,0:T(8,128)(2,1)} %get-tuple-element.20), channel_id=1, source_target_pairs={{0,2},{1,3},{2,0},{3,1},{4,6},{5,7},{6,4},{7,5},{8,10},{9,11},{10,... | collective-permute-start | bytes 811016 | tf_op jit(solution)/shard_map/ppermute | solution.py:372
  64.2 0.0 collective-permute-done.2.refs_3_
  64.3 0.3 collective-permute-start
  64.6 0.0 copy-done.11
  64.6 0.0 copy-done.12
  64.6 0.0 copy-done.13
  64.6 0.0 copy-done.14
  64.6 0.5 add_add_fusion.refs_0_
  65.1 0.0 collective-permute-done.3.refs_4_
  65.1 0.0 collective-permute-done.1.refs_2_
  65.1 0.0 copy-done.6
  65.1 0.0 copy-done.7
  65.1 0.0 copy-done.8
  65.1 0.0 copy-done.3
  65.1 0.8 copy-done.1
  66.0 1.0 %copy-done = bf16[4752,128]{1,0:T(8,128)(2,1)} copy-done((bf16[4752,128]{1,0:T(8,128)(2,1)}, bf16[4752,128]{1,0:T(8,128)(2,1)S(1)}, u32[]{:S(2)}) %copy-start) | copy-done | bytes 1216536
  67.0 14.7 %chunk.4 = (bf16[19008,128]{1,0:T(8,128)(2,1)}, f32[16,128]{1,0:T(8,128)}, f32[8,128]{1,0:T(8,128)}) custom-call(s32[42]{0:T(128)} %add_add_fusion.refs_0_, bf16[19008,128]{1,0:T(8,128)(2,1)} %bitcast.19, bf16[4752,128]{1,0:T(8,128)(2,1)} %copy-done, bf16[1584,128]{1,0:T(8,128)(2,1)} %copy-done.3, bf16[3168,128]{1,0:T(8,128)(2,1)} %copy-done.1, ...), custom_call_target="tpu_custom_call" | custom-call | tf_op jit(solution)/shard_map/chunk/pallas_call | solution.py:278
  81.7 0.0 collective-permute-done.10.refs_1_
  81.7 0.0 copy-start.2
  81.7 0.9 copy-done.2
  82.6 5.2 %chunk.5 = (bf16[19008,128]{1,0:T(8,128)(2,1)}, f32[16,128]{1,0:T(8,128)}) custom-call(s32[42]{0:T(128)} %add_add_fusion.refs_0_, bf16[3168,128]{1,0:T(8,128)(2,1)} %copy-done.2, bf16[19008,128]{1,0:T(8,128)(2,1)} %bitcast.13, bf16[72,8,528]{2,1,0:T(8,128)(2,1)} %broadcast_in_dim.15.refs_1_.refs_3_.refs_6_, ...), custom_call_target="tpu_custom_call", output_to_operand_aliasing={{0}: (7, {})} | custom-call | tf_op jit(solution)/shard_map/chunk/pallas_call | solution.py:278
  87.8 0.0 collective-permute-done.9.refs_1_
  87.8 0.7 copy-done.5
  88.5 3.3 %chunk.6 = (bf16[19008,128]{1,0:T(8,128)(2,1)}, f32[16,128]{1,0:T(8,128)}) custom-call(s32[42]{0:T(128)} %add_add_fusion.refs_0_, bf16[1056,128]{1,0:T(8,128)(2,1)} %copy-done.5, bf16[19008,128]{1,0:T(8,128)(2,1)} %bitcast.14, bf16[72,8,528]{2,1,0:T(8,128)(2,1)} %broadcast_in_dim.15.refs_1_.refs_3_.refs_6_, ...), custom_call_target="tpu_custom_call", output_to_operand_aliasing={{0}: (7, {})} | custom-call | tf_op jit(solution)/shard_map/chunk/pallas_call | solution.py:278
  91.7 0.0 collective-permute-done.refs_1_
  91.7 2.7 %chunk.7 = (bf16[19008,128]{1,0:T(8,128)(2,1)}, f32[1,128]{1,0:T(1,128)}) custom-call(s32[42]{0:T(128)} %add_add_fusion.refs_0_, bf16[528,128]{1,0:T(8,128)(2,1)} %collective-permute-done.refs_1_, bf16[19008,128]{1,0:T(8,128)(2,1)} %bitcast.15, bf16[72,8,528]{2,1,0:T(8,128)(2,1)} %broadcast_in_dim.15.refs_1_.refs_3_.refs_6_, ...), custom_call_target="tpu_custom_call", output_to_operand_aliasing={{0}: (7, {})} | custom-call | tf_op jit(solution)/shard_map/chunk/pallas_call | solution.py:278
  94.4 0.9 collective-permute-start.13
  95.4 0.8 collective-permute-start.12
  96.2 0.1 collective-permute-start.11
  96.3 1.3 %collective-permute-done.13 = f32[1,128]{1,0:T(1,128)S(1)} collective-permute-done((f32[1,128]{1,0:T(1,128)}, f32[1,128]{1,0:T(1,128)S(1)}, u32[]{:S(2)}, u32[]{:S(2)}) %collective-permute-start.13) | collective-permute-done | bytes 544 | tf_op jit(solution)/shard_map/ppermute | solution.py:372
  97.6 1.4 %collective-permute-done.12 = f32[1,128]{1,0:T(1,128)S(1)} collective-permute-done((f32[1,128]{1,0:T(1,128)}, f32[1,128]{1,0:T(1,128)S(1)}, u32[]{:S(2)}, u32[]{:S(2)}) %collective-permute-start.12) | collective-permute-done | bytes 544 | tf_op jit(solution)/shard_map/ppermute | solution.py:372
  99.0 0.0 collective-permute-done.11
  99.0 1.2 %add_bitcast_fusion = f32[128]{0:T(128)} fusion(f32[1,128]{1,0:T(1,128)S(1)} %collective-permute-done.13, f32[1,128]{1,0:T(1,128)S(1)} %collective-permute-done.12, f32[1,128]{1,0:T(1,128)} %get-tuple-element.29, f32[1,128]{1,0:T(1,128)S(1)} %collective-permute-done.11), kind=kLoop, calls=%fused_computation.3 | loop fusion | flops 384 | bytes 2560 | tf_op jit(solution)/shard_map/reshape | solution.py:458
  (11 shorter events, 0.1 us)
Async XLA Ops:
  0.6 17.5 %collective-permute-start.5 = (s32[1,128]{1,0:T(1,128)}, s32[1,128]{1,0:T(1,128)S(1)}, u32[]{:S(2)}, u32[]{:S(2)}) collective-permute-start(s32[1,128]{1,0:T(1,128)} %bitcast.22), channel_id=1, source_target_pairs={{0,16},{1,21},{2,26},{3,31},{4,20},{5,25},{6,30},{7,3},{8,24},{9,2... | collective-permute-start | bytes 1544 | tf_op jit(solution)/shard_map/ppermute | solution.py:402
  4.7 15.0 %collective-permute-start.4 = (s32[1,128]{1,0:T(1,128)}, s32[1,128]{1,0:T(1,128)S(1)}, u32[]{:S(2)}, u32[]{:S(2)}) collective-permute-start(s32[1,128]{1,0:T(1,128)} %bitcast.23), channel_id=1, source_target_pairs={{0,0},{1,5},{2,10},{3,15},{4,4},{5,9},{6,14},{7,19},{8,8},{9,13},{... | collective-permute-start | bytes 1544 | tf_op jit(solution)/shard_map/ppermute | solution.py:402
  7.2 10.5 %copy-start.4 = (s32[76032]{0:T(1024)S(1)}, s32[76032]{0:T(1024)}, u32[]{:S(2)}) copy-start(s32[76032]{0:T(1024)} %param.12) | copy-start | bytes 912388
  9.8 54.4 %collective-permute-start.2 = (bf16[1584,128]{1,0:T(8,128)(2,1)}, bf16[1584,128]{1,0:T(8,128)(2,1)S(1)}, u32[]{:S(2)}, u32[]{:S(2)}) collective-permute-start(bf16[1584,128]{1,0:T(8,128)(2,1)} %cut.3), channel_id=1, source_target_pairs={{0,3},{1,2},{2,1},{3,0},{4,7},{5,6},{6,5},{7,4},{8,11},{9,10},{10,... | collective-permute-start | bytes 1216520 | tf_op jit(solution)/shard_map/ppermute | solution.py:372
  16.8 48.3 %collective-permute-start.3 = (bf16[3168,128]{1,0:T(8,128)(2,1)}, bf16[3168,128]{1,0:T(8,128)(2,1)S(1)}, u32[]{:S(2)}, u32[]{:S(2)}) collective-permute-start(bf16[3168,128]{1,0:T(8,128)(2,1)} %get-tuple-element.18), channel_id=1, source_target_pairs={{0,3},{1,2},{2,1},{3,0},{4,7},{5,6},{6,5},{7,4},{8,11},{9,10},{10,... | collective-permute-start | bytes 2433032 | tf_op jit(solution)/shard_map/ppermute | solution.py:372
  16.9 48.2 %collective-permute-start.1 = (bf16[4752,128]{1,0:T(8,128)(2,1)}, bf16[4752,128]{1,0:T(8,128)(2,1)S(1)}, u32[]{:S(2)}, u32[]{:S(2)}) collective-permute-start(bf16[4752,128]{1,0:T(8,128)(2,1)} %get-tuple-element.17), channel_id=1, source_target_pairs={{0,1},{1,0},{2,3},{3,2},{4,5},{5,4},{6,7},{7,6},{8,9},{9,8},{10,11... | collective-permute-start | bytes 3649544 | tf_op jit(solution)/shard_map/ppermute | solution.py:372
  18.2 2.6 %copy-start.9 = (s32[1,128]{1,0:T(1,128)}, s32[1,128]{1,0:T(1,128)S(1)}, u32[]{:S(2)}) copy-start(s32[1,128]{1,0:T(1,128)S(1)} %collective-permute-done.5.refs_5_) | copy-start | bytes 1540
  18.2 63.5 %collective-permute-start.10 = (bf16[3168,128]{1,0:T(8,128)(2,1)}, bf16[3168,128]{1,0:T(8,128)(2,1)S(1)}, u32[]{:S(2)}, u32[]{:S(2)}) collective-permute-start(bf16[3168,128]{1,0:T(8,128)(2,1)} %get-tuple-element.21), channel_id=1, source_target_pairs={{0,2},{1,3},{2,0},{3,1},{4,6},{5,7},{6,4},{7,5},{8,10},{9,11},{10,... | collective-permute-start | bytes 2433032 | tf_op jit(solution)/shard_map/ppermute | solution.py:372
  19.7 1.0 copy-start.10
  20.7 43.8 %copy-start.11 = (s32[42]{0:T(128)S(1)}, s32[42]{0:T(128)}, u32[]{:S(2)}) copy-start(s32[42]{0:T(128)} %constant.34.clone) | copy-start | bytes 508
  20.7 43.8 %copy-start.12 = (s32[42]{0:T(128)S(1)}, s32[42]{0:T(128)}, u32[]{:S(2)}) copy-start(s32[42]{0:T(128)} %constant.33.clone) | copy-start | bytes 508
  20.7 43.8 %copy-start.13 = (s32[42]{0:T(128)S(1)}, s32[42]{0:T(128)}, u32[]{:S(2)}) copy-start(s32[42]{0:T(128)} %constant.32.clone) | copy-start | bytes 508
  20.7 43.8 %copy-start.14 = (s32[42]{0:T(128)S(1)}, s32[42]{0:T(128)}, u32[]{:S(2)}) copy-start(s32[42]{0:T(128)} %constant.31.clone) | copy-start | bytes 508
  39.8 17.5 %collective-permute-start.8 = (f32[8,128]{1,0:T(8,128)}, f32[8,128]{1,0:T(8,128)S(1)}, u32[]{:S(2)}, u32[]{:S(2)}) collective-permute-start(f32[8,128]{1,0:T(8,128)} %stats.1.refs_8_), channel_id=1, source_target_pairs={{0,3},{1,2},{2,1},{3,0},{4,7},{5,6},{6,5},{7,4},{8,11},{9,10},{10,... | collective-permute-start | bytes 12296 | tf_op jit(solution)/shard_map/ppermute | solution.py:372
  57.3 7.8 %copy-start.6 = (f32[8,128]{1,0:T(8,128)}, f32[8,128]{1,0:T(8,128)S(1)}, u32[]{:S(2)}) copy-start(f32[8,128]{1,0:T(8,128)S(1)} %collective-permute-done.8.refs_11_) | copy-start | bytes 12292
  57.3 3.8 %collective-permute-start.7 = (f32[8,128]{1,0:T(8,128)}, f32[8,128]{1,0:T(8,128)S(1)}, u32[]{:S(2)}, u32[]{:S(2)}) collective-permute-start(f32[8,128]{1,0:T(8,128)} %stats.1.refs_8_), channel_id=1, source_target_pairs={{0,2},{1,3},{2,0},{3,1},{4,6},{5,7},{6,4},{7,5},{8,10},{9,11},{10,... | collective-permute-start | bytes 12296 | tf_op jit(solution)/shard_map/ppermute | solution.py:372
  61.1 4.0 %copy-start.7 = (f32[8,128]{1,0:T(8,128)}, f32[8,128]{1,0:T(8,128)S(1)}, u32[]{:S(2)}) copy-start(f32[8,128]{1,0:T(8,128)S(1)} %collective-permute-done.7.refs_10_) | copy-start | bytes 12292
  61.1 1.4 %collective-permute-start.6 = (f32[8,128]{1,0:T(8,128)}, f32[8,128]{1,0:T(8,128)S(1)}, u32[]{:S(2)}, u32[]{:S(2)}) collective-permute-start(f32[8,128]{1,0:T(8,128)} %stats.1.refs_8_), channel_id=1, source_target_pairs={{0,1},{1,0},{2,3},{3,2},{4,5},{5,4},{6,7},{7,6},{8,9},{9,8},{10,11... | collective-permute-start | bytes 12296 | tf_op jit(solution)/shard_map/ppermute | solution.py:372
  62.5 2.6 %copy-start.8 = (f32[8,128]{1,0:T(8,128)}, f32[8,128]{1,0:T(8,128)S(1)}, u32[]{:S(2)}) copy-start(f32[8,128]{1,0:T(8,128)S(1)} %collective-permute-done.6.refs_9_) | copy-start | bytes 12292
  62.5 25.3 %collective-permute-start.9 = (bf16[1056,128]{1,0:T(8,128)(2,1)}, bf16[1056,128]{1,0:T(8,128)(2,1)S(1)}, u32[]{:S(2)}, u32[]{:S(2)}) collective-permute-start(bf16[1056,128]{1,0:T(8,128)(2,1)} %get-tuple-element.20), channel_id=1, source_target_pairs={{0,2},{1,3},{2,0},{3,1},{4,6},{5,7},{6,4},{7,5},{8,10},{9,11},{10,... | collective-permute-start | bytes 811016 | tf_op jit(solution)/shard_map/ppermute | solution.py:372
  64.3 0.9 copy-start.3
  64.3 27.5 %collective-permute-start = (bf16[528,128]{1,0:T(8,128)(2,1)}, bf16[528,128]{1,0:T(8,128)(2,1)}, u32[]{:S(2)}, u32[]{:S(2)}) collective-permute-start(bf16[528,128]{1,0:T(8,128)(2,1)} %get-tuple-element.16), channel_id=1, source_target_pairs={{0,2},{1,3},{2,0},{3,1},{4,6},{5,7},{6,4},{7,5},{8,10},{9,11},{10,... | collective-permute-start | bytes 405512 | tf_op jit(solution)/shard_map/ppermute | solution.py:372
  65.1 0.9 copy-start.1
  66.0 1.0 %copy-start = (bf16[4752,128]{1,0:T(8,128)(2,1)}, bf16[4752,128]{1,0:T(8,128)(2,1)S(1)}, u32[]{:S(2)}) copy-start(bf16[4752,128]{1,0:T(8,128)(2,1)S(1)} %collective-permute-done.1.refs_2_) | copy-start | bytes 3649540
  81.7 0.9 copy-start.2
  87.8 0.7 copy-start.5
  94.4 3.2 %collective-permute-start.13 = (f32[1,128]{1,0:T(1,128)}, f32[1,128]{1,0:T(1,128)S(1)}, u32[]{:S(2)}, u32[]{:S(2)}) collective-permute-start(f32[1,128]{1,0:T(1,128)} %get-tuple-element.29), channel_id=1, source_target_pairs={{0,3},{1,2},{2,1},{3,0},{4,7},{5,6},{6,5},{7,4},{8,11},{9,10},{10,... | collective-permute-start | bytes 1544 | tf_op jit(solution)/shard_map/ppermute | solution.py:372
  95.4 3.6 %collective-permute-start.12 = (f32[1,128]{1,0:T(1,128)}, f32[1,128]{1,0:T(1,128)S(1)}, u32[]{:S(2)}, u32[]{:S(2)}) collective-permute-start(f32[1,128]{1,0:T(1,128)} %get-tuple-element.29), channel_id=1, source_target_pairs={{0,2},{1,3},{2,0},{3,1},{4,6},{5,7},{6,4},{7,5},{8,10},{9,11},{10,... | collective-permute-start | bytes 1544 | tf_op jit(solution)/shard_map/ppermute | solution.py:372
  96.2 2.8 %collective-permute-start.11 = (f32[1,128]{1,0:T(1,128)}, f32[1,128]{1,0:T(1,128)S(1)}, u32[]{:S(2)}, u32[]{:S(2)}) collective-permute-start(f32[1,128]{1,0:T(1,128)} %get-tuple-element.29), channel_id=1, source_target_pairs={{0,1},{1,0},{2,3},{3,2},{4,5},{5,4},{6,7},{7,6},{8,9},{9,8},{10,11... | collective-permute-start | bytes 1544 | tf_op jit(solution)/shard_map/ppermute | solution.py:372

commit v2 on v1

--- a/solution.py
+++ b/solution.py
@@ -12,6 +12,8 @@
 LOW = -3e38
 ROWS = 16
 LINES = 8
+WAYS = 3
+STEP = 544
 LN2 = 0.6931471805599453
 F32 = jnp.float32
 BF16 = jnp.bfloat16
@@ -29,105 +31,136 @@
     return op(value.reshape(-1, height, value.shape[-1]), axis=0)
 
 
-def mask_bias(mask_ref, n):
-    lines = mask_ref[n]
-    ones = jnp.ones((lines.shape[0], 128), BF16)
-    spread = lax.dot_general(lines, ones, (((0,), (0,)), ((), ())), preferred_element_type=F32)
-    return spread.astype(BF16)
+def addend_rows(rows, masks, pieces):
+    parts = []
+    for row, mask in zip(rows, masks):
+        left = -row
+        part = [jnp.ones_like(row) if k == mask else jnp.zeros_like(row) for k in range(2)]
+        for _ in range(pieces):
+            piece = left.astype(BF16).astype(F32)
+            part.append(piece)
+            left = left - piece
+        part.append(jnp.zeros((LINES - 2 - pieces, row.shape[1]), F32))
+        parts.append(jnp.concatenate(part, axis=0))
+    return jnp.concatenate(parts, axis=1).astype(BF16)
+
+
+def addend(mask_ref, n, weights):
+    return lax.dot_general(mask_ref[n], weights, (((0,), (0,)), ((), ())), preferred_element_type=F32)
 
 
 def wide_rows(line, height):
     return jnp.broadcast_to(line, (height, line.shape[-1]))
 
 
-def stats_kernel(t_ref, tb_ref, s_ref, sb_ref, *rest, step, counts):
-    ids, (o_ref, mt, ms, lt, ls, t_held, s_held) = rest[:-7], rest[-7:]
+def stats_kernel(t_ref, s_ref, m_ref, o_ref, tops, sums, block, *, step):
     g = pl.program_id(0)
     rows, lanes = t_ref.shape
+    steps = rows // step
+    tiles = step // ROWS
 
     @pl.when(g == 0)
     def _():
-        mt[...] = jnp.full(mt.shape, LOW, F32)
-        ms[...] = jnp.full(ms.shape, LOW, F32)
-        lt[...] = jnp.zeros(lt.shape, F32)
-        ls[...] = jnp.zeros(ls.shape, F32)
+        tops[...] = jnp.full(tops.shape, LOW, F32)
+        sums[...] = jnp.zeros(sums.shape, F32)
 
     def part(n):
         return pl.ds(pl.multiple_of(n * step, step), step)
 
     def first(n, carry):
-        t = t_ref[part(n), :] + mask_bias(tb_ref, n)
-        s = s_ref[part(n), :] + mask_bias(sb_ref, n)
-        t_held[part(n), :] = t
-        s_held[part(n), :] = s
-        return (
-            jnp.maximum(carry[0], fold(jnp.max, t, 16)),
-            jnp.maximum(carry[1], fold(jnp.max, s, 16)),
-        )
-
-    low = jnp.full((16, lanes), LOW, BF16)
-    t_high, s_high = lax.fori_loop(0, rows // step, first, (low, low))
-    a = jnp.maximum(mt[...], fold(jnp.max, t_high.astype(F32)))
-    b = jnp.maximum(ms[...], fold(jnp.max, s_high.astype(F32)))
-
-    def spread(top):
-        return jnp.broadcast_to(top[None], (step // 8, 8, lanes)).reshape(step, lanes)
+        tops = list(carry)
+        for k in range(tiles):
+            tile = pl.ds(pl.multiple_of(n * step + k * ROWS, ROWS), ROWS)
+            at = k % WAYS
+            tops[at] = jnp.maximum(tops[at], t_ref[tile, :])
+            tops[WAYS + at] = jnp.maximum(tops[WAYS + at], s_ref[tile, :])
+        return tuple(tops)
+
+    low = jnp.full((ROWS, lanes), LOW, BF16)
+    highs = lax.fori_loop(0, steps, first, (low,) * (2 * WAYS))
+    t_top, s_top = [
+        jnp.max(functools.reduce(jnp.maximum, highs[k:k + WAYS]).astype(F32), axis=0, keepdims=True)
+        for k in (0, WAYS)]
+    weights = addend_rows([t_top, s_top], [0, 1], 1)
 
     def second(n, carry):
-        return (
-            carry[0] + fold(jnp.sum, jnp.exp(t_held[part(n), :].astype(F32) - spread(a))),
-            carry[1] + fold(jnp.sum, jnp.exp(s_held[part(n), :].astype(F32) - spread(b))),
-        )
-
-    start = (lt[...] * jnp.exp(mt[...] - a), ls[...] * jnp.exp(ms[...] - b))
-    p, q = lax.fori_loop(0, rows // step, second, start)
-    mt[...] = a
-    ms[...] = b
-    lt[...] = p
-    ls[...] = q
+        both = addend(m_ref, n, weights)
+        t = t_ref[part(n), :].astype(F32) + both[:, :lanes]
+        s = s_ref[part(n), :].astype(F32) + both[:, lanes:]
+        return (carry[0] + fold(jnp.sum, jnp.exp(t)), carry[1] + fold(jnp.sum, jnp.exp(s)))
+
+    zero = jnp.zeros((8, lanes), F32)
+    t_sum, s_sum = [
+        jnp.sum(total, axis=0, keepdims=True)
+        for total in lax.fori_loop(0, steps, second, (zero, zero), unroll=True)]
+    block[0:1, :] = t_top
+    block[1:2, :] = t_sum
+    block[2:3, :] = s_top
+    block[3:4, :] = s_sum
+
+    @pl.when(jnp.min(jnp.minimum(t_sum, s_sum)) < 1e-10)
+    def _():
+        blank = jnp.zeros((1, lanes), F32)
+        plain = addend_rows([blank, blank], [0, 1], 1)
+
+        def masked(n):
+            both = addend(m_ref, n, plain)
+            return (
+                t_ref[part(n), :].astype(F32) + both[:, :lanes],
+                s_ref[part(n), :].astype(F32) + both[:, lanes:])
+
+        def high(n, carry):
+            return tuple(jnp.maximum(top, fold(jnp.max, value)) for top, value in zip(carry, masked(n)))
+
+        low = jnp.full((8, lanes), LOW, F32)
+        tops = [jnp.max(top, axis=0, keepdims=True) for top in lax.fori_loop(0, steps, high, (low, low))]
+
+        def gather(n, carry):
+            return tuple(
+                total + fold(jnp.sum, jnp.exp(value - wide_rows(top, step)))
+                for total, value, top in zip(carry, masked(n), tops))
+
+        totals = lax.fori_loop(0, steps, gather, (zero, zero))
+        for k in range(2):
+            block[2 * k:2 * k + 1, :] = tops[k]
+            block[2 * k + 1:2 * k + 2, :] = jnp.sum(totals[k], axis=0, keepdims=True)
+
+    for k in range(2):
+        old = tops[k:k + 1, :]
+        top = block[2 * k:2 * k + 1, :]
+        new = jnp.maximum(old, top)
+        sums[k:k + 1, :] = (
+            sums[k:k + 1, :] * jnp.exp(old - new) + block[2 * k + 1:2 * k + 2, :] * jnp.exp(top - new))
+        tops[k:k + 1, :] = new
 
     @pl.when(g == pl.num_programs(0) - 1)
     def _():
-        def close(m, l):
-            top = jnp.max(m, axis=0, keepdims=True)
-            return top, jnp.sum(l * jnp.exp(m - top), axis=0, keepdims=True)
-
-        t_top, t_sum = close(a, p)
-        s_top, s_sum = close(b, q)
-        kept = jnp.zeros((1, lanes), F32)
-        for ref, counted in zip(ids, counts):
-            share = jnp.where(ref[...] >= 0, 1.0, 0.0)
-            if counted is not None:
-                share = jnp.where(lax.axis_index("voc") < counted, share, 0.0)
-            kept = kept + share
         o_ref[...] = jnp.concatenate(
-            [t_top, t_sum, s_top, s_sum, kept, jnp.zeros((3, lanes), F32)], axis=0)
-
-
-def run_stats(teacher, student, bias, ids, counts, limit):
+            [tops[0:1, :], sums[0:1, :], tops[1:2, :], sums[1:2, :], jnp.zeros((4, lanes), F32)], axis=0)
+
+
+def run_stats(teacher, student, mask, limit):
     total, lanes = teacher.shape
     rows = largest_part(total, limit)
     count = total // rows
     near = pl.BlockSpec((rows, lanes), lambda g: (g, 0))
-    step = bias.shape[-1]
-    lines = (rows // step,) + bias.shape[1:]
-    t_mask = pl.BlockSpec(lines, lambda g: (g, 0, 0))
-    s_mask = pl.BlockSpec(lines, lambda g: (g + count, 0, 0))
-    one = pl.BlockSpec((1, lanes), lambda g: (0, 0))
+    step = mask.shape[-1]
+    lines = (rows // step,) + mask.shape[1:]
+    held = pl.BlockSpec(lines, lambda g: (g, 0, 0))
 
     def kernel(*refs):
-        stats_kernel(*refs, step=step, counts=counts)
+        stats_kernel(*refs, step=step)
 
     return pl.pallas_call(
         kernel,
         out_shape=jax.ShapeDtypeStruct((8, lanes), F32),
         grid=(count,),
-        in_specs=[near, t_mask, near, s_mask] + [one] * len(ids),
+        in_specs=[near, near, held],
         out_specs=pl.BlockSpec((8, lanes), lambda g: (0, 0)),
-        scratch_shapes=[pltpu.VMEM((8, lanes), F32)] * 4 + [pltpu.VMEM((rows, lanes), BF16)] * 2,
+        scratch_shapes=[pltpu.VMEM((8, lanes), F32)] * 3,
         compiler_params=pltpu.CompilerParams(dimension_semantics=("arbitrary",)),
         name="stats",
-    )(teacher, bias, student, bias, *ids)
+    )(teacher, student, mask)
 
 
 def join_stats(refs, target, tokens):
@@ -159,6 +192,7 @@
     refs = refs[3:]
     g = pl.program_id(0)
     rows, lanes = s_ref.shape
+    weights_ref, refs = refs[-1], refs[:-1]
     if shares:
         share_refs, (g_ref, d_out, vec_ref) = refs[:shares], refs[shares:]
 
@@ -183,34 +217,38 @@
         def _():
             d_sum[...] = d_in[...]
 
+    @pl.when(g == 0)
+    def _():
+        weights_ref[...] = addend_rows([vec_ref[0:1, :], vec_ref[1:2, :]], [1, 1], 3)
+
     at = 3 * (slot + g)
     base = spots[at + 1]
-    target = wide_rows(tgt_ref[...], 8)
-    iota = lax.broadcasted_iota(jnp.int32, (step, lanes), 0)
-    t_lse = wide_rows(vec_ref[0:1, :], step)
-    s_lse = wide_rows(vec_ref[1:2, :], step)
+    away = wide_rows(tgt_ref[...], 8) - lax.broadcasted_iota(jnp.int32, (8, lanes), 0)
+    tile = lax.broadcasted_iota(jnp.int32, (step // 8, 8, lanes), 0)
     weight = wide_rows(vec_ref[2:3, :], step)
+    weights = weights_ref[...]
 
     def run(t_ref, first=0):
         def body(n, carry):
             div, picked = carry
             r = pl.multiple_of(n * step, step)
-            bias = mask_bias(b_ref, n)
-            t = (t_ref[pl.ds(first + r, step), :] + bias).astype(F32)
-            s = (s_ref[pl.ds(r, step), :] + bias).astype(F32)
-            tp = jnp.exp(t - t_lse)
-            sp = jnp.exp(s - s_lse)
-            away = target - (base + r)
-            hit = iota == jnp.broadcast_to(away[None], (step // 8, 8, lanes)).reshape(step, lanes)
+            both = addend(b_ref, n, weights)
+            t = t_ref[pl.ds(first + r, step), :].astype(F32)
+            s = s_ref[pl.ds(r, step), :].astype(F32)
+            tp = jnp.exp(t + both[:, :lanes])
+            sp = jnp.exp(s + both[:, lanes:])
+            gap = away - (base + r)
+            line = jnp.where((gap & 7) == 0, gap >> 3, -1)
+            hit = (tile == line[None]).reshape(step, lanes)
             if cols is not None:
-                hit = hit & (iota + (spots[at + 2] + r) < cols)
+                hit = hit & (lax.broadcasted_iota(jnp.int32, (step, lanes), 0) + (spots[at + 2] + r) < cols)
             grad = (sp - tp) - jnp.where(hit, weight, 0.0)
             g_ref[pl.ds(r, step), :] = grad.astype(BF16)
             div = div + fold(jnp.sum, tp * (t - s))
             picked = picked + fold(jnp.sum, jnp.where(hit, s, 0.0))
             return (div, picked)
 
-        div, picked = lax.fori_loop(0, rows // step, body, (d_sum[0:8, :], d_sum[8:16, :]))
+        div, picked = lax.fori_loop(0, rows // step, body, (d_sum[0:8, :], d_sum[8:16, :]), unroll=True)
         d_sum[0:8, :] = div
         d_sum[8:16, :] = picked
 
@@ -229,12 +267,12 @@
 
 
 def run_chunk(spots, slot, rows, pieces, student, bias, target, cols, stats=(), tokens=0, state=None, last=False):
-    total, lanes = student.shape
+    _, lanes = student.shape
     step = bias.shape[-1]
     lines = (rows // step,) + bias.shape[1:]
     spans = [length for _, length, _ in pieces]
     moved = pl.BlockSpec((rows, lanes), lambda g, pref: (pref[3 * (slot + g)], 0))
-    after = pl.BlockSpec(lines, lambda g, pref: (pref[3 * (slot + g)] + total // rows, 0, 0))
+    after = pl.BlockSpec(lines, lambda g, pref: (pref[3 * (slot + g)], 0, 0))
 
     def fixed(height):
         return pl.BlockSpec((height, lanes), lambda g, pref: (0, 0))
@@ -271,6 +309,7 @@
         out_specs.append(fixed(height))
         if last:
             scratch = [pltpu.VMEM((16, lanes), F32)]
+    scratch.append(pltpu.VMEM((LINES, 2 * lanes), BF16))
 
     def kernel(*refs):
         chunk_kernel(*refs, spans=spans, slot=slot, step=step, cols=cols, shares=len(stats), tokens=tokens, last=last)
@@ -291,13 +330,15 @@
     )(*operands)
 
 
-def cut_kernel(where, t_ref, *rest, parts, held):
+def cut_kernel(t_ref, *rest, parts, held, partner):
     outs, rest = rest[:len(parts)], rest[len(parts):]
     stops = outs if held else rest[:len(parts)]
     sems = rest[-1]
     reads, writes = [], []
-    for k, (slot, start, size) in enumerate(parts):
-        reads.append(pltpu.make_async_copy(t_ref.at[where[slot], pl.ds(start, size), :], stops[k], sems.at[k]))
+    me = lax.axis_index("voc")
+    for k, (shift, start, size) in enumerate(parts):
+        block = partner(me, shift)
+        reads.append(pltpu.make_async_copy(t_ref.at[block, pl.ds(start, size), :], stops[k], sems.at[k]))
         reads[-1].start()
     for k in range(len(parts)):
         reads[k].wait()
@@ -308,26 +349,22 @@
         copy.wait()
 
 
-def cut(where, teacher, parts, held):
+def cut(teacher, parts, held, partner):
     lanes = teacher.shape[-1]
     space = pltpu.VMEM if held else pl.ANY
     scratch = [] if held else [pltpu.VMEM((size, lanes), BF16) for _, _, size in parts]
 
     def kernel(*refs):
-        cut_kernel(*refs, parts=parts, held=held)
+        cut_kernel(*refs, parts=parts, held=held, partner=partner)
 
     return pl.pallas_call(
         kernel,
         out_shape=tuple(jax.ShapeDtypeStruct((size, lanes), BF16) for _, _, size in parts),
-        grid_spec=pltpu.PrefetchScalarGridSpec(
-            num_scalar_prefetch=1,
-            grid=(1,),
-            in_specs=[pl.BlockSpec(memory_space=pl.ANY)],
-            out_specs=tuple(pl.BlockSpec(memory_space=space) for _ in parts),
-            scratch_shapes=scratch + [pltpu.SemaphoreType.DMA((2 * len(parts),))],
-        ),
+        in_specs=[pl.BlockSpec(memory_space=pl.ANY)],
+        out_specs=tuple(pl.BlockSpec(memory_space=space) for _ in parts),
+        scratch_shapes=scratch + [pltpu.SemaphoreType.DMA((2 * len(parts),))],
         name="cut",
-    )(where, teacher)
+    )(teacher)
 
 
 def plan(padded, voc_count):
@@ -342,11 +379,11 @@
         if chunked and index == 0:
             pieces += [(shift, 0, big, big), (shift, big, 2 * big, big)]
         elif chunked and index == len(far) - 1:
-            pieces += [(shift, 0, 2 * big, big), (shift, 2 * big, 2 * small, small),
+            pieces += [(shift, 0, big, big), (shift, big, big, big), (shift, 2 * big, 2 * small, small),
                        (shift, 2 * big + 2 * small, small, small)]
         else:
             pieces.append((shift, 0, padded, big))
-    late = [k for k, piece in enumerate(pieces) if len(far) > 1 and piece[0] == far[-1]]
+    late = [k for k, piece in enumerate(pieces) if len(far) > 1 and piece[0] == far[-1] and (piece[1] or not chunked)]
     pieces += [(shift, 0, padded, big) for shift in near]
     early = [k for k in range(len(pieces)) if k not in late]
     return pieces, early, late, big
@@ -382,39 +419,48 @@
     student = blocked(student_logits).reshape(voc_count * padded, tok_rows)
     pieces, early, late, big = plan(padded, voc_count)
 
-    blocks = partner(voc_index, np.array([piece[0] for piece in pieces], np.int32)).astype(jnp.int32)
-    cuts = [(k, piece[1], piece[2]) for k, piece in enumerate(pieces)]
-    parts = list(cut(blocks, teacher, cuts[:1], True))
-    parts += list(cut(blocks, teacher, cuts[1:], False))
+    cuts = [piece[:3] for piece in pieces]
+    parts = list(cut(teacher, cuts[:1], True, partner))
+    parts += list(cut(teacher, cuts[1:], False, partner))
     arrived = []
     for k, piece in enumerate(pieces):
         arrived.append(swap(parts[k], piece[0]))
 
     target = target_ids.reshape(1, tok_rows)
-    ids, counts = [], []
-    for j in range(-(-tok_count // voc_count)):
-        pairs = []
-        for t in range(tok_count):
-            for v in range(voc_count):
-                shift = j * voc_count + v
-                if shift < tok_count:
-                    pairs.append((t * voc_count + v, (t + shift) % tok_count * voc_count + v))
-        ids.append(lax.ppermute(target, ("tok", "voc"), pairs))
-        counts.append(None if (j + 1) * voc_count <= tok_count else tok_count - j * voc_count)
+    kept = (target >= 0).astype(F32)
+    merged = 1
+    step = 0
+    while tok_count // merged > voc_count:
+        pairs = [(i, i ^ merged) for i in range(tok_count)]
+        if step == 0:
+            kept = kept + (lax.ppermute(target, "tok", pairs) >= 0).astype(F32)
+        else:
+            kept = kept + lax.ppermute(kept, "tok", pairs)
+        merged *= 2
+        step += 1
+    left = tok_count // merged
+    pairs = [
+        (t * voc_count + v, ((t // merged + v) % left * merged + t % merged) * voc_count + v)
+        for t in range(tok_count) for v in range(left)
+    ]
+    kept = lax.ppermute(kept, ("tok", "voc"), pairs)
 
     flags = vocab_used.reshape(voc_count, voc_count, block_cols)
     flags = jnp.stack([
         lax.dynamic_index_in_dim(flags, voc_index, 0, keepdims=False),
         lax.dynamic_index_in_dim(flags, voc_index, 1, keepdims=False),
     ])
-    line = jnp.where(flags == 1, 0.0, NEG / LINES).astype(BF16).reshape(2 * voc_count, block_cols)
+    line = jnp.where(flags == 1, 0.0, NEG).astype(BF16).reshape(2 * voc_count, block_cols)
     if split:
-        line = jnp.pad(line, ((0, 0), (0, padded - block_cols)), constant_values=NEG / LINES)
-    step = largest_part(padded, 544)
-    line = line.reshape(2 * voc_count * padded // step, 1, step)
-    bias = jnp.broadcast_to(line, (line.shape[0], LINES, step))
-
-    stats = run_stats(flat, student, bias, ids, counts, 1600)
+        line = jnp.pad(line, ((0, 0), (0, padded - block_cols)), constant_values=NEG)
+    step = largest_part(padded, STEP)
+    line = line.reshape(2, voc_count * padded // step, 1, step)
+    kind = lax.broadcasted_iota(jnp.int32, (1, LINES, 1), 1)
+    ones = jnp.where(kind < 5, 1.0, 0.0).astype(BF16)
+    bias = jnp.where(kind == 0, line[0], jnp.where(kind == 1, line[1], ones))
+
+    stats = run_stats(flat, student, bias, 1600)
+    stats = jnp.concatenate([stats[:4], kept, stats[5:]], axis=0)
     gathered = [stats]
     for shift in range(1, voc_count):
         gathered.append(swap(stats, shift))

time: 101 us -> 89.1 us (0.88)
  the two profiles are of different devices: /device:TPU:0 before, /device:TPU:5 now
where the time goes in v2:
time: 89.1 us; the launch traced here: 88.4 us
  Pallas kernels  53.9 us (60%)
  starting transfers between devices  18.4 us (21%)
  waiting for transfers between devices  7.09 us (8%)
  local copies, waits for them, and re-layouts  5.4 us (6%)
  other arithmetic  2.63 us (3%)
    pallas_call x1, Pallas kernels, run_stats(): pl.pallas_call(kernel, out_shape=jax.ShapeDtypeStruct((8, lanes), F32), g...  27.8 us
    pallas_call x4, Pallas kernels, run_chunk(): pl.pallas_call(kernel, out_shape=tuple(out_shape), grid_spec=pltpu.Prefet...  21.3 us
    ppermute x13, starting transfers between devices, swap(): lax.ppermute(value, 'voc', [(i, partner(i, shift)) for i in range(voc_cou...  15.1 us
    ppermute x13, waiting for transfers between devices, swap(): lax.ppermute(value, 'voc', [(i, partner(i, shift)) for i in range(voc_cou...  7.09 us
    pallas_call x2, Pallas kernels, cut(): pl.pallas_call(kernel, out_shape=tuple((jax.ShapeDtypeStruct((size, lanes...  4.84 us
    unnamed x33, local copies, waits for them, and re-layouts  3.4 us
    ppermute x1, starting transfers between devices, body(): kept = lax.ppermute(kept, ('tok', 'voc'), pairs)  3.2 us
  transfers between devices with their start and end apart: 15, of which 5 were waited for; matrix products, arithmetic and copies ran while one was open for 4% of the time, Pallas kernels for 58%

profile of v2, /device:TPU:5, one launch (start us, length us, event | category | flops | bytes accessed | tf_op | source)
XLA Modules:
  0.0 88.4 jit_solution(3523682595126209351)
XLA Ops:
  0.6 0.1 collective-permute-start.5
  0.7 0.0 copy-start.5
  0.7 0.0 copy-start.8
  0.7 1.8 %cut.3 = bf16[1584,128]{1,0:T(8,128)(2,1)} custom-call(bf16[4,4752,128]{2,1,0:T(8,128)(2,1)} %bitcast.20), custom_call_target="tpu_custom_call" | custom-call | tf_op jit(solution)/shard_map/cut/pallas_call | solution.py:360
  2.6 2.3 %collective-permute-start.2 = (bf16[1584,128]{1,0:T(8,128)(2,1)}, bf16[1584,128]{1,0:T(8,128)(2,1)S(1)}, u32[]{:S(2)}, u32[]{:S(2)}) collective-permute-start(bf16[1584,128]{1,0:T(8,128)(2,1)} %cut.3), channel_id=1, source_target_pairs={{0,3},{1,2},{2,1},{3,0},{4,7},{5,6},{6,5},{7,4},{8,11},{9,10},{10,... | collective-permute-start | bytes 1216520 | tf_op jit(solution)/shard_map/ppermute | solution.py:409
  4.9 3.0 %cut.2 = (bf16[3168,128]{1,0:T(8,128)(2,1)}, bf16[1584,128]{1,0:T(8,128)(2,1)}, bf16[1584,128]{1,0:T(8,128)(2,1)}, bf16[1056,128]{1,0:T(8,128)(2,1)}, bf16[528,1...) custom-call(bf16[4,4752,128]{2,1,0:T(8,128)(2,1)} %bitcast.21), custom_call_target="tpu_custom_call" | custom-call | tf_op jit(solution)/shard_map/cut/pallas_call | solution.py:360
  7.9 0.1 collective-permute-start.4
  8.0 1.2 %collective-permute-start.3 = (bf16[3168,128]{1,0:T(8,128)(2,1)}, bf16[3168,128]{1,0:T(8,128)(2,1)S(1)}, u32[]{:S(2)}, u32[]{:S(2)}) collective-permute-start(bf16[3168,128]{1,0:T(8,128)(2,1)} %get-tuple-element.19), channel_id=1, source_target_pairs={{0,3},{1,2},{2,1},{3,0},{4,7},{5,6},{6,5},{7,4},{8,11},{9,10},{10,... | collective-permute-start | bytes 2433032 | tf_op jit(solution)/shard_map/ppermute | solution.py:409
  9.1 0.7 collective-permute-start.1
  9.8 0.0 copy-done.5
  9.8 0.3 reshape.46
  10.1 0.1 constant_dynamic-slice_fusion
  10.4 0.1 broadcast_in_dim.63
  10.5 0.1 broadcast_in_dim.66
  10.6 0.0 collective-permute-done.5
  10.6 0.0 copy-done.8
  10.6 3.2 %collective-permute-start.6 = (f32[1,128]{1,0:T(1,128)S(1)}, f32[1,128]{1,0:T(1,128)S(1)}, u32[]{:S(2)}, u32[]{:S(2)}) collective-permute-start(f32[1,128]{1,0:T(1,128)S(1)} %fusion.2), channel_id=1, source_target_pairs={{0,0},{1,9},{2,18},{3,27},{4,4},{5,13},{6,22},{7,31},{8,8},{9,17},... | collective-permute-start | bytes 1544 | tf_op jit(solution)/shard_map/ppermute | solution.py:446
  13.9 0.9 select_select_fusion.refs_2_.refs_7_.refs_3_
  14.7 27.8 %stats.1 = f32[8,128]{1,0:T(8,128)} custom-call(bf16[19008,128]{1,0:T(8,128)(2,1)} %bitcast.22, bf16[19008,128]{1,0:T(8,128)(2,1)} %bitcast.15, bf16[36,8,528]{2,1,0:T(8,128)(2,1)} %select_select_fusion.refs_2_.refs_7_.refs_3_), custom_call_target="tpu_custom_call" | custom-call | tf_op jit(solution)/shard_map/stats/pallas_call | solution.py:154
  42.5 0.7 slice.17
  43.2 0.7 slice.16
  43.9 0.0 collective-permute-done.6
  43.9 0.0 copy-start.7
  43.9 0.1 collective-permute-start.9
  44.0 3.0 %collective-permute-done.9.refs_12_ = f32[8,128]{1,0:T(8,128)S(1)} collective-permute-done((f32[8,128]{1,0:T(8,128)S(1)}, f32[8,128]{1,0:T(8,128)S(1)}, u32[]{:S(2)}, u32[]{:S(2)}) %collective-permute-start.9) | collective-permute-done | bytes 4128 | tf_op jit(solution)/shard_map/ppermute | solution.py:409
  47.0 5.1 %collective-permute-start.8 = (f32[8,128]{1,0:T(8,128)S(1)}, f32[8,128]{1,0:T(8,128)S(1)}, u32[]{:S(2)}, u32[]{:S(2)}) collective-permute-start(f32[8,128]{1,0:T(8,128)S(1)} %pad_maximum_fusion.refs_9_), channel_id=1, source_target_pairs={{0,2},{1,3},{2,0},{3,1},{4,6},{5,7},{6,4},{7,5},{8,10},{9,11},{10,... | collective-permute-start | bytes 12296 | tf_op jit(solution)/shard_map/ppermute | solution.py:409
  52.2 1.0 %collective-permute-done.8.refs_11_ = f32[8,128]{1,0:T(8,128)S(1)} collective-permute-done((f32[8,128]{1,0:T(8,128)S(1)}, f32[8,128]{1,0:T(8,128)S(1)}, u32[]{:S(2)}, u32[]{:S(2)}) %collective-permute-start.8) | collective-permute-done | bytes 4128 | tf_op jit(solution)/shard_map/ppermute | solution.py:409
  53.2 1.3 %collective-permute-start.7 = (f32[8,128]{1,0:T(8,128)S(1)}, f32[8,128]{1,0:T(8,128)S(1)}, u32[]{:S(2)}, u32[]{:S(2)}) collective-permute-start(f32[8,128]{1,0:T(8,128)S(1)} %pad_maximum_fusion.refs_9_), channel_id=1, source_target_pairs={{0,1},{1,0},{2,3},{3,2},{4,5},{5,4},{6,7},{7,6},{8,9},{9,8},{10,11... | collective-permute-start | bytes 12296 | tf_op jit(solution)/shard_map/ppermute | solution.py:409
  54.5 0.8 collective-permute-done.7.refs_10_
  55.3 0.5 collective-permute-start.11
  55.8 0.0 collective-permute-done.2.refs_3_
  55.8 1.0 %collective-permute-start.10 = (bf16[1056,128]{1,0:T(8,128)(2,1)}, bf16[1056,128]{1,0:T(8,128)(2,1)S(1)}, u32[]{:S(2)}, u32[]{:S(2)}) collective-permute-start(bf16[1056,128]{1,0:T(8,128)(2,1)} %get-tuple-element.22), channel_id=1, source_target_pairs={{0,2},{1,3},{2,0},{3,1},{4,6},{5,7},{6,4},{7,5},{8,10},{9,11},{10,... | collective-permute-start | bytes 811016 | tf_op jit(solution)/shard_map/ppermute | solution.py:409
  56.8 0.0 collective-permute-done.4.refs_5_
  56.8 0.5 collective-permute-start
  57.3 0.0 copy-done.12
  57.3 0.0 copy-done.13
  57.3 0.0 copy-done.14
  57.3 0.0 copy-done.15
  57.3 0.5 add_add_fusion.refs_0_
  57.8 0.0 collective-permute-done.3.refs_4_
  57.8 0.0 collective-permute-done.1.refs_2_
  57.8 0.0 copy-done.7
  57.8 0.0 copy-done.9
  57.8 0.0 copy-done.10
  57.8 0.0 copy-done.11
  57.8 0.0 copy-done.2
  57.9 0.8 copy-done.1
  58.7 1.1 %copy-done = bf16[4752,128]{1,0:T(8,128)(2,1)} copy-done((bf16[4752,128]{1,0:T(8,128)(2,1)}, bf16[4752,128]{1,0:T(8,128)(2,1)S(1)}, u32[]{:S(2)}) %copy-start) | copy-done | bytes 1216536
  59.8 12.4 %chunk.4 = (bf16[19008,128]{1,0:T(8,128)(2,1)}, f32[16,128]{1,0:T(8,128)}, f32[8,128]{1,0:T(8,128)}) custom-call(s32[42]{0:T(128)} %add_add_fusion.refs_0_, bf16[19008,128]{1,0:T(8,128)(2,1)} %bitcast.23, bf16[4752,128]{1,0:T(8,128)(2,1)} %copy-done, bf16[1584,128]{1,0:T(8,128)(2,1)} %copy-done.2, bf16[3168,128]{1,0:T(8,128)(2,1)} %copy-done.1, ...), custom_call_target="tpu_custom_call" | custom-call | tf_op jit(solution)/shard_map/chunk/pallas_call | solution.py:317
  72.1 0.0 collective-permute-done.11.refs_1_
  72.1 0.7 copy-done.4
  72.9 3.2 %chunk.5 = (bf16[19008,128]{1,0:T(8,128)(2,1)}, f32[16,128]{1,0:T(8,128)}) custom-call(s32[42]{0:T(128)} %add_add_fusion.refs_0_, bf16[1584,128]{1,0:T(8,128)(2,1)} %copy-done.4, bf16[19008,128]{1,0:T(8,128)(2,1)} %bitcast.17, bf16[36,8,528]{2,1,0:T(8,128)(2,1)} %select_select_fusion.refs_2_.refs_7_.refs_3_, ...), custom_call_target="tpu_custom_call", output_to_operand_aliasing={{0}: (7, {})} | custom-call | tf_op jit(solution)/shard_map/chunk/pallas_call | solution.py:317
  76.0 0.0 collective-permute-done.10.refs_1_
  76.1 0.7 copy-done.6
  76.8 3.1 %chunk.6 = (bf16[19008,128]{1,0:T(8,128)(2,1)}, f32[16,128]{1,0:T(8,128)}) custom-call(s32[42]{0:T(128)} %add_add_fusion.refs_0_, bf16[1056,128]{1,0:T(8,128)(2,1)} %copy-done.6, bf16[19008,128]{1,0:T(8,128)(2,1)} %bitcast.18, bf16[36,8,528]{2,1,0:T(8,128)(2,1)} %select_select_fusion.refs_2_.refs_7_.refs_3_, ...), custom_call_target="tpu_custom_call", output_to_operand_aliasing={{0}: (7, {})} | custom-call | tf_op jit(solution)/shard_map/chunk/pallas_call | solution.py:317
  79.9 0.0 collective-permute-done.refs_1_
  79.9 2.6 %chunk.7 = (bf16[19008,128]{1,0:T(8,128)(2,1)}, f32[1,128]{1,0:T(1,128)}) custom-call(s32[42]{0:T(128)} %add_add_fusion.refs_0_, bf16[528,128]{1,0:T(8,128)(2,1)} %collective-permute-done.refs_1_, bf16[19008,128]{1,0:T(8,128)(2,1)} %bitcast.19, bf16[36,8,528]{2,1,0:T(8,128)(2,1)} %select_select_fusion.refs_2_.refs_7_.refs_3_, ...), custom_call_target="tpu_custom_call", output_to_operand_aliasing={{0}: (7, {})} | custom-call | tf_op jit(solution)/shard_map/chunk/pallas_call | solution.py:317
  82.5 2.0 %collective-permute-start.14 = (f32[1,128]{1,0:T(1,128)}, f32[1,128]{1,0:T(1,128)S(1)}, u32[]{:S(2)}, u32[]{:S(2)}) collective-permute-start(f32[1,128]{1,0:T(1,128)} %get-tuple-element.31), channel_id=1, source_target_pairs={{0,3},{1,2},{2,1},{3,0},{4,7},{5,6},{6,5},{7,4},{8,11},{9,10},{10,... | collective-permute-start | bytes 1544 | tf_op jit(solution)/shard_map/ppermute | solution.py:409
  84.6 0.3 collective-permute-start.13
  84.9 0.1 collective-permute-start.12
  85.0 0.9 %collective-permute-done.14 = f32[1,128]{1,0:T(1,128)S(1)} collective-permute-done((f32[1,128]{1,0:T(1,128)}, f32[1,128]{1,0:T(1,128)S(1)}, u32[]{:S(2)}, u32[]{:S(2)}) %collective-permute-start.14) | collective-permute-done | bytes 544 | tf_op jit(solution)/shard_map/ppermute | solution.py:409
  85.9 1.3 %collective-permute-done.13 = f32[1,128]{1,0:T(1,128)S(1)} collective-permute-done((f32[1,128]{1,0:T(1,128)}, f32[1,128]{1,0:T(1,128)S(1)}, u32[]{:S(2)}, u32[]{:S(2)}) %collective-permute-start.13) | collective-permute-done | bytes 544 | tf_op jit(solution)/shard_map/ppermute | solution.py:409
  87.2 0.0 collective-permute-done.12
  87.2 1.2 %add_bitcast_fusion = f32[128]{0:T(128)} fusion(f32[1,128]{1,0:T(1,128)S(1)} %collective-permute-done.14, f32[1,128]{1,0:T(1,128)S(1)} %collective-permute-done.13, f32[1,128]{1,0:T(1,128)} %get-tuple-element.31, f32[1,128]{1,0:T(1,128)S(1)} %collective-permute-done.12), kind=kLoop, calls=%fused_computation.11 | loop fusion | flops 384 | bytes 2560 | tf_op jit(solution)/shard_map/reshape | solution.py:504
  (22 shorter events, 0.2 us)
Async XLA Ops:
  0.6 10.0 %collective-permute-start.5 = (s32[1,128]{1,0:T(1,128)}, s32[1,128]{1,0:T(1,128)S(1)}, u32[]{:S(2)}, u32[]{:S(2)}) collective-permute-start(s32[1,128]{1,0:T(1,128)} %bitcast.26), channel_id=1, source_target_pairs={{0,4},{4,0},{8,12},{12,8},{16,20},{20,16},{24,28},{28,24},{1,5},{5... | collective-permute-start | bytes 1544 | tf_op jit(solution)/shard_map/ppermute | solution.py:436
  0.7 9.1 %copy-start.5 = (s32[76032]{0:T(1024)S(1)}, s32[76032]{0:T(1024)}, u32[]{:S(2)}) copy-start(s32[76032]{0:T(1024)} %param.11) | copy-start | bytes 912388
  0.7 9.9 %copy-start.8 = (s32[128]{0:T(128)S(1)}, s32[128]{0:T(128)}, u32[]{:S(2)}) copy-start(s32[128]{0:T(128)} %param.10) | copy-start | bytes 1540
  2.6 53.2 %collective-permute-start.2 = (bf16[1584,128]{1,0:T(8,128)(2,1)}, bf16[1584,128]{1,0:T(8,128)(2,1)S(1)}, u32[]{:S(2)}, u32[]{:S(2)}) collective-permute-start(bf16[1584,128]{1,0:T(8,128)(2,1)} %cut.3), channel_id=1, source_target_pairs={{0,3},{1,2},{2,1},{3,0},{4,7},{5,6},{6,5},{7,4},{8,11},{9,10},{10,... | collective-permute-start | bytes 1216520 | tf_op jit(solution)/shard_map/ppermute | solution.py:409
  7.9 48.9 %collective-permute-start.4 = (bf16[1584,128]{1,0:T(8,128)(2,1)}, bf16[1584,128]{1,0:T(8,128)(2,1)S(1)}, u32[]{:S(2)}, u32[]{:S(2)}) collective-permute-start(bf16[1584,128]{1,0:T(8,128)(2,1)} %get-tuple-element.20), channel_id=1, source_target_pairs={{0,2},{1,3},{2,0},{3,1},{4,6},{5,7},{6,4},{7,5},{8,10},{9,11},{10,... | collective-permute-start | bytes 1216520 | tf_op jit(solution)/shard_map/ppermute | solution.py:409
  8.0 49.8 %collective-permute-start.3 = (bf16[3168,128]{1,0:T(8,128)(2,1)}, bf16[3168,128]{1,0:T(8,128)(2,1)S(1)}, u32[]{:S(2)}, u32[]{:S(2)}) collective-permute-start(bf16[3168,128]{1,0:T(8,128)(2,1)} %get-tuple-element.19), channel_id=1, source_target_pairs={{0,3},{1,2},{2,1},{3,0},{4,7},{5,6},{6,5},{7,4},{8,11},{9,10},{10,... | collective-permute-start | bytes 2433032 | tf_op jit(solution)/shard_map/ppermute | solution.py:409
  9.1 48.7 %collective-permute-start.1 = (bf16[4752,128]{1,0:T(8,128)(2,1)}, bf16[4752,128]{1,0:T(8,128)(2,1)S(1)}, u32[]{:S(2)}, u32[]{:S(2)}) collective-permute-start(bf16[4752,128]{1,0:T(8,128)(2,1)} %get-tuple-element.18), channel_id=1, source_target_pairs={{0,1},{1,0},{2,3},{3,2},{4,5},{5,4},{6,7},{7,6},{8,9},{9,8},{10,11... | collective-permute-start | bytes 3649544 | tf_op jit(solution)/shard_map/ppermute | solution.py:409
  10.6 33.3 %collective-permute-start.6 = (f32[1,128]{1,0:T(1,128)S(1)}, f32[1,128]{1,0:T(1,128)S(1)}, u32[]{:S(2)}, u32[]{:S(2)}) collective-permute-start(f32[1,128]{1,0:T(1,128)S(1)} %fusion.2), channel_id=1, source_target_pairs={{0,0},{1,9},{2,18},{3,27},{4,4},{5,13},{6,22},{7,31},{8,8},{9,17},... | collective-permute-start | bytes 1544 | tf_op jit(solution)/shard_map/ppermute | solution.py:446
  14.7 42.5 %copy-start.12 = (s32[42]{0:T(128)S(1)}, s32[42]{0:T(128)}, u32[]{:S(2)}) copy-start(s32[42]{0:T(128)} %constant.38.clone) | copy-start | bytes 508
  14.7 42.5 %copy-start.13 = (s32[42]{0:T(128)S(1)}, s32[42]{0:T(128)}, u32[]{:S(2)}) copy-start(s32[42]{0:T(128)} %constant.37.clone) | copy-start | bytes 508
  14.7 42.5 %copy-start.14 = (s32[42]{0:T(128)S(1)}, s32[42]{0:T(128)}, u32[]{:S(2)}) copy-start(s32[42]{0:T(128)} %constant.36.clone) | copy-start | bytes 508
  14.7 42.6 %copy-start.15 = (s32[42]{0:T(128)S(1)}, s32[42]{0:T(128)}, u32[]{:S(2)}) copy-start(s32[42]{0:T(128)} %constant.11.clone) | copy-start | bytes 508
  43.9 13.9 %copy-start.7 = (f32[8,128]{1,0:T(8,128)}, f32[8,128]{1,0:T(8,128)S(1)}, u32[]{:S(2)}) copy-start(f32[8,128]{1,0:T(8,128)S(1)} %pad_maximum_fusion.refs_9_) | copy-start | bytes 12292
  43.9 3.1 %collective-permute-start.9 = (f32[8,128]{1,0:T(8,128)S(1)}, f32[8,128]{1,0:T(8,128)S(1)}, u32[]{:S(2)}, u32[]{:S(2)}) collective-permute-start(f32[8,128]{1,0:T(8,128)S(1)} %pad_maximum_fusion.refs_9_), channel_id=1, source_target_pairs={{0,3},{1,2},{2,1},{3,0},{4,7},{5,6},{6,5},{7,4},{8,11},{9,10},{10,... | collective-permute-start | bytes 12296 | tf_op jit(solution)/shard_map/ppermute | solution.py:409
  47.0 10.8 %copy-start.9 = (f32[8,128]{1,0:T(8,128)}, f32[8,128]{1,0:T(8,128)S(1)}, u32[]{:S(2)}) copy-start(f32[8,128]{1,0:T(8,128)S(1)} %collective-permute-done.9.refs_12_) | copy-start | bytes 12292
  47.0 6.1 %collective-permute-start.8 = (f32[8,128]{1,0:T(8,128)S(1)}, f32[8,128]{1,0:T(8,128)S(1)}, u32[]{:S(2)}, u32[]{:S(2)}) collective-permute-start(f32[8,128]{1,0:T(8,128)S(1)} %pad_maximum_fusion.refs_9_), channel_id=1, source_target_pairs={{0,2},{1,3},{2,0},{3,1},{4,6},{5,7},{6,4},{7,5},{8,10},{9,11},{10,... | collective-permute-start | bytes 12296 | tf_op jit(solution)/shard_map/ppermute | solution.py:409
  53.2 4.7 %copy-start.10 = (f32[8,128]{1,0:T(8,128)}, f32[8,128]{1,0:T(8,128)S(1)}, u32[]{:S(2)}) copy-start(f32[8,128]{1,0:T(8,128)S(1)} %collective-permute-done.8.refs_11_) | copy-start | bytes 12292
  53.2 2.1 %collective-permute-start.7 = (f32[8,128]{1,0:T(8,128)S(1)}, f32[8,128]{1,0:T(8,128)S(1)}, u32[]{:S(2)}, u32[]{:S(2)}) collective-permute-start(f32[8,128]{1,0:T(8,128)S(1)} %pad_maximum_fusion.refs_9_), channel_id=1, source_target_pairs={{0,1},{1,0},{2,3},{3,2},{4,5},{5,4},{6,7},{7,6},{8,9},{9,8},{10,11... | collective-permute-start | bytes 12296 | tf_op jit(solution)/shard_map/ppermute | solution.py:409
  55.3 2.6 %copy-start.11 = (f32[8,128]{1,0:T(8,128)}, f32[8,128]{1,0:T(8,128)S(1)}, u32[]{:S(2)}) copy-start(f32[8,128]{1,0:T(8,128)S(1)} %collective-permute-done.7.refs_10_) | copy-start | bytes 12292
  55.3 16.8 %collective-permute-start.11 = (bf16[1584,128]{1,0:T(8,128)(2,1)}, bf16[1584,128]{1,0:T(8,128)(2,1)S(1)}, u32[]{:S(2)}, u32[]{:S(2)}) collective-permute-start(bf16[1584,128]{1,0:T(8,128)(2,1)} %get-tuple-element.23), channel_id=1, source_target_pairs={{0,2},{1,3},{2,0},{3,1},{4,6},{5,7},{6,4},{7,5},{8,10},{9,11},{10,... | collective-permute-start | bytes 1216520 | tf_op jit(solution)/shard_map/ppermute | solution.py:409
  55.8 2.1 %copy-start.2 = (bf16[1584,128]{1,0:T(8,128)(2,1)}, bf16[1584,128]{1,0:T(8,128)(2,1)S(1)}, u32[]{:S(2)}) copy-start(bf16[1584,128]{1,0:T(8,128)(2,1)S(1)} %collective-permute-done.2.refs_3_) | copy-start | bytes 1216516
  55.8 20.3 %collective-permute-start.10 = (bf16[1056,128]{1,0:T(8,128)(2,1)}, bf16[1056,128]{1,0:T(8,128)(2,1)S(1)}, u32[]{:S(2)}, u32[]{:S(2)}) collective-permute-start(bf16[1056,128]{1,0:T(8,128)(2,1)} %get-tuple-element.22), channel_id=1, source_target_pairs={{0,2},{1,3},{2,0},{3,1},{4,6},{5,7},{6,4},{7,5},{8,10},{9,11},{10,... | collective-permute-start | bytes 811016 | tf_op jit(solution)/shard_map/ppermute | solution.py:409
  56.8 1.1 %copy-start.3 = (bf16[1584,128]{1,0:T(8,128)(2,1)}, bf16[1584,128]{1,0:T(8,128)(2,1)S(1)}, u32[]{:S(2)}) copy-start(bf16[1584,128]{1,0:T(8,128)(2,1)S(1)} %collective-permute-done.4.refs_5_) | copy-start | bytes 1216516
  56.8 23.1 %collective-permute-start = (bf16[528,128]{1,0:T(8,128)(2,1)}, bf16[528,128]{1,0:T(8,128)(2,1)}, u32[]{:S(2)}, u32[]{:S(2)}) collective-permute-start(bf16[528,128]{1,0:T(8,128)(2,1)} %get-tuple-element.17), channel_id=1, source_target_pairs={{0,2},{1,3},{2,0},{3,1},{4,6},{5,7},{6,4},{7,5},{8,10},{9,11},{10,... | collective-permute-start | bytes 405512 | tf_op jit(solution)/shard_map/ppermute | solution.py:409
  57.8 0.9 %copy-start.1 = (bf16[3168,128]{1,0:T(8,128)(2,1)}, bf16[3168,128]{1,0:T(8,128)(2,1)S(1)}, u32[]{:S(2)}) copy-start(bf16[3168,128]{1,0:T(8,128)(2,1)S(1)} %collective-permute-done.3.refs_4_) | copy-start | bytes 2433028
  58.7 1.1 %copy-start = (bf16[4752,128]{1,0:T(8,128)(2,1)}, bf16[4752,128]{1,0:T(8,128)(2,1)S(1)}, u32[]{:S(2)}) copy-start(bf16[4752,128]{1,0:T(8,128)(2,1)S(1)} %collective-permute-done.1.refs_2_) | copy-start | bytes 3649540
  72.1 0.7 copy-start.4
  76.1 0.7 copy-start.6
  82.5 3.3 %collective-permute-start.14 = (f32[1,128]{1,0:T(1,128)}, f32[1,128]{1,0:T(1,128)S(1)}, u32[]{:S(2)}, u32[]{:S(2)}) collective-permute-start(f32[1,128]{1,0:T(1,128)} %get-tuple-element.31), channel_id=1, source_target_pairs={{0,3},{1,2},{2,1},{3,0},{4,7},{5,6},{6,5},{7,4},{8,11},{9,10},{10,... | collective-permute-start | bytes 1544 | tf_op jit(solution)/shard_map/ppermute | solution.py:409
  84.6 2.6 %collective-permute-start.13 = (f32[1,128]{1,0:T(1,128)}, f32[1,128]{1,0:T(1,128)S(1)}, u32[]{:S(2)}, u32[]{:S(2)}) collective-permute-start(f32[1,128]{1,0:T(1,128)} %get-tuple-element.31), channel_id=1, source_target_pairs={{0,2},{1,3},{2,0},{3,1},{4,6},{5,7},{6,4},{7,5},{8,10},{9,11},{10,... | collective-permute-start | bytes 1544 | tf_op jit(solution)/shard_map/ppermute | solution.py:409
  84.9 2.3 %collective-permute-start.12 = (f32[1,128]{1,0:T(1,128)}, f32[1,128]{1,0:T(1,128)S(1)}, u32[]{:S(2)}, u32[]{:S(2)}) collective-permute-start(f32[1,128]{1,0:T(1,128)} %get-tuple-element.31), channel_id=1, source_target_pairs={{0,1},{1,0},{2,3},{3,2},{4,5},{5,4},{6,7},{7,6},{8,9},{9,8},{10,11... | collective-permute-start | bytes 1544 | tf_op jit(solution)/shard_map/ppermute | solution.py:409

commit v3 on v2

--- a/solution.py
+++ b/solution.py
@@ -12,7 +12,9 @@
 LOW = -3e38
 ROWS = 16
 LINES = 8
+HELD_BYTES = 3 * 2**20
 WAYS = 3
+AHEAD = 1
 STEP = 544
 LN2 = 0.6931471805599453
 F32 = jnp.float32
@@ -72,14 +74,14 @@
         for k in range(tiles):
             tile = pl.ds(pl.multiple_of(n * step + k * ROWS, ROWS), ROWS)
             at = k % WAYS
-            tops[at] = jnp.maximum(tops[at], t_ref[tile, :])
-            tops[WAYS + at] = jnp.maximum(tops[WAYS + at], s_ref[tile, :])
+            tops[at] = jnp.maximum(tops[at], t_ref[tile, :].astype(F32))
+            tops[WAYS + at] = jnp.maximum(tops[WAYS + at], s_ref[tile, :].astype(F32))
         return tuple(tops)
 
-    low = jnp.full((ROWS, lanes), LOW, BF16)
-    highs = lax.fori_loop(0, steps, first, (low,) * (2 * WAYS))
+    low = jnp.full((ROWS, lanes), LOW, F32)
+    highs = lax.fori_loop(0, steps, first, (low,) * (2 * WAYS), unroll=True)
     t_top, s_top = [
-        jnp.max(functools.reduce(jnp.maximum, highs[k:k + WAYS]).astype(F32), axis=0, keepdims=True)
+        jnp.max(functools.reduce(jnp.maximum, highs[k:k + WAYS]), axis=0, keepdims=True)
         for k in (0, WAYS)]
     weights = addend_rows([t_top, s_top], [0, 1], 1)
 
@@ -186,7 +188,7 @@
     return jnp.concatenate([t_lse + LN2, s_lse - jnp.log(0.5 + weight), weight, base, blank], axis=0)
 
 
-def chunk_kernel(spots, *refs, spans, slot, step, cols, shares, tokens, last):
+def chunk_kernel(spots, *refs, spans, slot, step, cols, shares, tokens):
     pieces, refs = refs[:len(spans)], refs[len(spans):]
     s_ref, b_ref, tgt_ref = refs[:3]
     refs = refs[3:]
@@ -201,21 +203,11 @@
             vec_ref[...] = join_stats(share_refs, tgt_ref[...], tokens)
             d_out[...] = jnp.zeros(d_out.shape, F32)
     else:
-        vec_ref, d_in, _, g_ref, d_out = refs[:5]
-        if last:
-            d_sum = refs[5]
-        else:
-            d_sum = d_out
-
-            @pl.when(g == 0)
-            def _():
-                d_out[...] = d_in[...]
-    if shares:
-        d_sum = d_out
-    if last:
+        vec_ref, d_in, _, g_ref, d_out = refs
+
         @pl.when(g == 0)
         def _():
-            d_sum[...] = d_in[...]
+            d_out[...] = d_in[...]
 
     @pl.when(g == 0)
     def _():
@@ -248,29 +240,25 @@
             picked = picked + fold(jnp.sum, jnp.where(hit, s, 0.0))
             return (div, picked)
 
-        div, picked = lax.fori_loop(0, rows // step, body, (d_sum[0:8, :], d_sum[8:16, :]), unroll=True)
-        d_sum[0:8, :] = div
-        d_sum[8:16, :] = picked
+        div, picked = lax.fori_loop(0, rows // step, body, (d_out[0:8, :], d_out[8:16, :]), unroll=True)
+        d_out[0:8, :] = div
+        d_out[8:16, :] = picked
 
     done = 0
-    for ref, length in zip(pieces, spans):
+    for ref, (length, held) in zip(pieces, spans):
+        first = pl.multiple_of((g - done) * rows, rows) if held else 0
         if len(pieces) == 1:
-            run(ref, pl.multiple_of(g * rows, rows))
+            run(ref, first)
         else:
-            pl.when((g >= done) & (g < done + length))(functools.partial(run, ref))
+            pl.when((g >= done) & (g < done + length))(functools.partial(run, ref, first))
         done += length
-    if last:
-        @pl.when(g == pl.num_programs(0) - 1)
-        def _():
-            mixed = d_sum[0:8, :] - wide_rows(vec_ref[2:3, :], 8) * d_sum[8:16, :]
-            d_out[...] = jnp.sum(mixed, axis=0, keepdims=True) + vec_ref[3:4, :]
-
-
-def run_chunk(spots, slot, rows, pieces, student, bias, target, cols, stats=(), tokens=0, state=None, last=False):
+
+
+def run_chunk(spots, slot, rows, pieces, student, bias, target, cols, stats=(), tokens=0, state=None):
     _, lanes = student.shape
     step = bias.shape[-1]
     lines = (rows // step,) + bias.shape[1:]
-    spans = [length for _, length, _ in pieces]
+    spans = [(length, local is None) for _, length, local in pieces]
     moved = pl.BlockSpec((rows, lanes), lambda g, pref: (pref[3 * (slot + g)], 0))
     after = pl.BlockSpec(lines, lambda g, pref: (pref[3 * (slot + g)], 0, 0))
 
@@ -284,8 +272,11 @@
             mine = jnp.clip(g - done, 0, length - 1)
             return ((pref[3 * (slot + done + mine)] if local else mine), 0)
 
-        held = pl.BlockSpec(memory_space=pltpu.VMEM)
-        in_specs.append(held if len(pieces) == 1 else pl.BlockSpec((rows, lanes), where))
+        if local is None:
+            in_specs.append(pl.BlockSpec(memory_space=pltpu.VMEM))
+            array = pltpu.with_memory_space_constraint(array, pltpu.VMEM)
+        else:
+            in_specs.append(pl.BlockSpec((rows, lanes), where))
         operands.append(array)
         done += length
     in_specs += [moved, after, fixed(1)]
@@ -293,7 +284,6 @@
     out_shape = [jax.ShapeDtypeStruct(student.shape, BF16)]
     out_specs = [moved]
     aliases = {}
-    scratch = []
     if stats:
         in_specs += [fixed(8)] * len(stats)
         operands += list(stats)
@@ -304,22 +294,19 @@
         in_specs += [fixed(8), fixed(16), pl.BlockSpec(memory_space=pl.ANY)]
         operands += [vec, div, grad]
         aliases = {len(operands) - 1: 0}
-        height = 1 if last else 16
-        out_shape.append(jax.ShapeDtypeStruct((height, lanes), F32))
-        out_specs.append(fixed(height))
-        if last:
-            scratch = [pltpu.VMEM((16, lanes), F32)]
-    scratch.append(pltpu.VMEM((LINES, 2 * lanes), BF16))
+        out_shape.append(jax.ShapeDtypeStruct((16, lanes), F32))
+        out_specs.append(fixed(16))
+    scratch = [pltpu.VMEM((LINES, 2 * lanes), BF16)]
 
     def kernel(*refs):
-        chunk_kernel(*refs, spans=spans, slot=slot, step=step, cols=cols, shares=len(stats), tokens=tokens, last=last)
+        chunk_kernel(*refs, spans=spans, slot=slot, step=step, cols=cols, shares=len(stats), tokens=tokens)
 
     return pl.pallas_call(
         kernel,
         out_shape=tuple(out_shape),
         grid_spec=pltpu.PrefetchScalarGridSpec(
             num_scalar_prefetch=1,
-            grid=(sum(spans),),
+            grid=(sum(length for length, _ in spans),),
             in_specs=in_specs,
             out_specs=tuple(out_specs),
             scratch_shapes=scratch,
@@ -328,6 +315,93 @@
         compiler_params=pltpu.CompilerParams(dimension_semantics=("arbitrary",)),
         name="chunk",
     )(*operands)
+
+
+def hits(base, r, tgt_ref, step, lanes, limit):
+    gap = wide_rows(tgt_ref[...], 8) - lax.broadcasted_iota(jnp.int32, (8, lanes), 0) - (base + r)
+    line = jnp.where((gap & 7) == 0, gap >> 3, -1)
+    tile = lax.broadcasted_iota(jnp.int32, (step // 8, 8, lanes), 0)
+    hit = (tile == line[None]).reshape(step, lanes)
+    if limit is not None:
+        hit = hit & (lax.broadcasted_iota(jnp.int32, (step, lanes), 0) < limit - r)
+    return hit
+
+
+def tail_sum_kernel(t_ref, s_ref, m_ref, vec_ref, tgt_ref, d_ref, o_ref, *, first_id, limit):
+    rows, lanes = t_ref.shape
+    step = m_ref.shape[-1]
+    weights = addend_rows([vec_ref[0:1, :]], [1], 3)
+    base = first_id()
+    div = jnp.zeros((8, lanes), F32)
+    picked = jnp.zeros((8, lanes), F32)
+    for n in range(rows // step):
+        t = t_ref[n * step:(n + 1) * step, :].astype(F32)
+        s = s_ref[n * step:(n + 1) * step, :].astype(F32)
+        tp = jnp.exp(t + addend(m_ref, n, weights))
+        div = div + fold(jnp.sum, tp * (t - s))
+        hit = hits(base, n * step, tgt_ref, step, lanes, limit)
+        picked = picked + fold(jnp.sum, jnp.where(hit, s, 0.0))
+    total = div - wide_rows(vec_ref[2:3, :], 8) * picked
+    o_ref[...] = jnp.sum(total, axis=0, keepdims=True) + d_ref[...]
+
+
+def tail_grad_kernel(t_ref, s_ref, m_ref, vec_ref, tgt_ref, _, g_ref, out, sems, *, first_id, first_row, limit):
+    rows, lanes = t_ref.shape
+    step = m_ref.shape[-1]
+    weights = addend_rows([vec_ref[0:1, :], vec_ref[1:2, :]], [1, 1], 3)
+    weight = wide_rows(vec_ref[2:3, :], step)
+    base = first_id()
+    row = first_row()
+    copies = []
+    for n in range(rows // step):
+        part = pl.ds(n * step, step)
+        both = addend(m_ref, n, weights)
+        tp = jnp.exp(t_ref[part, :].astype(F32) + both[:, :lanes])
+        sp = jnp.exp(s_ref[part, :].astype(F32) + both[:, lanes:])
+        hit = hits(base, n * step, tgt_ref, step, lanes, limit)
+        out[part, :] = ((sp - tp) - jnp.where(hit, weight, 0.0)).astype(BF16)
+        place = pl.ds(pl.multiple_of(row + n * step, ROWS), step)
+        copies.append(pltpu.make_async_copy(out.at[part, :], g_ref.at[place, :], sems.at[n]))
+        copies[-1].start()
+    for copy in copies:
+        copy.wait()
+
+
+def held(value):
+    return pltpu.with_memory_space_constraint(value, pltpu.VMEM)
+
+
+def run_tail_sum(operands, first_id, limit):
+    lanes = operands[0].shape[1]
+
+    def kernel(*refs):
+        tail_sum_kernel(*refs, first_id=first_id, limit=limit)
+
+    return pl.pallas_call(
+        kernel,
+        out_shape=jax.ShapeDtypeStruct((1, lanes), F32),
+        in_specs=[pl.BlockSpec(memory_space=pltpu.VMEM)] * len(operands),
+        out_specs=pl.BlockSpec(memory_space=pltpu.VMEM),
+        name="tail_sum",
+    )(*[held(value) for value in operands])
+
+
+def run_tail_grad(operands, grad, first_id, first_row, limit):
+    rows, lanes = operands[0].shape
+    step = operands[2].shape[-1]
+
+    def kernel(*refs):
+        tail_grad_kernel(*refs, first_id=first_id, first_row=first_row, limit=limit)
+
+    return pl.pallas_call(
+        kernel,
+        out_shape=jax.ShapeDtypeStruct(grad.shape, grad.dtype),
+        in_specs=[pl.BlockSpec(memory_space=pltpu.VMEM)] * len(operands) + [pl.BlockSpec(memory_space=pl.ANY)],
+        out_specs=pl.BlockSpec(memory_space=pl.ANY),
+        scratch_shapes=[pltpu.VMEM((rows, lanes), BF16), pltpu.SemaphoreType.DMA((rows // step,))],
+        input_output_aliases={len(operands): 0},
+        name="tail_grad",
+    )(*[held(value) for value in operands], grad)
 
 
 def cut_kernel(t_ref, *rest, parts, held, partner):
@@ -379,8 +453,8 @@
         if chunked and index == 0:
             pieces += [(shift, 0, big, big), (shift, big, 2 * big, big)]
         elif chunked and index == len(far) - 1:
-            pieces += [(shift, 0, big, big), (shift, big, big, big), (shift, 2 * big, 2 * small, small),
-                       (shift, 2 * big + 2 * small, small, small)]
+            pieces += [(shift, 0, AHEAD * small, small), (shift, AHEAD * small, (6 - AHEAD) * small, small),
+                       (shift, 2 * big, big, big)]
         else:
             pieces.append((shift, 0, padded, big))
     late = [k for k, piece in enumerate(pieces) if len(far) > 1 and piece[0] == far[-1] and (piece[1] or not chunked)]
@@ -439,8 +513,10 @@
         merged *= 2
         step += 1
     left = tok_count // merged
+    even = left & (left - 1) == 0
     pairs = [
-        (t * voc_count + v, ((t // merged + v) % left * merged + t % merged) * voc_count + v)
+        (t * voc_count + v,
+         ((t // merged ^ v if even else (t // merged + v) % left) * merged + t % merged) * voc_count + v)
         for t in range(tok_count) for v in range(left)
     ]
     kept = lax.ppermute(kept, ("tok", "voc"), pairs)
@@ -460,7 +536,7 @@
     bias = jnp.where(kind == 0, line[0], jnp.where(kind == 1, line[1], ones))
 
     stats = run_stats(flat, student, bias, 1600)
-    stats = jnp.concatenate([stats[:4], kept, stats[5:]], axis=0)
+    stats = jnp.where(lax.broadcasted_iota(jnp.int32, stats.shape, 0) == 4, kept, stats)
     gathered = [stats]
     for shift in range(1, voc_count):
         gathered.append(swap(stats, shift))
@@ -476,14 +552,28 @@
         return size // rows
 
     groups = []
+    held = [pair[1] for pair in sorted((piece[2], k) for k, piece in enumerate(pieces))]
+    held = late + [k for k in reversed(held) if k in early]
+    size = 0
+    for n, k in enumerate(held):
+        size += pieces[k][2] * tok_rows * 2
+        if size > HELD_BYTES:
+            held = held[:n]
+            break
     first = [(flat, note(0, 0, padded, big), True)]
     for k in sorted(early, key=lambda k: k < len(pieces) - 1):
-        first.append((arrived[k], note(*pieces[k]), False))
+        if pieces[k][3] == big:
+            first.append((arrived[k], note(*pieces[k]), None if k in held else False))
     used = sum(length for _, length, _ in first)
+    apart = [k for k in early if pieces[k][3] != big]
     for k in late:
-        length = note(*pieces[k])
-        groups.append((used, pieces[k][3], [(arrived[k], length, False)]))
-        used += length
+        group = []
+        start = used
+        for j in apart + [k]:
+            group.append((arrived[j], note(*pieces[j]), None if j in held else False))
+            used += group[-1][1]
+        groups.append((start, pieces[k][3], group))
+        apart = []
     blocks = source(voc_index, np.array(shift_of, np.int32))
     spots = blocks * np.array(scale, np.int32) + voc_index * np.array(own, np.int32) + np.array(fixed, np.int32)
     spots = spots.astype(jnp.int32)
@@ -491,11 +581,28 @@
     cols = block_cols if split else None
     grad, div, vec = run_chunk(
         spots, 0, big, first, student, bias, target, cols, stats=gathered, tokens=tok_rows * tok_count)
-    for n, (slot, rows, piece) in enumerate(groups):
-        grad, div = run_chunk(
-            spots, slot, rows, piece, student, bias, target, cols, state=(vec, div, grad),
-            last=n == len(groups) - 1)
-    if not groups:
+    for slot, rows, piece in groups[:-1]:
+        grad, div = run_chunk(spots, slot, rows, piece, student, bias, target, cols, state=(vec, div, grad))
+    if groups:
+        shift, start, size, _ = pieces[late[-1]]
+
+        def first_row(me=None):
+            return source(lax.axis_index("voc") if me is None else me, shift) * padded + start
+
+        def first_id():
+            me = lax.axis_index("voc")
+            return (source(me, shift) * voc_count + me) * block_cols + start
+
+        step = bias.shape[-1]
+        row = first_row(voc_index)
+        rows = lax.dynamic_slice(student, (row, 0), (size, tok_rows))
+        lines = lax.dynamic_slice(bias, (row // step, 0, 0), (size // step,) + bias.shape[1:])
+        operands = [arrived[late[-1]], rows, lines, vec, target]
+        limit = block_cols - start if split else None
+        div = jnp.sum(div[:8] - vec[2:3] * div[8:], axis=0, keepdims=True) + vec[3:4]
+        div = run_tail_sum(operands + [div], first_id, limit)
+        grad = run_tail_grad(operands, grad, first_id, first_row, limit)
+    else:
         div = jnp.sum(div[:8] - vec[2:3] * div[8:], axis=0, keepdims=True) + vec[3:4]
     loss = div
     for shift in range(1, voc_count):

time: 89.1 us -> 83.4 us (0.936)
  waiting for transfers between devices: 7.09 us -> 3.01 us
  Pallas kernels: 53.9 us -> 50.5 us
    pallas_call x4 -> x2, Pallas kernels: 21.3 us -> 16.7 us  [run_chunk(): pl.pallas_call(kernel, out_shape=tuple(out_shape), grid_spec=pltpu.Prefet...]
    ppermute x13 -> x12, waiting for transfers between devices: 7.09 us -> 3.01 us  [swap(): lax.ppermute(value, 'voc', [(i, partner(i, shift)) for i in range(voc_cou...]
    pallas_call x0 -> x2, Pallas kernels: none -> 2.22 us  [the longest x1 1.24 us: run_tail_grad(): pl.pallas_call(kernel, out_shape=jax.ShapeDtypeStruct(grad.shape, grad.dt...]
    unnamed x33 -> x27, local copies, waits for them, and re-layouts: 3.4 us -> 1.42 us
    dynamic_slice x0 -> x2, local copies, waits for them, and re-layouts: none -> 1.78 us  [the longest x1 1.03 us: body(): rows = lax.dynamic_slice(student, (row, 0), (size, tok_rows))]
    slice x2 -> x0, local copies, waits for them, and re-layouts: 1.36 us -> none  [body(): stats = jnp.concatenate([stats[:4], kept, stats[5:]], axis=0)]
    pallas_call x1, Pallas kernels: 27.8 us -> 26.8 us  [run_stats(): pl.pallas_call(kernel, out_shape=jax.ShapeDtypeStruct((8, lanes), F32), g...]
    reshape x1, local copies, waits for them, and re-layouts: 0.27 us -> 1.23 us  [body(): flags = vocab_used.reshape(voc_count, voc_count, block_cols)]
  transfers between devices with their start and end apart: 15 -> 14, of which waited for: 5 -> 4; matrix products, arithmetic and copies ran while one was open for 4% -> 8% of each run, Pallas kernels for 58% -> 60%
where the time goes in v3:
time: 83.4 us; the launch traced here: 82.6 us
  Pallas kernels  50.5 us (61%)
  starting transfers between devices  19.2 us (23%)
  local copies, waits for them, and re-layouts  5.48 us (7%)
  other arithmetic  3.44 us (4%)
  waiting for transfers between devices  3.01 us (4%)
  between operations  0.89 us (1%)
    pallas_call x1, Pallas kernels, run_stats(): pl.pallas_call(kernel, out_shape=jax.ShapeDtypeStruct((8, lanes), F32), g...  26.8 us
    pallas_call x2, Pallas kernels, run_chunk(): pl.pallas_call(kernel, out_shape=tuple(out_shape), grid_spec=pltpu.Prefet...  16.7 us
    ppermute x12, starting transfers between devices, swap(): lax.ppermute(value, 'voc', [(i, partner(i, shift)) for i in range(voc_cou...  16 us
    pallas_call x2, Pallas kernels, cut(): pl.pallas_call(kernel, out_shape=tuple((jax.ShapeDtypeStruct((size, lanes...  4.78 us
    ppermute x1, starting transfers between devices, body(): kept = lax.ppermute(kept, ('tok', 'voc'), pairs)  3.2 us
    ppermute x12, waiting for transfers between devices, swap(): lax.ppermute(value, 'voc', [(i, partner(i, shift)) for i in range(voc_cou...  3.01 us
  transfers between devices with their start and end apart: 14, of which 4 were waited for; matrix products, arithmetic and copies ran while one was open for 8% of the time, Pallas kernels for 60%

profile of v3, /device:TPU:5, one launch (start us, length us, event | category | flops | bytes accessed | tf_op | source)
XLA Modules:
  0.0 82.6 jit_solution(6175002496214407730)
XLA Ops:
  0.6 0.1 collective-permute-start.4
  0.7 3.0 %cut.2 = (bf16[3168,128]{1,0:T(8,128)(2,1)}, bf16[528,128]{1,0:T(8,128)(2,1)}, bf16[2640,128]{1,0:T(8,128)(2,1)}, bf16[1584,128]{1,0:T(8,128)(2,1)}, bf16[4752,128]{1,0:T(8,128)(2,1)}) custom-call(bf16[4,4752,128]{2,1,0:T(8,128)(2,1)} %bitcast.27), custom_call_target="tpu_custom_call" | custom-call | tf_op jit(solution)/shard_map/cut/pallas_call | solution.py:434
  3.7 0.0 copy-start.1
  3.8 0.7 collective-permute-start.1
  4.5 1.7 %collective-permute-start.3 = (bf16[3168,128]{1,0:T(8,128)(2,1)}, bf16[3168,128]{1,0:T(8,128)(2,1)S(1)}, u32[]{:S(2)}, u32[]{:S(2)}) collective-permute-start(bf16[3168,128]{1,0:T(8,128)(2,1)} %get-tuple-element.14), channel_id=1, source_target_pairs={{0,3},{1,2},{2,1},{3,0},{4,7},{5,6},{6,5},{7,4},{8,11},{9,10},{10,... | collective-permute-start | bytes 2433032 | tf_op jit(solution)/shard_map/ppermute | solution.py:483
  6.1 1.8 %cut.3 = bf16[1584,128]{1,0:T(8,128)(2,1)} custom-call(bf16[4,4752,128]{2,1,0:T(8,128)(2,1)} %bitcast.28), custom_call_target="tpu_custom_call" | custom-call | tf_op jit(solution)/shard_map/cut/pallas_call | solution.py:434
  7.9 0.2 collective-permute-start.2
  8.1 1.7 %collective-permute-start.10 = (bf16[2640,128]{1,0:T(8,128)(2,1)}, bf16[2640,128]{1,0:T(8,128)(2,1)S(1)}, u32[]{:S(2)}, u32[]{:S(2)}) collective-permute-start(bf16[2640,128]{1,0:T(8,128)(2,1)} %get-tuple-element.17), channel_id=1, source_target_pairs={{0,2},{1,3},{2,0},{3,1},{4,6},{5,7},{6,4},{7,5},{8,10},{9,11},{10,... | collective-permute-start | bytes 2027528 | tf_op jit(solution)/shard_map/ppermute | solution.py:483
  9.8 1.2 %reshape.46 = s32[4,4,4752]{2,1,0:T(4,128)S(1)} reshape(s32[76032]{0:T(1024)} %param.11) | data formatting | bytes 608256 | tf_op jit(solution)/shard_map/reshape | solution.py:524
  11.0 0.1 constant_dynamic-slice_fusion.1
  11.3 0.1 broadcast_in_dim.76
  11.4 0.1 broadcast_in_dim.79
  11.5 0.9 %select_select_fusion.refs_2_.refs_6_.refs_4_ = bf16[36,8,528]{2,1,0:T(8,128)(2,1)} fusion(pred[8]{0:T(512)(128)(4,1)S(1)} %get-tuple-element.24, pred[8]{0:T(512)(128)(4,1)S(1)} %get-tuple-element.25, bf16[8]{0:T(256)(128)(2,1)S(1)} %fusion, bf16[36,528]{1,0:T(8,128)(2,1)S(1)} %broadcast_in_dim.79, bf16[36,528]{1,0:T(8,128)(2,1)S(1)} %broadcast_in_dim.76), kind=kLoop, calls=%fused_computation.1 | loop fusion | flops 304128 | bytes 380192 | tf_op jit(solution)/shard_map/jit(_where)/select_n | solution.py:536
  12.4 0.0 collective-permute-done.4
  12.4 0.0 copy-done.1
  12.4 3.2 %collective-permute-start.5 = (f32[1,128]{1,0:T(1,128)S(1)}, f32[1,128]{1,0:T(1,128)S(1)}, u32[]{:S(2)}, u32[]{:S(2)}) collective-permute-start(f32[1,128]{1,0:T(1,128)S(1)} %fusion.2), channel_id=1, source_target_pairs={{0,0},{1,9},{2,18},{3,27},{4,4},{5,13},{6,22},{7,31},{8,8},{9,1},{... | collective-permute-start | bytes 1544 | tf_op jit(solution)/shard_map/ppermute | solution.py:522
  15.6 0.0 copy-start.9
  15.6 0.0 copy-start.10
  15.7 0.0 copy-start.11
  15.7 0.0 copy-start.12
  15.7 26.8 %stats.1 = f32[8,128]{1,0:T(8,128)} custom-call(bf16[19008,128]{1,0:T(8,128)(2,1)} %bitcast.29, bf16[19008,128]{1,0:T(8,128)(2,1)} %bitcast.31, bf16[36,8,528]{2,1,0:T(8,128)(2,1)} %select_select_fusion.refs_2_.refs_6_.refs_4_), custom_call_target="tpu_custom_call" | custom-call | tf_op jit(solution)/shard_map/stats/pallas_call | solution.py:156
  42.4 0.0 collective-permute-done.5
  42.4 0.8 broadcast_select_fusion.refs_8_
  43.2 0.0 collective-permute-start.6
  43.2 1.0 %dynamic-slice_bitcast_fusion.refs_1_ = bf16[1584,128]{1,0:T(8,128)(2,1)S(1)} fusion(bf16[128,19008]{0,1:T(8,128)(2,1)} %param.9, s32[]{:T(128)S(6)} %select_n.42), kind=kLoop, calls=%fused_computation | loop fusion | bytes 811012 | tf_op jit(solution)/shard_map/dynamic_slice | solution.py:598
  44.2 0.1 collective-permute-done.6.refs_9_
  44.4 4.9 %collective-permute-start.7 = (f32[8,128]{1,0:T(8,128)S(1)}, f32[8,128]{1,0:T(8,128)S(1)}, u32[]{:S(2)}, u32[]{:S(2)}) collective-permute-start(f32[8,128]{1,0:T(8,128)S(1)} %broadcast_select_fusion.refs_8_), channel_id=1, source_target_pairs={{0,2},{1,3},{2,0},{3,1},{4,6},{5,7},{6,4},{7,5},{8,10},{9,11},{10,... | collective-permute-start | bytes 12296 | tf_op jit(solution)/shard_map/ppermute | solution.py:483
  49.3 0.0 copy-done.9
  49.3 0.0 copy-done.10
  49.3 0.0 copy-done.11
  49.3 0.0 copy-done.12
  49.3 0.5 add_add_fusion.refs_0_
  49.8 0.5 collective-permute-done.7.refs_10_
  50.2 0.6 copy-done.6
  50.8 3.0 %collective-permute-start.8 = (f32[8,128]{1,0:T(8,128)S(1)}, f32[8,128]{1,0:T(8,128)S(1)}, u32[]{:S(2)}, u32[]{:S(2)}) collective-permute-start(f32[8,128]{1,0:T(8,128)S(1)} %broadcast_select_fusion.refs_8_), channel_id=1, source_target_pairs={{0,3},{1,2},{2,1},{3,0},{4,7},{5,6},{6,5},{7,4},{8,11},{9,10},{10,... | collective-permute-start | bytes 12296 | tf_op jit(solution)/shard_map/ppermute | solution.py:483
  53.8 0.8 constant_dynamic-slice_fusion.refs_2_
  54.5 0.5 collective-permute-done.8.refs_11_
  55.1 0.3 collective-permute-start.9
  55.3 0.0 collective-permute-done.2.refs_3_
  55.3 0.7 copy-done.3
  56.1 1.2 %collective-permute-start = (bf16[1584,128]{1,0:T(8,128)(2,1)}, bf16[1584,128]{1,0:T(8,128)(2,1)S(1)}, u32[]{:S(2)}, u32[]{:S(2)}) collective-permute-start(bf16[1584,128]{1,0:T(8,128)(2,1)} %get-tuple-element.12), channel_id=1, source_target_pairs={{0,2},{1,3},{2,0},{3,1},{4,6},{5,7},{6,4},{7,5},{8,10},{9,11},{10,... | collective-permute-start | bytes 1216520 | tf_op jit(solution)/shard_map/ppermute | solution.py:483
  57.3 0.0 collective-permute-done.3.refs_4_
  57.3 0.0 copy-done.7
  57.3 0.0 collective-permute-done.1.refs_2_
  57.3 0.0 copy-done.4
  57.3 0.0 copy-done.5
  57.3 10.8 %chunk.2 = (bf16[19008,128]{1,0:T(8,128)(2,1)}, f32[16,128]{1,0:T(8,128)}, f32[8,128]{1,0:T(8,128)}) custom-call(s32[48]{0:T(128)} %add_add_fusion.refs_0_, bf16[19008,128]{1,0:T(8,128)(2,1)} %bitcast.30, bf16[4752,128]{1,0:T(8,128)(2,1)S(1)} %collective-permute-done.1.refs_2_, bf16[1584,128]{1,0:T(8,128)(2,1)} %copy-done.3, ...), custom_call_target="tpu_custom_call" | custom-call | tf_op jit(solution)/shard_map/chunk/pallas_call | solution.py:304
  68.2 0.7 slice_bitcast_fusion
  68.9 0.0 collective-permute-done.9.refs_1_
  68.9 0.0 collective-permute-done.10.refs_2_
  68.9 0.0 copy-start.2
  68.9 5.9 %chunk.3 = (bf16[19008,128]{1,0:T(8,128)(2,1)}, f32[16,128]{1,0:T(8,128)}) custom-call(s32[48]{0:T(128)} %add_add_fusion.refs_0_, bf16[528,128]{1,0:T(8,128)(2,1)} %collective-permute-done.9.refs_1_, bf16[2640,128]{1,0:T(8,128)(2,1)S(1)} %collective-permute-done.10.refs_2_, bf16[19008,128]{1,0:T(8,128)(2,1)} %bitcast.33, ...), custom_call_target="tpu_custom_call", output_to_operand_aliasing={{0}: (8, {})} | custom-call | tf_op jit(solution)/shard_map/chunk/pallas_call | solution.py:304
  74.8 0.7 subtract_reduce_fusion
  75.5 0.0 copy-done
  75.5 0.0 collective-permute-done.refs_0_
  75.5 1.0 %tail_sum.1 = f32[1,128]{1,0:T(1,128)} custom-call(bf16[1584,128]{1,0:T(8,128)(2,1)S(1)} %collective-permute-done.refs_0_, bf16[1584,128]{1,0:T(8,128)(2,1)S(1)} %dynamic-slice_bitcast_fusion.refs_1_, bf16[3,8,528]{2,1,0:T(8,128)(2,1)S(1)} %constant_dynamic-slice_fusion.refs_2_, f32[8,128]{1,0:T(8,128)S(1)} %copy-done, s32[1,128]{1,0:T(1,128)S(1)} %bitcast.25, ...), custom_call_target="tpu_custom_call" | custom-call | tf_op jit(solution)/shard_map/tail_sum/pallas_call | solution.py:380
  76.5 0.7 collective-permute-start.11
  77.2 1.7 %collective-permute-start.12 = (f32[1,128]{1,0:T(1,128)}, f32[1,128]{1,0:T(1,128)S(1)}, u32[]{:S(2)}, u32[]{:S(2)}) collective-permute-start(f32[1,128]{1,0:T(1,128)} %tail_sum.1), channel_id=1, source_target_pairs={{0,2},{1,3},{2,0},{3,1},{4,6},{5,7},{6,4},{7,5},{8,10},{9,11},{10,... | collective-permute-start | bytes 1544 | tf_op jit(solution)/shard_map/ppermute | solution.py:483
  78.9 0.0 collective-permute-start.13
  78.9 1.2 %tail_grad.1 = bf16[19008,128]{1,0:T(8,128)(2,1)} custom-call(bf16[1584,128]{1,0:T(8,128)(2,1)S(1)} %collective-permute-done.refs_0_, bf16[1584,128]{1,0:T(8,128)(2,1)S(1)} %dynamic-slice_bitcast_fusion.refs_1_, bf16[3,8,528]{2,1,0:T(8,128)(2,1)S(1)} %constant_dynamic-slice_fusion.refs_2_, f32[8,128]{1,0:T(8,128)S(1)} %copy-done, ...), custom_call_target="tpu_custom_call", output_to_operand_aliasing={{}: (5, {})} | custom-call | tf_op jit(solution)/shard_map/tail_grad/pallas_call | solution.py:396
  80.2 0.0 collective-permute-done.11
  80.2 0.0 collective-permute-done.12
  80.2 1.9 %collective-permute-done.13 = f32[1,128]{1,0:T(1,128)S(1)} collective-permute-done((f32[1,128]{1,0:T(1,128)}, f32[1,128]{1,0:T(1,128)S(1)}, u32[]{:S(2)}, u32[]{:S(2)}) %collective-permute-start.13) | collective-permute-done | bytes 544 | tf_op jit(solution)/shard_map/ppermute | solution.py:483
  82.0 0.5 add_bitcast_fusion
  (18 shorter events, 0.2 us)
Async XLA Ops:
  0.6 11.8 %collective-permute-start.4 = (s32[1,128]{1,0:T(1,128)}, s32[1,128]{1,0:T(1,128)S(1)}, u32[]{:S(2)}, u32[]{:S(2)}) collective-permute-start(s32[1,128]{1,0:T(1,128)} %bitcast.22), channel_id=1, source_target_pairs={{0,4},{4,0},{8,12},{12,8},{16,20},{20,16},{24,28},{28,24},{1,5},{5... | collective-permute-start | bytes 1544 | tf_op jit(solution)/shard_map/ppermute | solution.py:510
  3.7 8.7 %copy-start.1 = (s32[128]{0:T(128)S(1)}, s32[128]{0:T(128)}, u32[]{:S(2)}) copy-start(s32[128]{0:T(128)} %param.10) | copy-start | bytes 1540
  3.8 53.6 %collective-permute-start.1 = (bf16[4752,128]{1,0:T(8,128)(2,1)}, bf16[4752,128]{1,0:T(8,128)(2,1)S(1)}, u32[]{:S(2)}, u32[]{:S(2)}) collective-permute-start(bf16[4752,128]{1,0:T(8,128)(2,1)} %get-tuple-element.13), channel_id=1, source_target_pairs={{0,1},{1,0},{2,3},{3,2},{4,5},{5,4},{6,7},{7,6},{8,9},{9,8},{10,11... | collective-permute-start | bytes 3649544 | tf_op jit(solution)/shard_map/ppermute | solution.py:483
  4.5 52.8 %collective-permute-start.3 = (bf16[3168,128]{1,0:T(8,128)(2,1)}, bf16[3168,128]{1,0:T(8,128)(2,1)S(1)}, u32[]{:S(2)}, u32[]{:S(2)}) collective-permute-start(bf16[3168,128]{1,0:T(8,128)(2,1)} %get-tuple-element.14), channel_id=1, source_target_pairs={{0,3},{1,2},{2,1},{3,0},{4,7},{5,6},{6,5},{7,4},{8,11},{9,10},{10,... | collective-permute-start | bytes 2433032 | tf_op jit(solution)/shard_map/ppermute | solution.py:483
  7.9 47.4 %collective-permute-start.2 = (bf16[1584,128]{1,0:T(8,128)(2,1)}, bf16[1584,128]{1,0:T(8,128)(2,1)S(1)}, u32[]{:S(2)}, u32[]{:S(2)}) collective-permute-start(bf16[1584,128]{1,0:T(8,128)(2,1)} %cut.3), channel_id=1, source_target_pairs={{0,3},{1,2},{2,1},{3,0},{4,7},{5,6},{6,5},{7,4},{8,11},{9,10},{10,... | collective-permute-start | bytes 1216520 | tf_op jit(solution)/shard_map/ppermute | solution.py:483
  8.1 60.8 %collective-permute-start.10 = (bf16[2640,128]{1,0:T(8,128)(2,1)}, bf16[2640,128]{1,0:T(8,128)(2,1)S(1)}, u32[]{:S(2)}, u32[]{:S(2)}) collective-permute-start(bf16[2640,128]{1,0:T(8,128)(2,1)} %get-tuple-element.17), channel_id=1, source_target_pairs={{0,2},{1,3},{2,0},{3,1},{4,6},{5,7},{6,4},{7,5},{8,10},{9,11},{10,... | collective-permute-start | bytes 2027528 | tf_op jit(solution)/shard_map/ppermute | solution.py:483
  12.4 30.0 %collective-permute-start.5 = (f32[1,128]{1,0:T(1,128)S(1)}, f32[1,128]{1,0:T(1,128)S(1)}, u32[]{:S(2)}, u32[]{:S(2)}) collective-permute-start(f32[1,128]{1,0:T(1,128)S(1)} %fusion.2), channel_id=1, source_target_pairs={{0,0},{1,9},{2,18},{3,27},{4,4},{5,13},{6,22},{7,31},{8,8},{9,1},{... | collective-permute-start | bytes 1544 | tf_op jit(solution)/shard_map/ppermute | solution.py:522
  15.6 33.6 %copy-start.9 = (s32[48]{0:T(128)S(1)}, s32[48]{0:T(128)}, u32[]{:S(2)}) copy-start(s32[48]{0:T(128)} %constant.57.clone) | copy-start | bytes 580
  15.6 33.6 %copy-start.10 = (s32[48]{0:T(128)S(1)}, s32[48]{0:T(128)}, u32[]{:S(2)}) copy-start(s32[48]{0:T(128)} %constant.58.clone) | copy-start | bytes 580
  15.7 33.6 %copy-start.11 = (s32[48]{0:T(128)S(1)}, s32[48]{0:T(128)}, u32[]{:S(2)}) copy-start(s32[48]{0:T(128)} %constant.59.clone) | copy-start | bytes 580
  15.7 33.6 %copy-start.12 = (s32[48]{0:T(128)S(1)}, s32[48]{0:T(128)}, u32[]{:S(2)}) copy-start(s32[48]{0:T(128)} %constant.60.clone) | copy-start | bytes 580
  43.2 14.1 %copy-start.4 = (f32[8,128]{1,0:T(8,128)}, f32[8,128]{1,0:T(8,128)S(1)}, u32[]{:S(2)}) copy-start(f32[8,128]{1,0:T(8,128)S(1)} %broadcast_select_fusion.refs_8_) | copy-start | bytes 12292
  43.2 1.2 %collective-permute-start.6 = (f32[8,128]{1,0:T(8,128)S(1)}, f32[8,128]{1,0:T(8,128)S(1)}, u32[]{:S(2)}, u32[]{:S(2)}) collective-permute-start(f32[8,128]{1,0:T(8,128)S(1)} %broadcast_select_fusion.refs_8_), channel_id=1, source_target_pairs={{0,1},{1,0},{2,3},{3,2},{4,5},{5,4},{6,7},{7,6},{8,9},{9,8},{10,11... | collective-permute-start | bytes 12296 | tf_op jit(solution)/shard_map/ppermute | solution.py:483
  44.4 13.0 %copy-start.5 = (f32[8,128]{1,0:T(8,128)}, f32[8,128]{1,0:T(8,128)S(1)}, u32[]{:S(2)}) copy-start(f32[8,128]{1,0:T(8,128)S(1)} %collective-permute-done.6.refs_9_) | copy-start | bytes 12292
  44.4 5.9 %collective-permute-start.7 = (f32[8,128]{1,0:T(8,128)S(1)}, f32[8,128]{1,0:T(8,128)S(1)}, u32[]{:S(2)}, u32[]{:S(2)}) collective-permute-start(f32[8,128]{1,0:T(8,128)S(1)} %broadcast_select_fusion.refs_8_), channel_id=1, source_target_pairs={{0,2},{1,3},{2,0},{3,1},{4,6},{5,7},{6,4},{7,5},{8,10},{9,11},{10,... | collective-permute-start | bytes 12296 | tf_op jit(solution)/shard_map/ppermute | solution.py:483
  50.2 0.6 copy-start.6
  50.8 4.2 %collective-permute-start.8 = (f32[8,128]{1,0:T(8,128)S(1)}, f32[8,128]{1,0:T(8,128)S(1)}, u32[]{:S(2)}, u32[]{:S(2)}) collective-permute-start(f32[8,128]{1,0:T(8,128)S(1)} %broadcast_select_fusion.refs_8_), channel_id=1, source_target_pairs={{0,3},{1,2},{2,1},{3,0},{4,7},{5,6},{6,5},{7,4},{8,11},{9,10},{10,... | collective-permute-start | bytes 12296 | tf_op jit(solution)/shard_map/ppermute | solution.py:483
  55.1 2.2 %copy-start.7 = (f32[8,128]{1,0:T(8,128)}, f32[8,128]{1,0:T(8,128)S(1)}, u32[]{:S(2)}) copy-start(f32[8,128]{1,0:T(8,128)S(1)} %collective-permute-done.8.refs_11_) | copy-start | bytes 12292
  55.1 13.8 %collective-permute-start.9 = (bf16[528,128]{1,0:T(8,128)(2,1)}, bf16[528,128]{1,0:T(8,128)(2,1)}, u32[]{:S(2)}, u32[]{:S(2)}) collective-permute-start(bf16[528,128]{1,0:T(8,128)(2,1)} %get-tuple-element.16), channel_id=1, source_target_pairs={{0,2},{1,3},{2,0},{3,1},{4,6},{5,7},{6,4},{7,5},{8,10},{9,11},{10,... | collective-permute-start | bytes 405512 | tf_op jit(solution)/shard_map/ppermute | solution.py:483
  55.3 0.7 copy-start.3
  56.1 19.4 %collective-permute-start = (bf16[1584,128]{1,0:T(8,128)(2,1)}, bf16[1584,128]{1,0:T(8,128)(2,1)S(1)}, u32[]{:S(2)}, u32[]{:S(2)}) collective-permute-start(bf16[1584,128]{1,0:T(8,128)(2,1)} %get-tuple-element.12), channel_id=1, source_target_pairs={{0,2},{1,3},{2,0},{3,1},{4,6},{5,7},{6,4},{7,5},{8,10},{9,11},{10,... | collective-permute-start | bytes 1216520 | tf_op jit(solution)/shard_map/ppermute | solution.py:483
  68.9 6.6 %copy-start = (f32[8,128]{1,0:T(8,128)S(1)}, f32[8,128]{1,0:T(8,128)}, u32[]{:S(2)}) copy-start(f32[8,128]{1,0:T(8,128)} %get-tuple-element.15.refs_6_.refs_3_) | copy-start | bytes 12292
  68.9 6.6 %copy-start.2 = (s32[128]{0:T(128)S(1)}, s32[128]{0:T(128)}, u32[]{:S(2)}) copy-start(s32[128]{0:T(128)} %param.10) | copy-start | bytes 1540
  76.5 3.7 %collective-permute-start.11 = (f32[1,128]{1,0:T(1,128)}, f32[1,128]{1,0:T(1,128)S(1)}, u32[]{:S(2)}, u32[]{:S(2)}) collective-permute-start(f32[1,128]{1,0:T(1,128)} %tail_sum.1), channel_id=1, source_target_pairs={{0,1},{1,0},{2,3},{3,2},{4,5},{5,4},{6,7},{7,6},{8,9},{9,8},{10,11... | collective-permute-start | bytes 1544 | tf_op jit(solution)/shard_map/ppermute | solution.py:483
  77.2 3.0 %collective-permute-start.12 = (f32[1,128]{1,0:T(1,128)}, f32[1,128]{1,0:T(1,128)S(1)}, u32[]{:S(2)}, u32[]{:S(2)}) collective-permute-start(f32[1,128]{1,0:T(1,128)} %tail_sum.1), channel_id=1, source_target_pairs={{0,2},{1,3},{2,0},{3,1},{4,6},{5,7},{6,4},{7,5},{8,10},{9,11},{10,... | collective-permute-start | bytes 1544 | tf_op jit(solution)/shard_map/ppermute | solution.py:483
  78.9 3.1 %collective-permute-start.13 = (f32[1,128]{1,0:T(1,128)}, f32[1,128]{1,0:T(1,128)S(1)}, u32[]{:S(2)}, u32[]{:S(2)}) collective-permute-start(f32[1,128]{1,0:T(1,128)} %tail_sum.1), channel_id=1, source_target_pairs={{0,3},{1,2},{2,1},{3,0},{4,7},{5,6},{6,5},{7,4},{8,11},{9,10},{10,... | collective-permute-start | bytes 1544 | tf_op jit(solution)/shard_map/ppermute | solution.py:483
  78.9 3.1 %copy-start.8 = (f32[1,128]{1,0:T(1,128)S(1)}, f32[1,128]{1,0:T(1,128)}, u32[]{:S(2)}) copy-start(f32[1,128]{1,0:T(1,128)} %tail_sum.1) | copy-start | bytes 1540

commit v4 on v3

--- a/solution.py
+++ b/solution.py
@@ -12,7 +12,7 @@
 LOW = -3e38
 ROWS = 16
 LINES = 8
-HELD_BYTES = 3 * 2**20
+HELD_BYTES = 2.3 * 2**20
 WAYS = 3
 AHEAD = 1
 STEP = 544
@@ -379,7 +379,7 @@
 
     return pl.pallas_call(
         kernel,
-        out_shape=jax.ShapeDtypeStruct((1, lanes), F32),
+        out_shape=pltpu.VMEM((1, lanes), F32),
         in_specs=[pl.BlockSpec(memory_space=pltpu.VMEM)] * len(operands),
         out_specs=pl.BlockSpec(memory_space=pltpu.VMEM),
         name="tail_sum",
@@ -433,7 +433,9 @@
 
     return pl.pallas_call(
         kernel,
-        out_shape=tuple(jax.ShapeDtypeStruct((size, lanes), BF16) for _, _, size in parts),
+        out_shape=tuple(
+            pltpu.VMEM((size, lanes), BF16) if held else jax.ShapeDtypeStruct((size, lanes), BF16)
+            for _, _, size in parts),
         in_specs=[pl.BlockSpec(memory_space=pl.ANY)],
         out_specs=tuple(pl.BlockSpec(memory_space=space) for _ in parts),
         scratch_shapes=scratch + [pltpu.SemaphoreType.DMA((2 * len(parts),))],

time: 83.4 us -> 82.6 us (level)
  the two profiles are of different devices: /device:TPU:5 before, /device:TPU:0 now
where the time goes in v4:
time: 82.6 us; the launch traced here: 81.4 us
  Pallas kernels  49.1 us (59%)
  starting transfers between devices  14.8 us (18%)
  waiting for transfers between devices  7.49 us (9%)
  local copies, waits for them, and re-layouts  5.63 us (7%)
  other arithmetic  3.45 us (4%)
  between operations  0.89 us (1%)
    pallas_call x1, Pallas kernels, run_stats(): pl.pallas_call(kernel, out_shape=jax.ShapeDtypeStruct((8, lanes), F32), g...  26.3 us
    pallas_call x2, Pallas kernels, run_chunk(): pl.pallas_call(kernel, out_shape=tuple(out_shape), grid_spec=pltpu.Prefet...  17 us
    ppermute x12, starting transfers between devices, swap(): lax.ppermute(value, 'voc', [(i, partner(i, shift)) for i in range(voc_cou...  11.1 us
    ppermute x12, waiting for transfers between devices, swap(): lax.ppermute(value, 'voc', [(i, partner(i, shift)) for i in range(voc_cou...  7.48 us
    pallas_call x2, Pallas kernels, cut(): pl.pallas_call(kernel, out_shape=tuple((pltpu.VMEM((size, lanes), BF16) i...  4.02 us
    ppermute x1, starting transfers between devices, body(): kept = kept + (lax.ppermute(target, 'tok', pairs) >= 0).astype(F32)  3.06 us
  transfers between devices with their start and end apart: 14, of which 5 were waited for; matrix products, arithmetic and copies ran while one was open for 9% of the time, Pallas kernels for 60%

profile of v4, /device:TPU:0, one launch (start us, length us, event | category | flops | bytes accessed | tf_op | source)
XLA Modules:
  0.0 81.4 jit_solution(5807113151265903260)
XLA Ops:
  0.6 3.1 %collective-permute-start.4 = (s32[1,128]{1,0:T(1,128)}, s32[1,128]{1,0:T(1,128)S(1)}, u32[]{:S(2)}, u32[]{:S(2)}) collective-permute-start(s32[1,128]{1,0:T(1,128)} %bitcast.22), channel_id=1, source_target_pairs={{0,4},{4,0},{8,12},{12,8},{16,20},{20,16},{24,28},{28,24},{1,5},{5... | collective-permute-start | bytes 1544 | tf_op jit(solution)/shard_map/ppermute | solution.py:512
  3.7 3.0 %cut.2 = (bf16[3168,128]{1,0:T(8,128)(2,1)}, bf16[528,128]{1,0:T(8,128)(2,1)}, bf16[2640,128]{1,0:T(8,128)(2,1)}, bf16[1584,128]{1,0:T(8,128)(2,1)}, bf16[4752,128]{1,0:T(8,128)(2,1)}) custom-call(bf16[4,4752,128]{2,1,0:T(8,128)(2,1)} %bitcast.27), custom_call_target="tpu_custom_call" | custom-call | tf_op jit(solution)/shard_map/cut/pallas_call | solution.py:434
  6.7 0.0 copy-start.1
  6.7 0.1 collective-permute-start.1
  6.8 1.6 %collective-permute-start.3 = (bf16[3168,128]{1,0:T(8,128)(2,1)}, bf16[3168,128]{1,0:T(8,128)(2,1)S(1)}, u32[]{:S(2)}, u32[]{:S(2)}) collective-permute-start(bf16[3168,128]{1,0:T(8,128)(2,1)} %get-tuple-element.14), channel_id=1, source_target_pairs={{0,3},{1,2},{2,1},{3,0},{4,7},{5,6},{6,5},{7,4},{8,11},{9,10},{10,... | collective-permute-start | bytes 2433032 | tf_op jit(solution)/shard_map/ppermute | solution.py:485
  8.4 1.0 %cut.3 = bf16[1584,128]{1,0:T(8,128)(2,1)S(1)} custom-call(bf16[4,4752,128]{2,1,0:T(8,128)(2,1)} %bitcast.28), custom_call_target="tpu_custom_call" | custom-call | tf_op jit(solution)/shard_map/cut/pallas_call | solution.py:434
  9.4 0.3 collective-permute-start.2
  9.7 1.5 %collective-permute-start.10 = (bf16[2640,128]{1,0:T(8,128)(2,1)}, bf16[2640,128]{1,0:T(8,128)(2,1)S(1)}, u32[]{:S(2)}, u32[]{:S(2)}) collective-permute-start(bf16[2640,128]{1,0:T(8,128)(2,1)} %get-tuple-element.17), channel_id=1, source_target_pairs={{0,2},{1,3},{2,0},{3,1},{4,6},{5,7},{6,4},{7,5},{8,10},{9,11},{10,... | collective-permute-start | bytes 2027528 | tf_op jit(solution)/shard_map/ppermute | solution.py:485
  11.2 1.2 %reshape.46 = s32[4,4,4752]{2,1,0:T(4,128)S(1)} reshape(s32[76032]{0:T(1024)} %param.11) | data formatting | bytes 608256 | tf_op jit(solution)/shard_map/reshape | solution.py:526
  12.4 0.1 constant_dynamic-slice_fusion.1
  12.7 0.1 broadcast_in_dim.76
  12.8 0.1 broadcast_in_dim.79
  12.9 0.9 %select_select_fusion.refs_2_.refs_6_.refs_4_ = bf16[36,8,528]{2,1,0:T(8,128)(2,1)} fusion(pred[8]{0:T(512)(128)(4,1)S(1)} %get-tuple-element.24, pred[8]{0:T(512)(128)(4,1)S(1)} %get-tuple-element.25, bf16[8]{0:T(256)(128)(2,1)S(1)} %fusion, bf16[36,528]{1,0:T(8,128)(2,1)S(1)} %broadcast_in_dim.79, bf16[36,528]{1,0:T(8,128)(2,1)S(1)} %broadcast_in_dim.76), kind=kLoop, calls=%fused_computation.1 | loop fusion | flops 304128 | bytes 380192 | tf_op jit(solution)/shard_map/jit(_where)/select_n | solution.py:538
  13.8 0.0 collective-permute-done.4
  13.8 0.0 copy-done.1
  13.8 0.7 collective-permute-start.5
  14.5 0.0 copy-start.8
  14.5 0.0 copy-start.9
  14.5 0.0 copy-start.10
  14.6 0.0 copy-start.11
  14.6 26.3 %stats.1 = f32[8,128]{1,0:T(8,128)} custom-call(bf16[19008,128]{1,0:T(8,128)(2,1)} %bitcast.29, bf16[19008,128]{1,0:T(8,128)(2,1)} %bitcast.31, bf16[36,8,528]{2,1,0:T(8,128)(2,1)} %select_select_fusion.refs_2_.refs_6_.refs_4_), custom_call_target="tpu_custom_call" | custom-call | tf_op jit(solution)/shard_map/stats/pallas_call | solution.py:156
  40.9 0.0 collective-permute-done.5
  40.9 0.8 broadcast_select_fusion.refs_8_
  41.7 0.0 collective-permute-start.6
  41.7 1.0 %dynamic-slice_bitcast_fusion.refs_1_ = bf16[1584,128]{1,0:T(8,128)(2,1)S(1)} fusion(bf16[128,19008]{0,1:T(8,128)(2,1)} %param.9, s32[]{:T(128)S(6)} %select_n.42), kind=kLoop, calls=%fused_computation | loop fusion | bytes 811012 | tf_op jit(solution)/shard_map/dynamic_slice | solution.py:600
  42.7 0.1 collective-permute-done.6.refs_9_
  42.8 3.1 %collective-permute-start.7 = (f32[8,128]{1,0:T(8,128)S(1)}, f32[8,128]{1,0:T(8,128)S(1)}, u32[]{:S(2)}, u32[]{:S(2)}) collective-permute-start(f32[8,128]{1,0:T(8,128)S(1)} %broadcast_select_fusion.refs_8_), channel_id=1, source_target_pairs={{0,2},{1,3},{2,0},{3,1},{4,6},{5,7},{6,4},{7,5},{8,10},{9,11},{10,... | collective-permute-start | bytes 12296 | tf_op jit(solution)/shard_map/ppermute | solution.py:485
  46.0 0.0 copy-done.8
  46.0 0.0 copy-done.9
  46.0 0.0 copy-done.10
  46.0 0.0 copy-done.11
  46.0 0.5 add_add_fusion.refs_0_
  46.5 4.2 %collective-permute-done.7.refs_10_ = f32[8,128]{1,0:T(8,128)S(1)} collective-permute-done((f32[8,128]{1,0:T(8,128)S(1)}, f32[8,128]{1,0:T(8,128)S(1)}, u32[]{:S(2)}, u32[]{:S(2)}) %collective-permute-start.7) | collective-permute-done | bytes 4128 | tf_op jit(solution)/shard_map/ppermute | solution.py:485
  50.7 0.6 copy-done.6
  51.3 0.6 collective-permute-start.8
  51.9 0.8 constant_dynamic-slice_fusion.refs_2_
  52.6 1.7 %collective-permute-done.8.refs_11_ = f32[8,128]{1,0:T(8,128)S(1)} collective-permute-done((f32[8,128]{1,0:T(8,128)S(1)}, f32[8,128]{1,0:T(8,128)S(1)}, u32[]{:S(2)}, u32[]{:S(2)}) %collective-permute-start.8) | collective-permute-done | bytes 4128 | tf_op jit(solution)/shard_map/ppermute | solution.py:485
  54.3 1.5 %collective-permute-start.9 = (bf16[528,128]{1,0:T(8,128)(2,1)}, bf16[528,128]{1,0:T(8,128)(2,1)}, u32[]{:S(2)}, u32[]{:S(2)}) collective-permute-start(bf16[528,128]{1,0:T(8,128)(2,1)} %get-tuple-element.16), channel_id=1, source_target_pairs={{0,2},{1,3},{2,0},{3,1},{4,6},{5,7},{6,4},{7,5},{8,10},{9,11},{10,... | collective-permute-start | bytes 405512 | tf_op jit(solution)/shard_map/ppermute | solution.py:485
  55.8 0.0 collective-permute-done.2.refs_3_
  55.8 0.5 collective-permute-start
  56.4 0.0 collective-permute-done.3.refs_4_
  56.4 0.0 copy-done.7
  56.4 0.0 collective-permute-done.1.refs_2_
  56.4 0.0 copy-done.4
  56.4 0.0 copy-done.5
  56.4 0.9 %copy-done.3 = bf16[3168,128]{1,0:T(8,128)(2,1)} copy-done((bf16[3168,128]{1,0:T(8,128)(2,1)}, bf16[3168,128]{1,0:T(8,128)(2,1)S(1)}, u32[]{:S(2)}) %copy-start.3) | copy-done | bytes 811032
  57.3 11.1 %chunk.2 = (bf16[19008,128]{1,0:T(8,128)(2,1)}, f32[16,128]{1,0:T(8,128)}, f32[8,128]{1,0:T(8,128)}) custom-call(s32[48]{0:T(128)} %add_add_fusion.refs_0_, bf16[19008,128]{1,0:T(8,128)(2,1)} %bitcast.30, bf16[4752,128]{1,0:T(8,128)(2,1)S(1)} %collective-permute-done.1.refs_2_, bf16[1584,128]{1,0:T(8,128)(2,1)} %collective-permute-done.2.refs_3_, ...), custom_call_target="tpu_custom_call" | custom-call | tf_op jit(solution)/shard_map/chunk/pallas_call | solution.py:304
  68.4 0.7 slice_bitcast_fusion
  69.1 0.0 collective-permute-done.9.refs_1_
  69.1 0.0 collective-permute-done.10.refs_2_
  69.1 0.0 copy-start.2
  69.1 5.9 %chunk.3 = (bf16[19008,128]{1,0:T(8,128)(2,1)}, f32[16,128]{1,0:T(8,128)}) custom-call(s32[48]{0:T(128)} %add_add_fusion.refs_0_, bf16[528,128]{1,0:T(8,128)(2,1)} %collective-permute-done.9.refs_1_, bf16[2640,128]{1,0:T(8,128)(2,1)S(1)} %collective-permute-done.10.refs_2_, bf16[19008,128]{1,0:T(8,128)(2,1)} %bitcast.33, ...), custom_call_target="tpu_custom_call", output_to_operand_aliasing={{0}: (8, {})} | custom-call | tf_op jit(solution)/shard_map/chunk/pallas_call | solution.py:304
  75.0 0.7 subtract_reduce_fusion
  75.7 0.0 copy-done
  75.7 0.0 collective-permute-done.refs_0_
  75.7 0.5 tail_sum.1
  76.2 0.1 collective-permute-start.11
  76.3 1.6 %collective-permute-start.12 = (f32[1,128]{1,0:T(1,128)S(1)}, f32[1,128]{1,0:T(1,128)S(1)}, u32[]{:S(2)}, u32[]{:S(2)}) collective-permute-start(f32[1,128]{1,0:T(1,128)S(1)} %tail_sum.1), channel_id=1, source_target_pairs={{0,2},{1,3},{2,0},{3,1},{4,6},{5,7},{6,4},{7,5},{8,10},{9,11},{10,... | collective-permute-start | bytes 1544 | tf_op jit(solution)/shard_map/ppermute | solution.py:485
  77.9 0.3 collective-permute-start.13
  78.2 1.2 %tail_grad.1 = bf16[19008,128]{1,0:T(8,128)(2,1)} custom-call(bf16[1584,128]{1,0:T(8,128)(2,1)S(1)} %collective-permute-done.refs_0_, bf16[1584,128]{1,0:T(8,128)(2,1)S(1)} %dynamic-slice_bitcast_fusion.refs_1_, bf16[3,8,528]{2,1,0:T(8,128)(2,1)S(1)} %constant_dynamic-slice_fusion.refs_2_, f32[8,128]{1,0:T(8,128)S(1)} %copy-done, ...), custom_call_target="tpu_custom_call", output_to_operand_aliasing={{}: (5, {})} | custom-call | tf_op jit(solution)/shard_map/tail_grad/pallas_call | solution.py:396
  79.4 0.0 collective-permute-done.11
  79.4 0.5 collective-permute-done.12
  79.9 0.9 %collective-permute-done.13 = f32[1,128]{1,0:T(1,128)S(1)} collective-permute-done((f32[1,128]{1,0:T(1,128)S(1)}, f32[1,128]{1,0:T(1,128)S(1)}, u32[]{:S(2)}, u32[]{:S(2)}) %collective-permute-start.13) | collective-permute-done | bytes 544 | tf_op jit(solution)/shard_map/ppermute | solution.py:485
  80.9 0.5 add_bitcast_fusion
  (16 shorter events, 0.2 us)
Async XLA Ops:
  0.6 13.2 %collective-permute-start.4 = (s32[1,128]{1,0:T(1,128)}, s32[1,128]{1,0:T(1,128)S(1)}, u32[]{:S(2)}, u32[]{:S(2)}) collective-permute-start(s32[1,128]{1,0:T(1,128)} %bitcast.22), channel_id=1, source_target_pairs={{0,4},{4,0},{8,12},{12,8},{16,20},{20,16},{24,28},{28,24},{1,5},{5... | collective-permute-start | bytes 1544 | tf_op jit(solution)/shard_map/ppermute | solution.py:512
  6.7 7.1 %copy-start.1 = (s32[128]{0:T(128)S(1)}, s32[128]{0:T(128)}, u32[]{:S(2)}) copy-start(s32[128]{0:T(128)} %param.10) | copy-start | bytes 1540
  6.7 49.7 %collective-permute-start.1 = (bf16[4752,128]{1,0:T(8,128)(2,1)}, bf16[4752,128]{1,0:T(8,128)(2,1)S(1)}, u32[]{:S(2)}, u32[]{:S(2)}) collective-permute-start(bf16[4752,128]{1,0:T(8,128)(2,1)} %get-tuple-element.13), channel_id=1, source_target_pairs={{0,1},{1,0},{2,3},{3,2},{4,5},{5,4},{6,7},{7,6},{8,9},{9,8},{10,11... | collective-permute-start | bytes 3649544 | tf_op jit(solution)/shard_map/ppermute | solution.py:485
  6.8 49.6 %collective-permute-start.3 = (bf16[3168,128]{1,0:T(8,128)(2,1)}, bf16[3168,128]{1,0:T(8,128)(2,1)S(1)}, u32[]{:S(2)}, u32[]{:S(2)}) collective-permute-start(bf16[3168,128]{1,0:T(8,128)(2,1)} %get-tuple-element.14), channel_id=1, source_target_pairs={{0,3},{1,2},{2,1},{3,0},{4,7},{5,6},{6,5},{7,4},{8,11},{9,10},{10,... | collective-permute-start | bytes 2433032 | tf_op jit(solution)/shard_map/ppermute | solution.py:485
  9.4 46.4 %collective-permute-start.2 = (bf16[1584,128]{1,0:T(8,128)(2,1)S(1)}, bf16[1584,128]{1,0:T(8,128)(2,1)}, u32[]{:S(2)}, u32[]{:S(2)}) collective-permute-start(bf16[1584,128]{1,0:T(8,128)(2,1)S(1)} %cut.3), channel_id=1, source_target_pairs={{0,3},{1,2},{2,1},{3,0},{4,7},{5,6},{6,5},{7,4},{8,11},{9,10},{10,... | collective-permute-start | bytes 1216520 | tf_op jit(solution)/shard_map/ppermute | solution.py:485
  9.7 59.4 %collective-permute-start.10 = (bf16[2640,128]{1,0:T(8,128)(2,1)}, bf16[2640,128]{1,0:T(8,128)(2,1)S(1)}, u32[]{:S(2)}, u32[]{:S(2)}) collective-permute-start(bf16[2640,128]{1,0:T(8,128)(2,1)} %get-tuple-element.17), channel_id=1, source_target_pairs={{0,2},{1,3},{2,0},{3,1},{4,6},{5,7},{6,4},{7,5},{8,10},{9,11},{10,... | collective-permute-start | bytes 2027528 | tf_op jit(solution)/shard_map/ppermute | solution.py:485
  13.8 27.1 %collective-permute-start.5 = (f32[1,128]{1,0:T(1,128)S(1)}, f32[1,128]{1,0:T(1,128)S(1)}, u32[]{:S(2)}, u32[]{:S(2)}) collective-permute-start(f32[1,128]{1,0:T(1,128)S(1)} %fusion.2), channel_id=1, source_target_pairs={{0,0},{1,9},{2,18},{3,27},{4,4},{5,13},{6,22},{7,31},{8,8},{9,1},{... | collective-permute-start | bytes 1544 | tf_op jit(solution)/shard_map/ppermute | solution.py:524
  14.5 31.4 %copy-start.8 = (s32[48]{0:T(128)S(1)}, s32[48]{0:T(128)}, u32[]{:S(2)}) copy-start(s32[48]{0:T(128)} %constant.57.clone) | copy-start | bytes 580
  14.5 31.4 %copy-start.9 = (s32[48]{0:T(128)S(1)}, s32[48]{0:T(128)}, u32[]{:S(2)}) copy-start(s32[48]{0:T(128)} %constant.58.clone) | copy-start | bytes 580
  14.5 31.4 %copy-start.10 = (s32[48]{0:T(128)S(1)}, s32[48]{0:T(128)}, u32[]{:S(2)}) copy-start(s32[48]{0:T(128)} %constant.59.clone) | copy-start | bytes 580
  14.6 31.4 %copy-start.11 = (s32[48]{0:T(128)S(1)}, s32[48]{0:T(128)}, u32[]{:S(2)}) copy-start(s32[48]{0:T(128)} %constant.60.clone) | copy-start | bytes 580
  41.7 14.7 %copy-start.4 = (f32[8,128]{1,0:T(8,128)}, f32[8,128]{1,0:T(8,128)S(1)}, u32[]{:S(2)}) copy-start(f32[8,128]{1,0:T(8,128)S(1)} %broadcast_select_fusion.refs_8_) | copy-start | bytes 12292
  41.7 1.2 %collective-permute-start.6 = (f32[8,128]{1,0:T(8,128)S(1)}, f32[8,128]{1,0:T(8,128)S(1)}, u32[]{:S(2)}, u32[]{:S(2)}) collective-permute-start(f32[8,128]{1,0:T(8,128)S(1)} %broadcast_select_fusion.refs_8_), channel_id=1, source_target_pairs={{0,1},{1,0},{2,3},{3,2},{4,5},{5,4},{6,7},{7,6},{8,9},{9,8},{10,11... | collective-permute-start | bytes 12296 | tf_op jit(solution)/shard_map/ppermute | solution.py:485
  42.8 13.6 %copy-start.5 = (f32[8,128]{1,0:T(8,128)}, f32[8,128]{1,0:T(8,128)S(1)}, u32[]{:S(2)}) copy-start(f32[8,128]{1,0:T(8,128)S(1)} %collective-permute-done.6.refs_9_) | copy-start | bytes 12292
  42.8 7.9 %collective-permute-start.7 = (f32[8,128]{1,0:T(8,128)S(1)}, f32[8,128]{1,0:T(8,128)S(1)}, u32[]{:S(2)}, u32[]{:S(2)}) collective-permute-start(f32[8,128]{1,0:T(8,128)S(1)} %broadcast_select_fusion.refs_8_), channel_id=1, source_target_pairs={{0,2},{1,3},{2,0},{3,1},{4,6},{5,7},{6,4},{7,5},{8,10},{9,11},{10,... | collective-permute-start | bytes 12296 | tf_op jit(solution)/shard_map/ppermute | solution.py:485
  50.7 0.6 copy-start.6
  51.3 3.0 %collective-permute-start.8 = (f32[8,128]{1,0:T(8,128)S(1)}, f32[8,128]{1,0:T(8,128)S(1)}, u32[]{:S(2)}, u32[]{:S(2)}) collective-permute-start(f32[8,128]{1,0:T(8,128)S(1)} %broadcast_select_fusion.refs_8_), channel_id=1, source_target_pairs={{0,3},{1,2},{2,1},{3,0},{4,7},{5,6},{6,5},{7,4},{8,11},{9,10},{10,... | collective-permute-start | bytes 12296 | tf_op jit(solution)/shard_map/ppermute | solution.py:485
  54.3 2.0 %copy-start.7 = (f32[8,128]{1,0:T(8,128)}, f32[8,128]{1,0:T(8,128)S(1)}, u32[]{:S(2)}) copy-start(f32[8,128]{1,0:T(8,128)S(1)} %collective-permute-done.8.refs_11_) | copy-start | bytes 12292
  54.3 14.8 %collective-permute-start.9 = (bf16[528,128]{1,0:T(8,128)(2,1)}, bf16[528,128]{1,0:T(8,128)(2,1)}, u32[]{:S(2)}, u32[]{:S(2)}) collective-permute-start(bf16[528,128]{1,0:T(8,128)(2,1)} %get-tuple-element.16), channel_id=1, source_target_pairs={{0,2},{1,3},{2,0},{3,1},{4,6},{5,7},{6,4},{7,5},{8,10},{9,11},{10,... | collective-permute-start | bytes 405512 | tf_op jit(solution)/shard_map/ppermute | solution.py:485
  55.8 19.9 %collective-permute-start = (bf16[1584,128]{1,0:T(8,128)(2,1)}, bf16[1584,128]{1,0:T(8,128)(2,1)S(1)}, u32[]{:S(2)}, u32[]{:S(2)}) collective-permute-start(bf16[1584,128]{1,0:T(8,128)(2,1)} %get-tuple-element.12), channel_id=1, source_target_pairs={{0,2},{1,3},{2,0},{3,1},{4,6},{5,7},{6,4},{7,5},{8,10},{9,11},{10,... | collective-permute-start | bytes 1216520 | tf_op jit(solution)/shard_map/ppermute | solution.py:485
  56.4 0.9 %copy-start.3 = (bf16[3168,128]{1,0:T(8,128)(2,1)}, bf16[3168,128]{1,0:T(8,128)(2,1)S(1)}, u32[]{:S(2)}) copy-start(bf16[3168,128]{1,0:T(8,128)(2,1)S(1)} %collective-permute-done.3.refs_4_) | copy-start | bytes 2433028
  69.1 6.6 %copy-start = (f32[8,128]{1,0:T(8,128)S(1)}, f32[8,128]{1,0:T(8,128)}, u32[]{:S(2)}) copy-start(f32[8,128]{1,0:T(8,128)} %get-tuple-element.15.refs_6_.refs_3_) | copy-start | bytes 12292
  69.1 6.6 %copy-start.2 = (s32[128]{0:T(128)S(1)}, s32[128]{0:T(128)}, u32[]{:S(2)}) copy-start(s32[128]{0:T(128)} %param.10) | copy-start | bytes 1540
  76.2 3.2 %collective-permute-start.11 = (f32[1,128]{1,0:T(1,128)S(1)}, f32[1,128]{1,0:T(1,128)S(1)}, u32[]{:S(2)}, u32[]{:S(2)}) collective-permute-start(f32[1,128]{1,0:T(1,128)S(1)} %tail_sum.1), channel_id=1, source_target_pairs={{0,1},{1,0},{2,3},{3,2},{4,5},{5,4},{6,7},{7,6},{8,9},{9,8},{10,11... | collective-permute-start | bytes 1544 | tf_op jit(solution)/shard_map/ppermute | solution.py:485
  76.3 3.6 %collective-permute-start.12 = (f32[1,128]{1,0:T(1,128)S(1)}, f32[1,128]{1,0:T(1,128)S(1)}, u32[]{:S(2)}, u32[]{:S(2)}) collective-permute-start(f32[1,128]{1,0:T(1,128)S(1)} %tail_sum.1), channel_id=1, source_target_pairs={{0,2},{1,3},{2,0},{3,1},{4,6},{5,7},{6,4},{7,5},{8,10},{9,11},{10,... | collective-permute-start | bytes 1544 | tf_op jit(solution)/shard_map/ppermute | solution.py:485
  77.9 3.0 %collective-permute-start.13 = (f32[1,128]{1,0:T(1,128)S(1)}, f32[1,128]{1,0:T(1,128)S(1)}, u32[]{:S(2)}, u32[]{:S(2)}) collective-permute-start(f32[1,128]{1,0:T(1,128)S(1)} %tail_sum.1), channel_id=1, source_target_pairs={{0,3},{1,2},{2,1},{3,0},{4,7},{5,6},{6,5},{7,4},{8,11},{9,10},{10,... | collective-permute-start | bytes 1544 | tf_op jit(solution)/shard_map/ppermute | solution.py:485

commit v5 on v4

--- a/solution.py
+++ b/solution.py
@@ -165,15 +165,13 @@
     )(teacher, student, mask)
 
 
-def join_stats(refs, target, tokens):
+def join_stats(refs, kept, target, tokens):
     parts = [ref[...] for ref in refs]
     t_top = parts[0][0:1]
     s_top = parts[0][2:3]
-    kept = parts[0][4:5]
     for part in parts[1:]:
         t_top = jnp.maximum(t_top, part[0:1])
         s_top = jnp.maximum(s_top, part[2:3])
-        kept = kept + part[4:5]
     t_sum = jnp.zeros_like(t_top)
     s_sum = jnp.zeros_like(t_top)
     for part in parts:
@@ -196,11 +194,11 @@
     rows, lanes = s_ref.shape
     weights_ref, refs = refs[-1], refs[:-1]
     if shares:
-        share_refs, (g_ref, d_out, vec_ref) = refs[:shares], refs[shares:]
+        share_refs, (kept_ref, g_ref, d_out, vec_ref) = refs[:shares], refs[shares:]
 
         @pl.when(g == 0)
         def _():
-            vec_ref[...] = join_stats(share_refs, tgt_ref[...], tokens)
+            vec_ref[...] = join_stats(share_refs, kept_ref[...], tgt_ref[...], tokens)
             d_out[...] = jnp.zeros(d_out.shape, F32)
     else:
         vec_ref, d_in, _, g_ref, d_out = refs
@@ -254,7 +252,7 @@
         done += length
 
 
-def run_chunk(spots, slot, rows, pieces, student, bias, target, cols, stats=(), tokens=0, state=None):
+def run_chunk(spots, slot, rows, pieces, student, bias, target, cols, stats=(), kept=None, tokens=0, state=None):
     _, lanes = student.shape
     step = bias.shape[-1]
     lines = (rows // step,) + bias.shape[1:]
@@ -285,8 +283,8 @@
     out_specs = [moved]
     aliases = {}
     if stats:
-        in_specs += [fixed(8)] * len(stats)
-        operands += list(stats)
+        in_specs += [fixed(8)] * len(stats) + [fixed(1)]
+        operands += list(stats) + [kept]
         out_shape += [jax.ShapeDtypeStruct((16, lanes), F32), jax.ShapeDtypeStruct((8, lanes), F32)]
         out_specs += [fixed(16), fixed(8)]
     else:
@@ -504,24 +502,15 @@
 
     target = target_ids.reshape(1, tok_rows)
     kept = (target >= 0).astype(F32)
-    merged = 1
-    step = 0
-    while tok_count // merged > voc_count:
-        pairs = [(i, i ^ merged) for i in range(tok_count)]
-        if step == 0:
-            kept = kept + (lax.ppermute(target, "tok", pairs) >= 0).astype(F32)
-        else:
-            kept = kept + lax.ppermute(kept, "tok", pairs)
-        merged *= 2
-        step += 1
-    left = tok_count // merged
-    even = left & (left - 1) == 0
-    pairs = [
-        (t * voc_count + v,
-         ((t // merged ^ v if even else (t // merged + v) % left) * merged + t % merged) * voc_count + v)
-        for t in range(tok_count) for v in range(left)
-    ]
-    kept = lax.ppermute(kept, ("tok", "voc"), pairs)
+    if tok_count & (tok_count - 1):
+        kept = lax.psum(kept, "tok")
+    else:
+        for step in range(tok_count.bit_length() - 1):
+            pairs = [(i, i ^ 1 << step) for i in range(tok_count)]
+            if step == 0:
+                kept = kept + (lax.ppermute(target, "tok", pairs) >= 0).astype(F32)
+            else:
+                kept = kept + lax.ppermute(kept, "tok", pairs)
 
     flags = vocab_used.reshape(voc_count, voc_count, block_cols)
     flags = jnp.stack([
@@ -538,7 +527,6 @@
     bias = jnp.where(kind == 0, line[0], jnp.where(kind == 1, line[1], ones))
 
     stats = run_stats(flat, student, bias, 1600)
-    stats = jnp.where(lax.broadcasted_iota(jnp.int32, stats.shape, 0) == 4, kept, stats)
     gathered = [stats]
     for shift in range(1, voc_count):
         gathered.append(swap(stats, shift))
@@ -582,7 +570,8 @@
 
     cols = block_cols if split else None
     grad, div, vec = run_chunk(
-        spots, 0, big, first, student, bias, target, cols, stats=gathered, tokens=tok_rows * tok_count)
+        spots, 0, big, first, student, bias, target, cols, stats=gathered, kept=kept,
+        tokens=tok_rows * tok_count)
     for slot, rows, piece in groups[:-1]:
         grad, div = run_chunk(spots, slot, rows, piece, student, bias, target, cols, state=(vec, div, grad))
     if groups:

time: 82.6 us -> 96.6 us (1.17)
  waiting for transfers between devices: 7.49 us -> 21.1 us
    ppermute x12, waiting for transfers between devices: 7.48 us -> 19 us  [swap(): lax.ppermute(value, 'voc', [(i, partner(i, shift)) for i in range(voc_cou...]
    ppermute x1 -> x2, starting transfers between devices: 0.66 us -> 4.07 us  [body(): kept = kept + lax.ppermute(kept, 'tok', pairs)]
    ppermute x12, starting transfers between devices: 11.1 us -> 7.91 us  [swap(): lax.ppermute(value, 'voc', [(i, partner(i, shift)) for i in range(voc_cou...]
    ppermute x1 -> x2, waiting for transfers between devices: 0.01 us -> 2.1 us  [body(): kept = kept + lax.ppermute(kept, 'tok', pairs)]
    add x0 -> x2, other arithmetic: none -> 1.19 us  [body(): kept = kept + lax.ppermute(kept, 'tok', pairs)]
    unnamed x25 -> x31, local copies, waits for them, and re-layouts: 1.56 us -> 2.14 us
  transfers between devices with their start and end apart: 14 -> 15, of which waited for: 5 -> 4; matrix products, arithmetic and copies ran while one was open for 9% -> 7% of each run, Pallas kernels for 60% -> 51%
where the time goes in v5:
time: 96.6 us; the launch traced here: 95.3 us
  Pallas kernels  49.1 us (51%)
  waiting for transfers between devices  21.1 us (22%)
  starting transfers between devices  15 us (16%)
  local copies, waits for them, and re-layouts  5.23 us (5%)
  other arithmetic  3.87 us (4%)
  between operations  0.98 us (1%)
    pallas_call x1, Pallas kernels, run_stats(): pl.pallas_call(kernel, out_shape=jax.ShapeDtypeStruct((8, lanes), F32), g...  26.3 us
    ppermute x12, waiting for transfers between devices, swap(): lax.ppermute(value, 'voc', [(i, partner(i, shift)) for i in range(voc_cou...  19 us
    pallas_call x2, Pallas kernels, run_chunk(): pl.pallas_call(kernel, out_shape=tuple(out_shape), grid_spec=pltpu.Prefet...  17 us
    ppermute x12, starting transfers between devices, swap(): lax.ppermute(value, 'voc', [(i, partner(i, shift)) for i in range(voc_cou...  7.91 us
    ppermute x2, starting transfers between devices, body(): kept = kept + lax.ppermute(kept, 'tok', pairs)  4.07 us
    pallas_call x2, Pallas kernels, cut(): pl.pallas_call(kernel, out_shape=tuple((pltpu.VMEM((size, lanes), BF16) i...  4.03 us
    ppermute x1, starting transfers between devices, body(): kept = kept + (lax.ppermute(target, 'tok', pairs) >= 0).astype(F32)  3.06 us
    unnamed x31, local copies, waits for them, and re-layouts  2.14 us
  transfers between devices with their start and end apart: 15, of which 4 were waited for; matrix products, arithmetic and copies ran while one was open for 7% of the time, Pallas kernels for 51%

profile of v5, /device:TPU:0, one launch (start us, length us, event | category | flops | bytes accessed | tf_op | source)
XLA Modules:
  0.0 95.3 jit_solution(11340880894741951613)
XLA Ops:
  0.6 0.0 copy-start.1
  0.6 0.0 copy-start.4
  0.7 3.1 %collective-permute-start.7 = (s32[1,128]{1,0:T(1,128)}, s32[1,128]{1,0:T(1,128)S(1)}, u32[]{:S(2)}, u32[]{:S(2)}) collective-permute-start(s32[1,128]{1,0:T(1,128)} %bitcast.21), channel_id=1, source_target_pairs={{0,4},{4,0},{8,12},{12,8},{16,20},{20,16},{24,28},{28,24},{1,5},{5... | collective-permute-start | bytes 1544 | tf_op jit(solution)/shard_map/ppermute | solution.py:511
  3.7 3.0 %cut.2 = (bf16[3168,128]{1,0:T(8,128)(2,1)}, bf16[528,128]{1,0:T(8,128)(2,1)}, bf16[2640,128]{1,0:T(8,128)(2,1)}, bf16[1584,128]{1,0:T(8,128)(2,1)}, bf16[4752,128]{1,0:T(8,128)(2,1)}) custom-call(bf16[4,4752,128]{2,1,0:T(8,128)(2,1)} %bitcast.26), custom_call_target="tpu_custom_call" | custom-call | tf_op jit(solution)/shard_map/cut/pallas_call | solution.py:432
  6.7 0.1 collective-permute-start.1
  6.8 1.6 %collective-permute-start.3 = (bf16[3168,128]{1,0:T(8,128)(2,1)}, bf16[3168,128]{1,0:T(8,128)(2,1)S(1)}, u32[]{:S(2)}, u32[]{:S(2)}) collective-permute-start(bf16[3168,128]{1,0:T(8,128)(2,1)} %get-tuple-element.14), channel_id=1, source_target_pairs={{0,3},{1,2},{2,1},{3,0},{4,7},{5,6},{6,5},{7,4},{8,11},{9,10},{10,... | collective-permute-start | bytes 2433032 | tf_op jit(solution)/shard_map/ppermute | solution.py:483
  8.4 0.0 copy-done.4
  8.4 0.3 reshape.46
  8.7 0.1 constant_dynamic-slice_fusion.1
  8.9 0.1 broadcast_in_dim.66
  9.1 0.1 broadcast_in_dim.69
  9.2 0.0 collective-permute-done.7
  9.2 0.0 copy-done.1
  9.2 1.6 %collective-permute-start.8 = (f32[1,128]{1,0:T(1,128)S(1)}, f32[1,128]{1,0:T(1,128)S(1)}, u32[]{:S(2)}, u32[]{:S(2)}) collective-permute-start(f32[1,128]{1,0:T(1,128)S(1)} %fusion.2), channel_id=1, source_target_pairs={{0,8},{4,12},{8,0},{12,4},{16,24},{20,28},{24,16},{28,20},{1,9},{5... | collective-permute-start | bytes 1544 | tf_op jit(solution)/shard_map/ppermute | solution.py:513
  10.9 0.9 select_select_fusion.refs_2_.refs_6_.refs_4_
  11.7 26.3 %stats.1.refs_8_ = f32[8,128]{1,0:T(8,128)} custom-call(bf16[19008,128]{1,0:T(8,128)(2,1)} %bitcast.27, bf16[19008,128]{1,0:T(8,128)(2,1)} %bitcast.30, bf16[36,8,528]{2,1,0:T(8,128)(2,1)} %select_select_fusion.refs_2_.refs_6_.refs_4_), custom_call_target="tpu_custom_call" | custom-call | tf_op jit(solution)/shard_map/stats/pallas_call | solution.py:156
  38.1 0.0 copy-start.11
  38.1 0.0 copy-start.12
  38.1 0.1 collective-permute-start.4
  38.2 1.0 %cut.3 = bf16[1584,128]{1,0:T(8,128)(2,1)S(1)} custom-call(bf16[4,4752,128]{2,1,0:T(8,128)(2,1)} %bitcast.28), custom_call_target="tpu_custom_call" | custom-call | tf_op jit(solution)/shard_map/cut/pallas_call | solution.py:432
  39.2 0.1 collective-permute-start.2
  39.3 0.0 collective-permute-done.8
  39.3 0.0 copy-start.13
  39.3 2.4 %collective-permute-start.9 = (f32[1,128]{1,0:T(1,128)S(1)}, f32[1,128]{1,0:T(1,128)S(1)}, u32[]{:S(2)}, u32[]{:S(2)}) collective-permute-start(f32[1,128]{1,0:T(1,128)S(1)} %add.52), channel_id=1, source_target_pairs={{0,16},{4,20},{8,24},{12,28},{16,0},{20,4},{24,8},{28,12},{1,17},{... | collective-permute-start | bytes 1544 | tf_op jit(solution)/shard_map/ppermute | solution.py:513
  41.8 2.1 %collective-permute-done.9 = f32[1,128]{1,0:T(1,128)S(1)} collective-permute-done((f32[1,128]{1,0:T(1,128)S(1)}, f32[1,128]{1,0:T(1,128)S(1)}, u32[]{:S(2)}, u32[]{:S(2)}) %collective-permute-start.9) | collective-permute-done | bytes 544 | tf_op jit(solution)/shard_map/ppermute | solution.py:513
  43.9 0.0 copy-done.13
  43.9 0.6 copy-done.14
  44.4 2.1 %collective-permute-start.11 = (bf16[2640,128]{1,0:T(8,128)(2,1)}, bf16[2640,128]{1,0:T(8,128)(2,1)S(1)}, u32[]{:S(2)}, u32[]{:S(2)}) collective-permute-start(bf16[2640,128]{1,0:T(8,128)(2,1)} %get-tuple-element.17), channel_id=1, source_target_pairs={{0,2},{1,3},{2,0},{3,1},{4,6},{5,7},{6,4},{7,5},{8,10},{9,11},{10,... | collective-permute-start | bytes 2027528 | tf_op jit(solution)/shard_map/ppermute | solution.py:483
  46.5 1.0 %dynamic-slice_bitcast_fusion.refs_1_ = bf16[1584,128]{1,0:T(8,128)(2,1)S(1)} fusion(bf16[128,19008]{0,1:T(8,128)(2,1)} %param.9, s32[]{:T(128)S(6)} %select_n.38), kind=kLoop, calls=%fused_computation | loop fusion | bytes 811012 | tf_op jit(solution)/shard_map/dynamic_slice | solution.py:589
  47.5 0.0 collective-permute-done.4.refs_9_
  47.5 0.0 copy-done.5
  47.6 0.1 collective-permute-start.5
  47.7 0.5 add_add_fusion.refs_0_
  48.2 17.3 %collective-permute-done.5.refs_10_ = f32[8,128]{1,0:T(8,128)S(1)} collective-permute-done((f32[8,128]{1,0:T(8,128)S(1)}, f32[8,128]{1,0:T(8,128)S(1)}, u32[]{:S(2)}, u32[]{:S(2)}) %collective-permute-start.5) | collective-permute-done | bytes 4128 | tf_op jit(solution)/shard_map/ppermute | solution.py:483
  65.5 0.6 copy-done.7
  66.1 0.0 collective-permute-start.6
  66.1 0.8 constant_dynamic-slice_fusion.refs_2_
  66.9 1.2 %add.53.refs_12_ = f32[1,128]{1,0:T(1,128)} add(f32[1,128]{1,0:T(1,128)} %copy-done.13, f32[1,128]{1,0:T(1,128)} %copy-done.14) | non-fusion elementwise | flops 128 | bytes 1536 | tf_op jit(solution)/shard_map/add | solution.py:513
  68.1 1.1 %collective-permute-done.6.refs_11_ = f32[8,128]{1,0:T(8,128)S(1)} collective-permute-done((f32[8,128]{1,0:T(8,128)S(1)}, f32[8,128]{1,0:T(8,128)S(1)}, u32[]{:S(2)}, u32[]{:S(2)}) %collective-permute-start.6) | collective-permute-done | bytes 4128 | tf_op jit(solution)/shard_map/ppermute | solution.py:483
  69.1 0.4 collective-permute-start.10
  69.5 0.0 collective-permute-done.2.refs_3_
  69.5 1.6 %collective-permute-start = (bf16[1584,128]{1,0:T(8,128)(2,1)}, bf16[1584,128]{1,0:T(8,128)(2,1)S(1)}, u32[]{:S(2)}, u32[]{:S(2)}) collective-permute-start(bf16[1584,128]{1,0:T(8,128)(2,1)} %get-tuple-element.12), channel_id=1, source_target_pairs={{0,2},{1,3},{2,0},{3,1},{4,6},{5,7},{6,4},{7,5},{8,10},{9,11},{10,... | collective-permute-start | bytes 1216520 | tf_op jit(solution)/shard_map/ppermute | solution.py:483
  71.2 0.0 collective-permute-done.3.refs_4_
  71.2 0.0 copy-done.8
  71.2 0.0 collective-permute-done.1.refs_2_
  71.2 0.9 copy-done.3
  72.1 11.1 %chunk.2 = (bf16[19008,128]{1,0:T(8,128)(2,1)}, f32[16,128]{1,0:T(8,128)}, f32[8,128]{1,0:T(8,128)}) custom-call(s32[48]{0:T(128)} %add_add_fusion.refs_0_, bf16[19008,128]{1,0:T(8,128)(2,1)} %bitcast.29, bf16[4752,128]{1,0:T(8,128)(2,1)S(1)} %collective-permute-done.1.refs_2_, bf16[1584,128]{1,0:T(8,128)(2,1)} %collective-permute-done.2.refs_3_, ...), custom_call_target="tpu_custom_call" | custom-call | tf_op jit(solution)/shard_map/chunk/pallas_call | solution.py:302
  83.2 0.7 slice_bitcast_fusion
  83.9 0.0 collective-permute-done.10.refs_1_
  83.9 0.0 collective-permute-done.11.refs_2_
  83.9 0.0 copy-start.2
  83.9 5.9 %chunk.3 = (bf16[19008,128]{1,0:T(8,128)(2,1)}, f32[16,128]{1,0:T(8,128)}) custom-call(s32[48]{0:T(128)} %add_add_fusion.refs_0_, bf16[528,128]{1,0:T(8,128)(2,1)} %collective-permute-done.10.refs_1_, bf16[2640,128]{1,0:T(8,128)(2,1)S(1)} %collective-permute-done.11.refs_2_, bf16[19008,128]{1,0:T(8,128)(2,1)} %bitcast.32, ...), custom_call_target="tpu_custom_call", output_to_operand_aliasing={{0}: (8, {})} | custom-call | tf_op jit(solution)/shard_map/chunk/pallas_call | solution.py:302
  89.8 0.7 subtract_reduce_fusion
  90.5 0.0 collective-permute-done.refs_0_
  90.5 0.0 copy-done.2
  90.5 0.5 tail_sum.1
  91.0 0.1 collective-permute-start.12
  91.1 0.5 collective-permute-start.13
  91.6 1.4 %collective-permute-start.14 = (f32[1,128]{1,0:T(1,128)S(1)}, f32[1,128]{1,0:T(1,128)S(1)}, u32[]{:S(2)}, u32[]{:S(2)}) collective-permute-start(f32[1,128]{1,0:T(1,128)S(1)} %tail_sum.1), channel_id=1, source_target_pairs={{0,3},{1,2},{2,1},{3,0},{4,7},{5,6},{6,5},{7,4},{8,11},{9,10},{10,... | collective-permute-start | bytes 1544 | tf_op jit(solution)/shard_map/ppermute | solution.py:483
  92.9 1.2 %tail_grad.1 = bf16[19008,128]{1,0:T(8,128)(2,1)} custom-call(bf16[1584,128]{1,0:T(8,128)(2,1)S(1)} %collective-permute-done.refs_0_, bf16[1584,128]{1,0:T(8,128)(2,1)S(1)} %dynamic-slice_bitcast_fusion.refs_1_, bf16[3,8,528]{2,1,0:T(8,128)(2,1)S(1)} %constant_dynamic-slice_fusion.refs_2_, f32[8,128]{1,0:T(8,128)S(1)} %copy-done, ...), custom_call_target="tpu_custom_call", output_to_operand_aliasing={{}: (5, {})} | custom-call | tf_op jit(solution)/shard_map/tail_grad/pallas_call | solution.py:394
  94.2 0.0 collective-permute-done.12
  94.2 0.5 collective-permute-done.13
  94.7 0.0 collective-permute-done.14
  94.7 0.5 add_bitcast_fusion
  (24 shorter events, 0.2 us)
Async XLA Ops:
  0.6 8.6 %copy-start.1 = (s32[128]{0:T(128)S(1)}, s32[128]{0:T(128)}, u32[]{:S(2)}) copy-start(s32[128]{0:T(128)} %param.10) | copy-start | bytes 1540
  0.6 7.8 %copy-start.4 = (s32[76032]{0:T(1024)S(1)}, s32[76032]{0:T(1024)}, u32[]{:S(2)}) copy-start(s32[76032]{0:T(1024)} %param.11) | copy-start | bytes 912388
  0.7 8.5 %collective-permute-start.7 = (s32[1,128]{1,0:T(1,128)}, s32[1,128]{1,0:T(1,128)S(1)}, u32[]{:S(2)}, u32[]{:S(2)}) collective-permute-start(s32[1,128]{1,0:T(1,128)} %bitcast.21), channel_id=1, source_target_pairs={{0,4},{4,0},{8,12},{12,8},{16,20},{20,16},{24,28},{28,24},{1,5},{5... | collective-permute-start | bytes 1544 | tf_op jit(solution)/shard_map/ppermute | solution.py:511
  6.7 64.5 %collective-permute-start.1 = (bf16[4752,128]{1,0:T(8,128)(2,1)}, bf16[4752,128]{1,0:T(8,128)(2,1)S(1)}, u32[]{:S(2)}, u32[]{:S(2)}) collective-permute-start(bf16[4752,128]{1,0:T(8,128)(2,1)} %get-tuple-element.13), channel_id=1, source_target_pairs={{0,1},{1,0},{2,3},{3,2},{4,5},{5,4},{6,7},{7,6},{8,9},{9,8},{10,11... | collective-permute-start | bytes 3649544 | tf_op jit(solution)/shard_map/ppermute | solution.py:483
  6.8 64.4 %collective-permute-start.3 = (bf16[3168,128]{1,0:T(8,128)(2,1)}, bf16[3168,128]{1,0:T(8,128)(2,1)S(1)}, u32[]{:S(2)}, u32[]{:S(2)}) collective-permute-start(bf16[3168,128]{1,0:T(8,128)(2,1)} %get-tuple-element.14), channel_id=1, source_target_pairs={{0,3},{1,2},{2,1},{3,0},{4,7},{5,6},{6,5},{7,4},{8,11},{9,10},{10,... | collective-permute-start | bytes 2433032 | tf_op jit(solution)/shard_map/ppermute | solution.py:483
  9.2 30.1 %collective-permute-start.8 = (f32[1,128]{1,0:T(1,128)S(1)}, f32[1,128]{1,0:T(1,128)S(1)}, u32[]{:S(2)}, u32[]{:S(2)}) collective-permute-start(f32[1,128]{1,0:T(1,128)S(1)} %fusion.2), channel_id=1, source_target_pairs={{0,8},{4,12},{8,0},{12,4},{16,24},{20,28},{24,16},{28,20},{1,9},{5... | collective-permute-start | bytes 1544 | tf_op jit(solution)/shard_map/ppermute | solution.py:513
  38.1 9.5 %copy-start.5 = (f32[8,128]{1,0:T(8,128)S(1)}, f32[8,128]{1,0:T(8,128)}, u32[]{:S(2)}) copy-start(f32[8,128]{1,0:T(8,128)} %stats.1.refs_8_) | copy-start | bytes 12292
  38.1 9.6 %copy-start.9 = (s32[48]{0:T(128)S(1)}, s32[48]{0:T(128)}, u32[]{:S(2)}) copy-start(s32[48]{0:T(128)} %constant.56.clone) | copy-start | bytes 580
  38.1 9.6 %copy-start.10 = (s32[48]{0:T(128)S(1)}, s32[48]{0:T(128)}, u32[]{:S(2)}) copy-start(s32[48]{0:T(128)} %constant.57.clone) | copy-start | bytes 580
  38.1 9.6 %copy-start.11 = (s32[48]{0:T(128)S(1)}, s32[48]{0:T(128)}, u32[]{:S(2)}) copy-start(s32[48]{0:T(128)} %constant.58.clone) | copy-start | bytes 580
  38.1 9.6 %copy-start.12 = (s32[48]{0:T(128)S(1)}, s32[48]{0:T(128)}, u32[]{:S(2)}) copy-start(s32[48]{0:T(128)} %constant.59.clone) | copy-start | bytes 580
  38.1 9.4 %collective-permute-start.4 = (f32[8,128]{1,0:T(8,128)}, f32[8,128]{1,0:T(8,128)S(1)}, u32[]{:S(2)}, u32[]{:S(2)}) collective-permute-start(f32[8,128]{1,0:T(8,128)} %stats.1.refs_8_), channel_id=1, source_target_pairs={{0,1},{1,0},{2,3},{3,2},{4,5},{5,4},{6,7},{7,6},{8,9},{9,8},{10,11... | collective-permute-start | bytes 12296 | tf_op jit(solution)/shard_map/ppermute | solution.py:483
  39.2 30.3 %collective-permute-start.2 = (bf16[1584,128]{1,0:T(8,128)(2,1)S(1)}, bf16[1584,128]{1,0:T(8,128)(2,1)}, u32[]{:S(2)}, u32[]{:S(2)}) collective-permute-start(bf16[1584,128]{1,0:T(8,128)(2,1)S(1)} %cut.3), channel_id=1, source_target_pairs={{0,3},{1,2},{2,1},{3,0},{4,7},{5,6},{6,5},{7,4},{8,11},{9,10},{10,... | collective-permute-start | bytes 1216520 | tf_op jit(solution)/shard_map/ppermute | solution.py:483
  39.3 4.5 %copy-start.13 = (f32[1,128]{1,0:T(1,128)}, f32[1,128]{1,0:T(1,128)S(1)}, u32[]{:S(2)}) copy-start(f32[1,128]{1,0:T(1,128)S(1)} %add.52) | copy-start | bytes 1540
  39.3 4.5 %collective-permute-start.9 = (f32[1,128]{1,0:T(1,128)S(1)}, f32[1,128]{1,0:T(1,128)S(1)}, u32[]{:S(2)}, u32[]{:S(2)}) collective-permute-start(f32[1,128]{1,0:T(1,128)S(1)} %add.52), channel_id=1, source_target_pairs={{0,16},{4,20},{8,24},{12,28},{16,0},{20,4},{24,8},{28,12},{1,17},{... | collective-permute-start | bytes 1544 | tf_op jit(solution)/shard_map/ppermute | solution.py:513
  43.9 0.6 copy-start.14
  44.4 39.5 %collective-permute-start.11 = (bf16[2640,128]{1,0:T(8,128)(2,1)}, bf16[2640,128]{1,0:T(8,128)(2,1)S(1)}, u32[]{:S(2)}, u32[]{:S(2)}) collective-permute-start(bf16[2640,128]{1,0:T(8,128)(2,1)} %get-tuple-element.17), channel_id=1, source_target_pairs={{0,2},{1,3},{2,0},{3,1},{4,6},{5,7},{6,4},{7,5},{8,10},{9,11},{10,... | collective-permute-start | bytes 2027528 | tf_op jit(solution)/shard_map/ppermute | solution.py:483
  47.6 23.6 %copy-start.6 = (f32[8,128]{1,0:T(8,128)}, f32[8,128]{1,0:T(8,128)S(1)}, u32[]{:S(2)}) copy-start(f32[8,128]{1,0:T(8,128)S(1)} %collective-permute-done.4.refs_9_) | copy-start | bytes 12292
  47.6 18.0 %collective-permute-start.5 = (f32[8,128]{1,0:T(8,128)S(1)}, f32[8,128]{1,0:T(8,128)S(1)}, u32[]{:S(2)}, u32[]{:S(2)}) collective-permute-start(f32[8,128]{1,0:T(8,128)S(1)} %copy-done.5), channel_id=1, source_target_pairs={{0,2},{1,3},{2,0},{3,1},{4,6},{5,7},{6,4},{7,5},{8,10},{9,11},{10,... | collective-permute-start | bytes 12296 | tf_op jit(solution)/shard_map/ppermute | solution.py:483
  65.5 0.6 copy-start.7
  66.1 3.0 %collective-permute-start.6 = (f32[8,128]{1,0:T(8,128)S(1)}, f32[8,128]{1,0:T(8,128)S(1)}, u32[]{:S(2)}, u32[]{:S(2)}) collective-permute-start(f32[8,128]{1,0:T(8,128)S(1)} %copy-done.5), channel_id=1, source_target_pairs={{0,3},{1,2},{2,1},{3,0},{4,7},{5,6},{6,5},{7,4},{8,11},{9,10},{10,... | collective-permute-start | bytes 12296 | tf_op jit(solution)/shard_map/ppermute | solution.py:483
  69.1 2.0 %copy-start.8 = (f32[8,128]{1,0:T(8,128)}, f32[8,128]{1,0:T(8,128)S(1)}, u32[]{:S(2)}) copy-start(f32[8,128]{1,0:T(8,128)S(1)} %collective-permute-done.6.refs_11_) | copy-start | bytes 12292
  69.1 14.8 %collective-permute-start.10 = (bf16[528,128]{1,0:T(8,128)(2,1)}, bf16[528,128]{1,0:T(8,128)(2,1)}, u32[]{:S(2)}, u32[]{:S(2)}) collective-permute-start(bf16[528,128]{1,0:T(8,128)(2,1)} %get-tuple-element.16), channel_id=1, source_target_pairs={{0,2},{1,3},{2,0},{3,1},{4,6},{5,7},{6,4},{7,5},{8,10},{9,11},{10,... | collective-permute-start | bytes 405512 | tf_op jit(solution)/shard_map/ppermute | solution.py:483
  69.5 21.0 %collective-permute-start = (bf16[1584,128]{1,0:T(8,128)(2,1)}, bf16[1584,128]{1,0:T(8,128)(2,1)S(1)}, u32[]{:S(2)}, u32[]{:S(2)}) collective-permute-start(bf16[1584,128]{1,0:T(8,128)(2,1)} %get-tuple-element.12), channel_id=1, source_target_pairs={{0,2},{1,3},{2,0},{3,1},{4,6},{5,7},{6,4},{7,5},{8,10},{9,11},{10,... | collective-permute-start | bytes 1216520 | tf_op jit(solution)/shard_map/ppermute | solution.py:483
  71.2 0.9 copy-start.3
  83.9 6.6 %copy-start = (f32[8,128]{1,0:T(8,128)S(1)}, f32[8,128]{1,0:T(8,128)}, u32[]{:S(2)}) copy-start(f32[8,128]{1,0:T(8,128)} %get-tuple-element.15.refs_6_.refs_3_) | copy-start | bytes 12292
  83.9 6.6 %copy-start.2 = (s32[128]{0:T(128)S(1)}, s32[128]{0:T(128)}, u32[]{:S(2)}) copy-start(s32[128]{0:T(128)} %param.10) | copy-start | bytes 1540
  91.0 3.2 %collective-permute-start.12 = (f32[1,128]{1,0:T(1,128)S(1)}, f32[1,128]{1,0:T(1,128)S(1)}, u32[]{:S(2)}, u32[]{:S(2)}) collective-permute-start(f32[1,128]{1,0:T(1,128)S(1)} %tail_sum.1), channel_id=1, source_target_pairs={{0,1},{1,0},{2,3},{3,2},{4,5},{5,4},{6,7},{7,6},{8,9},{9,8},{10,11... | collective-permute-start | bytes 1544 | tf_op jit(solution)/shard_map/ppermute | solution.py:483
  91.1 3.6 %collective-permute-start.13 = (f32[1,128]{1,0:T(1,128)S(1)}, f32[1,128]{1,0:T(1,128)S(1)}, u32[]{:S(2)}, u32[]{:S(2)}) collective-permute-start(f32[1,128]{1,0:T(1,128)S(1)} %tail_sum.1), channel_id=1, source_target_pairs={{0,2},{1,3},{2,0},{3,1},{4,6},{5,7},{6,4},{7,5},{8,10},{9,11},{10,... | collective-permute-start | bytes 1544 | tf_op jit(solution)/shard_map/ppermute | solution.py:483
  91.6 3.2 %collective-permute-start.14 = (f32[1,128]{1,0:T(1,128)S(1)}, f32[1,128]{1,0:T(1,128)S(1)}, u32[]{:S(2)}, u32[]{:S(2)}) collective-permute-start(f32[1,128]{1,0:T(1,128)S(1)} %tail_sum.1), channel_id=1, source_target_pairs={{0,3},{1,2},{2,1},{3,0},{4,7},{5,6},{6,5},{7,4},{8,11},{9,10},{10,... | collective-permute-start | bytes 1544 | tf_op jit(solution)/shard_map/ppermute | solution.py:483

commit v6 on v5

--- a/solution.py
+++ b/solution.py
@@ -12,9 +12,8 @@
 LOW = -3e38
 ROWS = 16
 LINES = 8
-HELD_BYTES = 2.3 * 2**20
+HELD_BYTES = 2.4 * 2**20
 WAYS = 3
-AHEAD = 1
 STEP = 544
 LN2 = 0.6931471805599453
 F32 = jnp.float32
@@ -453,11 +452,10 @@
         if chunked and index == 0:
             pieces += [(shift, 0, big, big), (shift, big, 2 * big, big)]
         elif chunked and index == len(far) - 1:
-            pieces += [(shift, 0, AHEAD * small, small), (shift, AHEAD * small, (6 - AHEAD) * small, small),
-                       (shift, 2 * big, big, big)]
+            pieces += [(shift, 0, 2 * big, big), (shift, 2 * big, big, big)]
         else:
             pieces.append((shift, 0, padded, big))
-    late = [k for k, piece in enumerate(pieces) if len(far) > 1 and piece[0] == far[-1] and (piece[1] or not chunked)]
+    late = [k for k, piece in enumerate(pieces) if len(far) > 1 and piece[0] == far[-1]]
     pieces += [(shift, 0, padded, big) for shift in near]
     early = [k for k in range(len(pieces)) if k not in late]
     return pieces, early, late, big

time: 96.6 us -> 81.8 us (0.85)
  waiting for transfers between devices: 21.1 us -> 12.7 us
  local copies, waits for them, and re-layouts: 5.23 us -> 3.18 us
  Pallas kernels: 49.1 us -> 47.1 us
  starting transfers between devices: 15 us -> 14 us
    ppermute x12 -> x11, waiting for transfers between devices: 19 us -> 10.3 us  [swap(): lax.ppermute(value, 'voc', [(i, partner(i, shift)) for i in range(voc_cou...]
    unnamed x31 -> x25, local copies, waits for them, and re-layouts: 2.14 us -> 0.08 us
    pallas_call x2, Pallas kernels: 17 us -> 15 us  [run_chunk(): pl.pallas_call(kernel, out_shape=tuple(out_shape), grid_spec=pltpu.Prefet...]
    ppermute x12 -> x11, starting transfers between devices: 7.91 us -> 7.11 us  [swap(): lax.ppermute(value, 'voc', [(i, partner(i, shift)) for i in range(voc_cou...]
  transfers between devices with their start and end apart: 15 -> 14, of which waited for: 4 -> 5; matrix products, arithmetic and copies ran while one was open for 7% -> 7% of each run, Pallas kernels for 51% -> 57%
where the time goes in v6:
time: 81.8 us; the launch traced here: 81.1 us
  Pallas kernels  47.1 us (58%)
  starting transfers between devices  14 us (17%)
  waiting for transfers between devices  12.7 us (16%)
  other arithmetic  3.2 us (4%)
  local copies, waits for them, and re-layouts  3.18 us (4%)
  between operations  0.92 us (1%)
    pallas_call x1, Pallas kernels, run_stats(): pl.pallas_call(kernel, out_shape=jax.ShapeDtypeStruct((8, lanes), F32), g...  26.3 us
    pallas_call x2, Pallas kernels, run_chunk(): pl.pallas_call(kernel, out_shape=tuple(out_shape), grid_spec=pltpu.Prefet...  15 us
    ppermute x11, waiting for transfers between devices, swap(): lax.ppermute(value, 'voc', [(i, partner(i, shift)) for i in range(voc_cou...  10.3 us
    ppermute x11, starting transfers between devices, swap(): lax.ppermute(value, 'voc', [(i, partner(i, shift)) for i in range(voc_cou...  7.11 us
    pallas_call x2, Pallas kernels, cut(): pl.pallas_call(kernel, out_shape=tuple((pltpu.VMEM((size, lanes), BF16) i...  4.02 us
    ppermute x2, starting transfers between devices, body(): kept = kept + lax.ppermute(kept, 'tok', pairs)  3.79 us
    ppermute x1, starting transfers between devices, body(): kept = kept + (lax.ppermute(target, 'tok', pairs) >= 0).astype(F32)  3.06 us
    ppermute x2, waiting for transfers between devices, body(): kept = kept + lax.ppermute(kept, 'tok', pairs)  2.39 us
  transfers between devices with their start and end apart: 14, of which 5 were waited for; matrix products, arithmetic and copies ran while one was open for 7% of the time, Pallas kernels for 57%

profile of v6, /device:TPU:0, one launch (start us, length us, event | category | flops | bytes accessed | tf_op | source)
XLA Modules:
  0.0 81.1 jit_solution(11637637598497054447)
XLA Ops:
  0.6 0.0 copy-start.1
  0.6 0.0 copy-start.3
  0.7 3.1 %collective-permute-start.7 = (s32[1,128]{1,0:T(1,128)}, s32[1,128]{1,0:T(1,128)S(1)}, u32[]{:S(2)}, u32[]{:S(2)}) collective-permute-start(s32[1,128]{1,0:T(1,128)} %bitcast.21), channel_id=1, source_target_pairs={{0,4},{4,0},{8,12},{12,8},{16,20},{20,16},{24,28},{28,24},{1,5},{5... | collective-permute-start | bytes 1544 | tf_op jit(solution)/shard_map/ppermute | solution.py:509
  3.7 3.0 %cut.2 = (bf16[3168,128]{1,0:T(8,128)(2,1)}, bf16[3168,128]{1,0:T(8,128)(2,1)}, bf16[1584,128]{1,0:T(8,128)(2,1)}, bf16[4752,128]{1,0:T(8,128)(2,1)}) custom-call(bf16[4,4752,128]{2,1,0:T(8,128)(2,1)} %bitcast.26), custom_call_target="tpu_custom_call" | custom-call | tf_op jit(solution)/shard_map/cut/pallas_call | solution.py:431
  6.7 0.1 collective-permute-start.1
  6.8 1.6 %collective-permute-start.3 = (bf16[3168,128]{1,0:T(8,128)(2,1)}, bf16[3168,128]{1,0:T(8,128)(2,1)}, u32[]{:S(2)}, u32[]{:S(2)}) collective-permute-start(bf16[3168,128]{1,0:T(8,128)(2,1)} %get-tuple-element.13), channel_id=1, source_target_pairs={{0,3},{1,2},{2,1},{3,0},{4,7},{5,6},{6,5},{7,4},{8,11},{9,10},{10,... | collective-permute-start | bytes 2433032 | tf_op jit(solution)/shard_map/ppermute | solution.py:481
  8.4 0.5 collective-permute-start.10
  8.9 0.0 copy-done.3
  8.9 0.3 reshape.46
  9.2 0.1 constant_dynamic-slice_fusion.1
  9.4 0.1 broadcast_in_dim.66
  9.6 0.1 broadcast_in_dim.69
  9.7 0.0 collective-permute-done.7
  9.7 0.0 copy-done.1
  9.7 1.6 %collective-permute-start.8 = (f32[1,128]{1,0:T(1,128)S(1)}, f32[1,128]{1,0:T(1,128)S(1)}, u32[]{:S(2)}, u32[]{:S(2)}) collective-permute-start(f32[1,128]{1,0:T(1,128)S(1)} %fusion.2), channel_id=1, source_target_pairs={{0,8},{4,12},{8,0},{12,4},{16,24},{20,28},{24,16},{28,20},{1,9},{5... | collective-permute-start | bytes 1544 | tf_op jit(solution)/shard_map/ppermute | solution.py:511
  11.4 0.9 %select_select_fusion.refs_2_.refs_6_.refs_3_ = bf16[36,8,528]{2,1,0:T(8,128)(2,1)} fusion(pred[8]{0:T(512)(128)(4,1)S(1)} %get-tuple-element.22, pred[8]{0:T(512)(128)(4,1)S(1)} %get-tuple-element.23, bf16[8]{0:T(256)(128)(2,1)S(1)} %fusion, bf16[36,528]{1,0:T(8,128)(2,1)S(1)} %broadcast_in_dim.69, bf16[36,528]{1,0:T(8,128)(2,1)S(1)} %broadcast_in_dim.66), kind=kLoop, calls=%fused_computation.1 | loop fusion | flops 304128 | bytes 380192 | tf_op jit(solution)/shard_map/jit(_where)/select_n | solution.py:525
  12.2 26.3 %stats.1.refs_8_ = f32[8,128]{1,0:T(8,128)} custom-call(bf16[19008,128]{1,0:T(8,128)(2,1)} %bitcast.27, bf16[19008,128]{1,0:T(8,128)(2,1)} %bitcast.30, bf16[36,8,528]{2,1,0:T(8,128)(2,1)} %select_select_fusion.refs_2_.refs_6_.refs_3_), custom_call_target="tpu_custom_call" | custom-call | tf_op jit(solution)/shard_map/stats/pallas_call | solution.py:155
  38.6 0.0 copy-start.10
  38.6 0.0 copy-start.11
  38.6 0.1 collective-permute-start.4
  38.7 1.0 %cut.3 = bf16[1584,128]{1,0:T(8,128)(2,1)S(1)} custom-call(bf16[4,4752,128]{2,1,0:T(8,128)(2,1)} %bitcast.28), custom_call_target="tpu_custom_call" | custom-call | tf_op jit(solution)/shard_map/cut/pallas_call | solution.py:431
  39.7 0.0 collective-permute-done.8
  39.7 2.1 %collective-permute-start.9 = (f32[1,128]{1,0:T(1,128)S(1)}, f32[1,128]{1,0:T(1,128)S(1)}, u32[]{:S(2)}, u32[]{:S(2)}) collective-permute-start(f32[1,128]{1,0:T(1,128)S(1)} %add.52), channel_id=1, source_target_pairs={{0,16},{4,20},{8,24},{12,28},{16,0},{20,4},{24,8},{28,12},{1,17},{... | collective-permute-start | bytes 1544 | tf_op jit(solution)/shard_map/ppermute | solution.py:511
  41.9 2.4 %collective-permute-done.9 = f32[1,128]{1,0:T(1,128)S(1)} collective-permute-done((f32[1,128]{1,0:T(1,128)S(1)}, f32[1,128]{1,0:T(1,128)S(1)}, u32[]{:S(2)}, u32[]{:S(2)}) %collective-permute-start.9) | collective-permute-done | bytes 544 | tf_op jit(solution)/shard_map/ppermute | solution.py:511
  44.3 0.0 collective-permute-start.2
  44.3 1.0 %dynamic-slice_bitcast_fusion.refs_1_ = bf16[1584,128]{1,0:T(8,128)(2,1)S(1)} fusion(bf16[128,19008]{0,1:T(8,128)(2,1)} %param.9, s32[]{:T(128)S(6)} %select_n.38), kind=kLoop, calls=%fused_computation | loop fusion | bytes 811012 | tf_op jit(solution)/shard_map/dynamic_slice | solution.py:587
  45.3 0.0 collective-permute-done.4.refs_9_
  45.3 0.0 copy-done.4
  45.3 0.0 copy-start.5
  45.3 1.0 %collective-permute-start.5 = (f32[8,128]{1,0:T(8,128)S(1)}, f32[8,128]{1,0:T(8,128)S(1)}, u32[]{:S(2)}, u32[]{:S(2)}) collective-permute-start(f32[8,128]{1,0:T(8,128)S(1)} %copy-done.4), channel_id=1, source_target_pairs={{0,2},{1,3},{2,0},{3,1},{4,6},{5,7},{6,4},{7,5},{8,10},{9,11},{10,... | collective-permute-start | bytes 12296 | tf_op jit(solution)/shard_map/ppermute | solution.py:481
  46.4 0.0 copy-done.8
  46.4 0.0 copy-done.9
  46.4 0.0 copy-done.10
  46.4 0.0 copy-done.11
  46.4 0.5 add_add_fusion.refs_0_
  46.9 8.2 %collective-permute-done.5.refs_10_ = f32[8,128]{1,0:T(8,128)S(1)} collective-permute-done((f32[8,128]{1,0:T(8,128)S(1)}, f32[8,128]{1,0:T(8,128)S(1)}, u32[]{:S(2)}, u32[]{:S(2)}) %collective-permute-start.5) | collective-permute-done | bytes 4128 | tf_op jit(solution)/shard_map/ppermute | solution.py:481
  55.1 0.6 collective-permute-start.6
  55.7 0.8 constant_dynamic-slice_fusion.refs_2_
  56.5 0.5 add.53.refs_12_
  57.0 1.1 %collective-permute-done.6.refs_11_ = f32[8,128]{1,0:T(8,128)S(1)} collective-permute-done((f32[8,128]{1,0:T(8,128)S(1)}, f32[8,128]{1,0:T(8,128)S(1)}, u32[]{:S(2)}, u32[]{:S(2)}) %collective-permute-start.6) | collective-permute-done | bytes 4128 | tf_op jit(solution)/shard_map/ppermute | solution.py:481
  58.1 1.3 %collective-permute-start = (bf16[1584,128]{1,0:T(8,128)(2,1)}, bf16[1584,128]{1,0:T(8,128)(2,1)S(1)}, u32[]{:S(2)}, u32[]{:S(2)}) collective-permute-start(bf16[1584,128]{1,0:T(8,128)(2,1)} %get-tuple-element.11), channel_id=1, source_target_pairs={{0,2},{1,3},{2,0},{3,1},{4,6},{5,7},{6,4},{7,5},{8,10},{9,11},{10,... | collective-permute-start | bytes 1216520 | tf_op jit(solution)/shard_map/ppermute | solution.py:481
  59.4 0.0 collective-permute-done.2.refs_3_
  59.4 0.0 collective-permute-done.3.refs_4_
  59.4 0.0 collective-permute-done.1.refs_2_
  59.4 0.0 copy-done.5
  59.4 0.0 copy-done.6
  59.4 0.0 copy-done.7
  59.4 11.1 %chunk.2 = (bf16[19008,128]{1,0:T(8,128)(2,1)}, f32[16,128]{1,0:T(8,128)}, f32[8,128]{1,0:T(8,128)}) custom-call(s32[36]{0:T(128)} %add_add_fusion.refs_0_, bf16[19008,128]{1,0:T(8,128)(2,1)} %bitcast.29, bf16[4752,128]{1,0:T(8,128)(2,1)S(1)} %collective-permute-done.1.refs_2_, bf16[1584,128]{1,0:T(8,128)(2,1)} %collective-permute-done.2.refs_3_, ...), custom_call_target="tpu_custom_call" | custom-call | tf_op jit(solution)/shard_map/chunk/pallas_call | solution.py:301
  70.5 0.7 slice_bitcast_fusion
  71.2 0.0 collective-permute-done.10.refs_1_
  71.2 3.9 %chunk.3 = (bf16[19008,128]{1,0:T(8,128)(2,1)}, f32[16,128]{1,0:T(8,128)}) custom-call(s32[36]{0:T(128)} %add_add_fusion.refs_0_, bf16[3168,128]{1,0:T(8,128)(2,1)S(1)} %collective-permute-done.10.refs_1_, bf16[19008,128]{1,0:T(8,128)(2,1)} %bitcast.32, ...), custom_call_target="tpu_custom_call", output_to_operand_aliasing={{0}: (7, {})} | custom-call | tf_op jit(solution)/shard_map/chunk/pallas_call | solution.py:301
  75.1 0.7 subtract_reduce_fusion
  75.8 0.0 copy-done
  75.8 0.0 collective-permute-done.refs_0_
  75.9 0.0 copy-done.2
  75.9 0.5 tail_sum.1
  76.3 0.1 collective-permute-start.11
  76.4 1.1 %collective-permute-start.12 = (f32[1,128]{1,0:T(1,128)S(1)}, f32[1,128]{1,0:T(1,128)S(1)}, u32[]{:S(2)}, u32[]{:S(2)}) collective-permute-start(f32[1,128]{1,0:T(1,128)S(1)} %tail_sum.1), channel_id=1, source_target_pairs={{0,2},{1,3},{2,0},{3,1},{4,6},{5,7},{6,4},{7,5},{8,10},{9,11},{10,... | collective-permute-start | bytes 1544 | tf_op jit(solution)/shard_map/ppermute | solution.py:481
  77.6 0.7 collective-permute-start.13
  78.3 1.2 %tail_grad.1 = bf16[19008,128]{1,0:T(8,128)(2,1)} custom-call(bf16[1584,128]{1,0:T(8,128)(2,1)S(1)} %collective-permute-done.refs_0_, bf16[1584,128]{1,0:T(8,128)(2,1)S(1)} %dynamic-slice_bitcast_fusion.refs_1_, bf16[3,8,528]{2,1,0:T(8,128)(2,1)S(1)} %constant_dynamic-slice_fusion.refs_2_, f32[8,128]{1,0:T(8,128)S(1)} %copy-done, ...), custom_call_target="tpu_custom_call", output_to_operand_aliasing={{}: (5, {})} | custom-call | tf_op jit(solution)/shard_map/tail_grad/pallas_call | solution.py:393
  79.5 0.0 collective-permute-done.11
  79.5 0.5 collective-permute-done.12
  80.1 0.5 collective-permute-done.13
  80.6 0.5 add_bitcast_fusion
  (16 shorter events, 0.1 us)
Async XLA Ops:
  0.6 9.1 %copy-start.1 = (s32[128]{0:T(128)S(1)}, s32[128]{0:T(128)}, u32[]{:S(2)}) copy-start(s32[128]{0:T(128)} %param.10) | copy-start | bytes 1540
  0.6 8.3 %copy-start.3 = (s32[76032]{0:T(1024)S(1)}, s32[76032]{0:T(1024)}, u32[]{:S(2)}) copy-start(s32[76032]{0:T(1024)} %param.11) | copy-start | bytes 912388
  0.7 9.1 %collective-permute-start.7 = (s32[1,128]{1,0:T(1,128)}, s32[1,128]{1,0:T(1,128)S(1)}, u32[]{:S(2)}, u32[]{:S(2)}) collective-permute-start(s32[1,128]{1,0:T(1,128)} %bitcast.21), channel_id=1, source_target_pairs={{0,4},{4,0},{8,12},{12,8},{16,20},{20,16},{24,28},{28,24},{1,5},{5... | collective-permute-start | bytes 1544 | tf_op jit(solution)/shard_map/ppermute | solution.py:509
  6.7 52.7 %collective-permute-start.1 = (bf16[4752,128]{1,0:T(8,128)(2,1)}, bf16[4752,128]{1,0:T(8,128)(2,1)S(1)}, u32[]{:S(2)}, u32[]{:S(2)}) collective-permute-start(bf16[4752,128]{1,0:T(8,128)(2,1)} %get-tuple-element.12), channel_id=1, source_target_pairs={{0,1},{1,0},{2,3},{3,2},{4,5},{5,4},{6,7},{7,6},{8,9},{9,8},{10,11... | collective-permute-start | bytes 3649544 | tf_op jit(solution)/shard_map/ppermute | solution.py:481
  6.8 52.6 %collective-permute-start.3 = (bf16[3168,128]{1,0:T(8,128)(2,1)}, bf16[3168,128]{1,0:T(8,128)(2,1)}, u32[]{:S(2)}, u32[]{:S(2)}) collective-permute-start(bf16[3168,128]{1,0:T(8,128)(2,1)} %get-tuple-element.13), channel_id=1, source_target_pairs={{0,3},{1,2},{2,1},{3,0},{4,7},{5,6},{6,5},{7,4},{8,11},{9,10},{10,... | collective-permute-start | bytes 2433032 | tf_op jit(solution)/shard_map/ppermute | solution.py:481
  8.4 62.8 %collective-permute-start.10 = (bf16[3168,128]{1,0:T(8,128)(2,1)}, bf16[3168,128]{1,0:T(8,128)(2,1)S(1)}, u32[]{:S(2)}, u32[]{:S(2)}) collective-permute-start(bf16[3168,128]{1,0:T(8,128)(2,1)} %get-tuple-element.15), channel_id=1, source_target_pairs={{0,2},{1,3},{2,0},{3,1},{4,6},{5,7},{6,4},{7,5},{8,10},{9,11},{10,... | collective-permute-start | bytes 2433032 | tf_op jit(solution)/shard_map/ppermute | solution.py:481
  9.7 30.0 %collective-permute-start.8 = (f32[1,128]{1,0:T(1,128)S(1)}, f32[1,128]{1,0:T(1,128)S(1)}, u32[]{:S(2)}, u32[]{:S(2)}) collective-permute-start(f32[1,128]{1,0:T(1,128)S(1)} %fusion.2), channel_id=1, source_target_pairs={{0,8},{4,12},{8,0},{12,4},{16,24},{20,28},{24,16},{28,20},{1,9},{5... | collective-permute-start | bytes 1544 | tf_op jit(solution)/shard_map/ppermute | solution.py:511
  38.6 6.7 %copy-start.4 = (f32[8,128]{1,0:T(8,128)S(1)}, f32[8,128]{1,0:T(8,128)}, u32[]{:S(2)}) copy-start(f32[8,128]{1,0:T(8,128)} %stats.1.refs_8_) | copy-start | bytes 12292
  38.6 7.8 %copy-start.8 = (s32[36]{0:T(128)S(1)}, s32[36]{0:T(128)}, u32[]{:S(2)}) copy-start(s32[36]{0:T(128)} %constant.56.clone) | copy-start | bytes 436
  38.6 7.8 %copy-start.9 = (s32[36]{0:T(128)S(1)}, s32[36]{0:T(128)}, u32[]{:S(2)}) copy-start(s32[36]{0:T(128)} %constant.57.clone) | copy-start | bytes 436
  38.6 7.8 %copy-start.10 = (s32[36]{0:T(128)S(1)}, s32[36]{0:T(128)}, u32[]{:S(2)}) copy-start(s32[36]{0:T(128)} %constant.58.clone) | copy-start | bytes 436
  38.6 7.8 %copy-start.11 = (s32[36]{0:T(128)S(1)}, s32[36]{0:T(128)}, u32[]{:S(2)}) copy-start(s32[36]{0:T(128)} %constant.59.clone) | copy-start | bytes 436
  38.6 6.7 %collective-permute-start.4 = (f32[8,128]{1,0:T(8,128)}, f32[8,128]{1,0:T(8,128)S(1)}, u32[]{:S(2)}, u32[]{:S(2)}) collective-permute-start(f32[8,128]{1,0:T(8,128)} %stats.1.refs_8_), channel_id=1, source_target_pairs={{0,1},{1,0},{2,3},{3,2},{4,5},{5,4},{6,7},{7,6},{8,9},{9,8},{10,11... | collective-permute-start | bytes 12296 | tf_op jit(solution)/shard_map/ppermute | solution.py:481
  39.7 4.5 %collective-permute-start.9 = (f32[1,128]{1,0:T(1,128)S(1)}, f32[1,128]{1,0:T(1,128)S(1)}, u32[]{:S(2)}, u32[]{:S(2)}) collective-permute-start(f32[1,128]{1,0:T(1,128)S(1)} %add.52), channel_id=1, source_target_pairs={{0,16},{4,20},{8,24},{12,28},{16,0},{20,4},{24,8},{28,12},{1,17},{... | collective-permute-start | bytes 1544 | tf_op jit(solution)/shard_map/ppermute | solution.py:511
  44.3 15.1 %collective-permute-start.2 = (bf16[1584,128]{1,0:T(8,128)(2,1)S(1)}, bf16[1584,128]{1,0:T(8,128)(2,1)}, u32[]{:S(2)}, u32[]{:S(2)}) collective-permute-start(bf16[1584,128]{1,0:T(8,128)(2,1)S(1)} %cut.3), channel_id=1, source_target_pairs={{0,3},{1,2},{2,1},{3,0},{4,7},{5,6},{6,5},{7,4},{8,11},{9,10},{10,... | collective-permute-start | bytes 1216520 | tf_op jit(solution)/shard_map/ppermute | solution.py:481
  45.3 14.1 %copy-start.5 = (f32[8,128]{1,0:T(8,128)}, f32[8,128]{1,0:T(8,128)S(1)}, u32[]{:S(2)}) copy-start(f32[8,128]{1,0:T(8,128)S(1)} %collective-permute-done.4.refs_9_) | copy-start | bytes 12292
  45.3 9.7 %collective-permute-start.5 = (f32[8,128]{1,0:T(8,128)S(1)}, f32[8,128]{1,0:T(8,128)S(1)}, u32[]{:S(2)}, u32[]{:S(2)}) collective-permute-start(f32[8,128]{1,0:T(8,128)S(1)} %copy-done.4), channel_id=1, source_target_pairs={{0,2},{1,3},{2,0},{3,1},{4,6},{5,7},{6,4},{7,5},{8,10},{9,11},{10,... | collective-permute-start | bytes 12296 | tf_op jit(solution)/shard_map/ppermute | solution.py:481
  55.1 4.3 %copy-start.6 = (f32[8,128]{1,0:T(8,128)}, f32[8,128]{1,0:T(8,128)S(1)}, u32[]{:S(2)}) copy-start(f32[8,128]{1,0:T(8,128)S(1)} %collective-permute-done.5.refs_10_) | copy-start | bytes 12292
  55.1 3.0 %collective-permute-start.6 = (f32[8,128]{1,0:T(8,128)S(1)}, f32[8,128]{1,0:T(8,128)S(1)}, u32[]{:S(2)}, u32[]{:S(2)}) collective-permute-start(f32[8,128]{1,0:T(8,128)S(1)} %copy-done.4), channel_id=1, source_target_pairs={{0,3},{1,2},{2,1},{3,0},{4,7},{5,6},{6,5},{7,4},{8,11},{9,10},{10,... | collective-permute-start | bytes 12296 | tf_op jit(solution)/shard_map/ppermute | solution.py:481
  58.1 1.3 %copy-start.7 = (f32[8,128]{1,0:T(8,128)}, f32[8,128]{1,0:T(8,128)S(1)}, u32[]{:S(2)}) copy-start(f32[8,128]{1,0:T(8,128)S(1)} %collective-permute-done.6.refs_11_) | copy-start | bytes 12292
  58.1 17.7 %collective-permute-start = (bf16[1584,128]{1,0:T(8,128)(2,1)}, bf16[1584,128]{1,0:T(8,128)(2,1)S(1)}, u32[]{:S(2)}, u32[]{:S(2)}) collective-permute-start(bf16[1584,128]{1,0:T(8,128)(2,1)} %get-tuple-element.11), channel_id=1, source_target_pairs={{0,2},{1,3},{2,0},{3,1},{4,6},{5,7},{6,4},{7,5},{8,10},{9,11},{10,... | collective-permute-start | bytes 1216520 | tf_op jit(solution)/shard_map/ppermute | solution.py:481
  71.2 4.6 %copy-start = (f32[8,128]{1,0:T(8,128)S(1)}, f32[8,128]{1,0:T(8,128)}, u32[]{:S(2)}) copy-start(f32[8,128]{1,0:T(8,128)} %get-tuple-element.14.refs_5_.refs_3_) | copy-start | bytes 12292
  71.2 4.6 %copy-start.2 = (s32[128]{0:T(128)S(1)}, s32[128]{0:T(128)}, u32[]{:S(2)}) copy-start(s32[128]{0:T(128)} %param.10) | copy-start | bytes 1540
  76.3 3.2 %collective-permute-start.11 = (f32[1,128]{1,0:T(1,128)S(1)}, f32[1,128]{1,0:T(1,128)S(1)}, u32[]{:S(2)}, u32[]{:S(2)}) collective-permute-start(f32[1,128]{1,0:T(1,128)S(1)} %tail_sum.1), channel_id=1, source_target_pairs={{0,1},{1,0},{2,3},{3,2},{4,5},{5,4},{6,7},{7,6},{8,9},{9,8},{10,11... | collective-permute-start | bytes 1544 | tf_op jit(solution)/shard_map/ppermute | solution.py:481
  76.4 3.6 %collective-permute-start.12 = (f32[1,128]{1,0:T(1,128)S(1)}, f32[1,128]{1,0:T(1,128)S(1)}, u32[]{:S(2)}, u32[]{:S(2)}) collective-permute-start(f32[1,128]{1,0:T(1,128)S(1)} %tail_sum.1), channel_id=1, source_target_pairs={{0,2},{1,3},{2,0},{3,1},{4,6},{5,7},{6,4},{7,5},{8,10},{9,11},{10,... | collective-permute-start | bytes 1544 | tf_op jit(solution)/shard_map/ppermute | solution.py:481
  77.6 3.0 %collective-permute-start.13 = (f32[1,128]{1,0:T(1,128)S(1)}, f32[1,128]{1,0:T(1,128)S(1)}, u32[]{:S(2)}, u32[]{:S(2)}) collective-permute-start(f32[1,128]{1,0:T(1,128)S(1)} %tail_sum.1), channel_id=1, source_target_pairs={{0,3},{1,2},{2,1},{3,0},{4,7},{5,6},{6,5},{7,4},{8,11},{9,10},{10,... | collective-permute-start | bytes 1544 | tf_op jit(solution)/shard_map/ppermute | solution.py:481

commit v7 on v6

--- a/solution.py
+++ b/solution.py
@@ -12,6 +12,7 @@
 LOW = -3e38
 ROWS = 16
 LINES = 8
+SPLITS = 3
 HELD_BYTES = 2.4 * 2**20
 WAYS = 3
 STEP = 544
@@ -409,12 +410,18 @@
     me = lax.axis_index("voc")
     for k, (shift, start, size) in enumerate(parts):
         block = partner(me, shift)
-        reads.append(pltpu.make_async_copy(t_ref.at[block, pl.ds(start, size), :], stops[k], sems.at[k]))
-        reads[-1].start()
-    for k in range(len(parts)):
-        reads[k].wait()
+        span = size // SPLITS if held and size % (SPLITS * ROWS) == 0 else size
+        group = []
+        for n in range(size // span):
+            source = t_ref.at[block, pl.ds(start + n * span, span), :]
+            group.append(pltpu.make_async_copy(source, stops[k].at[pl.ds(n * span, span), :], sems.at[k * SPLITS + n]))
+            group[-1].start()
+        reads.append(group)
+    for k, group in enumerate(reads):
+        for copy in group:
+            copy.wait()
         if not held:
-            writes.append(pltpu.make_async_copy(stops[k], outs[k], sems.at[len(parts) + k]))
+            writes.append(pltpu.make_async_copy(stops[k], outs[k], sems.at[len(parts) * SPLITS + k]))
             writes[-1].start()
     for copy in writes:
         copy.wait()
@@ -435,7 +442,7 @@
             for _, _, size in parts),
         in_specs=[pl.BlockSpec(memory_space=pl.ANY)],
         out_specs=tuple(pl.BlockSpec(memory_space=space) for _ in parts),
-        scratch_shapes=scratch + [pltpu.SemaphoreType.DMA((2 * len(parts),))],
+        scratch_shapes=scratch + [pltpu.SemaphoreType.DMA((len(parts) * (SPLITS + 1),))],
         name="cut",
     )(teacher)
 

time: 81.8 us -> 81.9 us (level)
  transfers between devices with their start and end apart: 14 -> 14, of which waited for: 5 -> 5; matrix products, arithmetic and copies ran while one was open for 7% -> 7% of each run, Pallas kernels for 57% -> 58%
where the time goes in v7:
time: 81.9 us; the launch traced here: 81.2 us
  Pallas kernels  47.2 us (58%)
  starting transfers between devices  14 us (17%)
  waiting for transfers between devices  12.7 us (16%)
  other arithmetic  3.2 us (4%)
  local copies, waits for them, and re-layouts  3.18 us (4%)
  between operations  0.92 us (1%)
    pallas_call x1, Pallas kernels, run_stats(): pl.pallas_call(kernel, out_shape=jax.ShapeDtypeStruct((8, lanes), F32), g...  26.3 us
    pallas_call x2, Pallas kernels, run_chunk(): pl.pallas_call(kernel, out_shape=tuple(out_shape), grid_spec=pltpu.Prefet...  15 us
    ppermute x11, waiting for transfers between devices, swap(): lax.ppermute(value, 'voc', [(i, partner(i, shift)) for i in range(voc_cou...  10.3 us
    ppermute x11, starting transfers between devices, swap(): lax.ppermute(value, 'voc', [(i, partner(i, shift)) for i in range(voc_cou...  7.11 us
    pallas_call x2, Pallas kernels, cut(): pl.pallas_call(kernel, out_shape=tuple((pltpu.VMEM((size, lanes), BF16) i...  4.14 us
    ppermute x2, starting transfers between devices, body(): kept = kept + lax.ppermute(kept, 'tok', pairs)  3.79 us
    ppermute x1, starting transfers between devices, body(): kept = kept + (lax.ppermute(target, 'tok', pairs) >= 0).astype(F32)  3.06 us
    ppermute x2, waiting for transfers between devices, body(): kept = kept + lax.ppermute(kept, 'tok', pairs)  2.38 us
  transfers between devices with their start and end apart: 14, of which 5 were waited for; matrix products, arithmetic and copies ran while one was open for 7% of the time, Pallas kernels for 58%

profile of v7, /device:TPU:0, one launch (start us, length us, event | category | flops | bytes accessed | tf_op | source)
XLA Modules:
  0.0 81.2 jit_solution(7444106480323715458)
XLA Ops:
  0.6 0.0 copy-start.1
  0.6 0.0 copy-start.3
  0.7 3.1 %collective-permute-start.7 = (s32[1,128]{1,0:T(1,128)}, s32[1,128]{1,0:T(1,128)S(1)}, u32[]{:S(2)}, u32[]{:S(2)}) collective-permute-start(s32[1,128]{1,0:T(1,128)} %bitcast.21), channel_id=1, source_target_pairs={{0,4},{4,0},{8,12},{12,8},{16,20},{20,16},{24,28},{28,24},{1,5},{5... | collective-permute-start | bytes 1544 | tf_op jit(solution)/shard_map/ppermute | solution.py:516
  3.7 3.1 %cut.2 = (bf16[3168,128]{1,0:T(8,128)(2,1)}, bf16[3168,128]{1,0:T(8,128)(2,1)}, bf16[1584,128]{1,0:T(8,128)(2,1)}, bf16[4752,128]{1,0:T(8,128)(2,1)}) custom-call(bf16[4,4752,128]{2,1,0:T(8,128)(2,1)} %bitcast.26), custom_call_target="tpu_custom_call" | custom-call | tf_op jit(solution)/shard_map/cut/pallas_call | solution.py:438
  6.8 0.1 collective-permute-start.1
  6.9 1.6 %collective-permute-start.3 = (bf16[3168,128]{1,0:T(8,128)(2,1)}, bf16[3168,128]{1,0:T(8,128)(2,1)}, u32[]{:S(2)}, u32[]{:S(2)}) collective-permute-start(bf16[3168,128]{1,0:T(8,128)(2,1)} %get-tuple-element.13), channel_id=1, source_target_pairs={{0,3},{1,2},{2,1},{3,0},{4,7},{5,6},{6,5},{7,4},{8,11},{9,10},{10,... | collective-permute-start | bytes 2433032 | tf_op jit(solution)/shard_map/ppermute | solution.py:488
  8.5 0.5 collective-permute-start.10
  9.0 0.0 copy-done.3
  9.0 0.3 reshape.46
  9.3 0.1 constant_dynamic-slice_fusion.1
  9.5 0.1 broadcast_in_dim.66
  9.6 0.1 broadcast_in_dim.69
  9.8 0.0 collective-permute-done.7
  9.8 0.0 copy-done.1
  9.8 1.6 %collective-permute-start.8 = (f32[1,128]{1,0:T(1,128)S(1)}, f32[1,128]{1,0:T(1,128)S(1)}, u32[]{:S(2)}, u32[]{:S(2)}) collective-permute-start(f32[1,128]{1,0:T(1,128)S(1)} %fusion.2), channel_id=1, source_target_pairs={{0,8},{4,12},{8,0},{12,4},{16,24},{20,28},{24,16},{28,20},{1,9},{5... | collective-permute-start | bytes 1544 | tf_op jit(solution)/shard_map/ppermute | solution.py:518
  11.4 0.9 %select_select_fusion.refs_2_.refs_6_.refs_3_ = bf16[36,8,528]{2,1,0:T(8,128)(2,1)} fusion(pred[8]{0:T(512)(128)(4,1)S(1)} %get-tuple-element.22, pred[8]{0:T(512)(128)(4,1)S(1)} %get-tuple-element.23, bf16[8]{0:T(256)(128)(2,1)S(1)} %fusion, bf16[36,528]{1,0:T(8,128)(2,1)S(1)} %broadcast_in_dim.69, bf16[36,528]{1,0:T(8,128)(2,1)S(1)} %broadcast_in_dim.66), kind=kLoop, calls=%fused_computation.1 | loop fusion | flops 304128 | bytes 380192 | tf_op jit(solution)/shard_map/jit(_where)/select_n | solution.py:532
  12.3 26.3 %stats.1.refs_8_ = f32[8,128]{1,0:T(8,128)} custom-call(bf16[19008,128]{1,0:T(8,128)(2,1)} %bitcast.27, bf16[19008,128]{1,0:T(8,128)(2,1)} %bitcast.30, bf16[36,8,528]{2,1,0:T(8,128)(2,1)} %select_select_fusion.refs_2_.refs_6_.refs_3_), custom_call_target="tpu_custom_call" | custom-call | tf_op jit(solution)/shard_map/stats/pallas_call | solution.py:156
  38.6 0.0 copy-start.10
  38.7 0.0 copy-start.11
  38.7 0.1 collective-permute-start.4
  38.7 1.1 %cut.3 = bf16[1584,128]{1,0:T(8,128)(2,1)S(1)} custom-call(bf16[4,4752,128]{2,1,0:T(8,128)(2,1)} %bitcast.28), custom_call_target="tpu_custom_call" | custom-call | tf_op jit(solution)/shard_map/cut/pallas_call | solution.py:438
  39.8 0.0 collective-permute-done.8
  39.9 2.2 %collective-permute-start.9 = (f32[1,128]{1,0:T(1,128)S(1)}, f32[1,128]{1,0:T(1,128)S(1)}, u32[]{:S(2)}, u32[]{:S(2)}) collective-permute-start(f32[1,128]{1,0:T(1,128)S(1)} %add.52), channel_id=1, source_target_pairs={{0,16},{4,20},{8,24},{12,28},{16,0},{20,4},{24,8},{28,12},{1,17},{... | collective-permute-start | bytes 1544 | tf_op jit(solution)/shard_map/ppermute | solution.py:518
  42.0 2.4 %collective-permute-done.9 = f32[1,128]{1,0:T(1,128)S(1)} collective-permute-done((f32[1,128]{1,0:T(1,128)S(1)}, f32[1,128]{1,0:T(1,128)S(1)}, u32[]{:S(2)}, u32[]{:S(2)}) %collective-permute-start.9) | collective-permute-done | bytes 544 | tf_op jit(solution)/shard_map/ppermute | solution.py:518
  44.4 0.0 collective-permute-start.2
  44.4 1.0 %dynamic-slice_bitcast_fusion.refs_1_ = bf16[1584,128]{1,0:T(8,128)(2,1)S(1)} fusion(bf16[128,19008]{0,1:T(8,128)(2,1)} %param.9, s32[]{:T(128)S(6)} %select_n.38), kind=kLoop, calls=%fused_computation | loop fusion | bytes 811012 | tf_op jit(solution)/shard_map/dynamic_slice | solution.py:594
  45.4 0.0 collective-permute-done.4.refs_9_
  45.4 0.0 copy-done.4
  45.4 0.0 copy-start.5
  45.5 1.0 %collective-permute-start.5 = (f32[8,128]{1,0:T(8,128)S(1)}, f32[8,128]{1,0:T(8,128)S(1)}, u32[]{:S(2)}, u32[]{:S(2)}) collective-permute-start(f32[8,128]{1,0:T(8,128)S(1)} %copy-done.4), channel_id=1, source_target_pairs={{0,2},{1,3},{2,0},{3,1},{4,6},{5,7},{6,4},{7,5},{8,10},{9,11},{10,... | collective-permute-start | bytes 12296 | tf_op jit(solution)/shard_map/ppermute | solution.py:488
  46.5 0.0 copy-done.8
  46.5 0.0 copy-done.9
  46.5 0.0 copy-done.10
  46.5 0.0 copy-done.11
  46.5 0.5 add_add_fusion.refs_0_
  47.0 8.2 %collective-permute-done.5.refs_10_ = f32[8,128]{1,0:T(8,128)S(1)} collective-permute-done((f32[8,128]{1,0:T(8,128)S(1)}, f32[8,128]{1,0:T(8,128)S(1)}, u32[]{:S(2)}, u32[]{:S(2)}) %collective-permute-start.5) | collective-permute-done | bytes 4128 | tf_op jit(solution)/shard_map/ppermute | solution.py:488
  55.2 0.6 collective-permute-start.6
  55.8 0.8 constant_dynamic-slice_fusion.refs_2_
  56.6 0.5 add.53.refs_12_
  57.1 1.1 %collective-permute-done.6.refs_11_ = f32[8,128]{1,0:T(8,128)S(1)} collective-permute-done((f32[8,128]{1,0:T(8,128)S(1)}, f32[8,128]{1,0:T(8,128)S(1)}, u32[]{:S(2)}, u32[]{:S(2)}) %collective-permute-start.6) | collective-permute-done | bytes 4128 | tf_op jit(solution)/shard_map/ppermute | solution.py:488
  58.2 1.3 %collective-permute-start = (bf16[1584,128]{1,0:T(8,128)(2,1)}, bf16[1584,128]{1,0:T(8,128)(2,1)S(1)}, u32[]{:S(2)}, u32[]{:S(2)}) collective-permute-start(bf16[1584,128]{1,0:T(8,128)(2,1)} %get-tuple-element.11), channel_id=1, source_target_pairs={{0,2},{1,3},{2,0},{3,1},{4,6},{5,7},{6,4},{7,5},{8,10},{9,11},{10,... | collective-permute-start | bytes 1216520 | tf_op jit(solution)/shard_map/ppermute | solution.py:488
  59.5 0.0 collective-permute-done.2.refs_3_
  59.5 0.0 collective-permute-done.3.refs_4_
  59.5 0.0 collective-permute-done.1.refs_2_
  59.5 0.0 copy-done.5
  59.5 0.0 copy-done.6
  59.5 0.0 copy-done.7
  59.5 11.1 %chunk.2 = (bf16[19008,128]{1,0:T(8,128)(2,1)}, f32[16,128]{1,0:T(8,128)}, f32[8,128]{1,0:T(8,128)}) custom-call(s32[36]{0:T(128)} %add_add_fusion.refs_0_, bf16[19008,128]{1,0:T(8,128)(2,1)} %bitcast.29, bf16[4752,128]{1,0:T(8,128)(2,1)S(1)} %collective-permute-done.1.refs_2_, bf16[1584,128]{1,0:T(8,128)(2,1)} %collective-permute-done.2.refs_3_, ...), custom_call_target="tpu_custom_call" | custom-call | tf_op jit(solution)/shard_map/chunk/pallas_call | solution.py:302
  70.7 0.7 slice_bitcast_fusion
  71.3 0.0 collective-permute-done.10.refs_1_
  71.3 3.9 %chunk.3 = (bf16[19008,128]{1,0:T(8,128)(2,1)}, f32[16,128]{1,0:T(8,128)}) custom-call(s32[36]{0:T(128)} %add_add_fusion.refs_0_, bf16[3168,128]{1,0:T(8,128)(2,1)S(1)} %collective-permute-done.10.refs_1_, bf16[19008,128]{1,0:T(8,128)(2,1)} %bitcast.32, ...), custom_call_target="tpu_custom_call", output_to_operand_aliasing={{0}: (7, {})} | custom-call | tf_op jit(solution)/shard_map/chunk/pallas_call | solution.py:302
  75.3 0.7 subtract_reduce_fusion
  76.0 0.0 copy-done
  76.0 0.0 collective-permute-done.refs_0_
  76.0 0.0 copy-done.2
  76.0 0.5 tail_sum.1
  76.5 0.1 collective-permute-start.11
  76.5 1.1 %collective-permute-start.12 = (f32[1,128]{1,0:T(1,128)S(1)}, f32[1,128]{1,0:T(1,128)S(1)}, u32[]{:S(2)}, u32[]{:S(2)}) collective-permute-start(f32[1,128]{1,0:T(1,128)S(1)} %tail_sum.1), channel_id=1, source_target_pairs={{0,2},{1,3},{2,0},{3,1},{4,6},{5,7},{6,4},{7,5},{8,10},{9,11},{10,... | collective-permute-start | bytes 1544 | tf_op jit(solution)/shard_map/ppermute | solution.py:488
  77.7 0.7 collective-permute-start.13
  78.4 1.2 %tail_grad.1 = bf16[19008,128]{1,0:T(8,128)(2,1)} custom-call(bf16[1584,128]{1,0:T(8,128)(2,1)S(1)} %collective-permute-done.refs_0_, bf16[1584,128]{1,0:T(8,128)(2,1)S(1)} %dynamic-slice_bitcast_fusion.refs_1_, bf16[3,8,528]{2,1,0:T(8,128)(2,1)S(1)} %constant_dynamic-slice_fusion.refs_2_, f32[8,128]{1,0:T(8,128)S(1)} %copy-done, ...), custom_call_target="tpu_custom_call", output_to_operand_aliasing={{}: (5, {})} | custom-call | tf_op jit(solution)/shard_map/tail_grad/pallas_call | solution.py:394
  79.6 0.0 collective-permute-done.11
  79.6 0.5 collective-permute-done.12
  80.2 0.5 collective-permute-done.13
  80.7 0.5 add_bitcast_fusion
  (16 shorter events, 0.1 us)
Async XLA Ops:
  0.6 9.2 %copy-start.1 = (s32[128]{0:T(128)S(1)}, s32[128]{0:T(128)}, u32[]{:S(2)}) copy-start(s32[128]{0:T(128)} %param.10) | copy-start | bytes 1540
  0.6 8.4 %copy-start.3 = (s32[76032]{0:T(1024)S(1)}, s32[76032]{0:T(1024)}, u32[]{:S(2)}) copy-start(s32[76032]{0:T(1024)} %param.11) | copy-start | bytes 912388
  0.7 9.1 %collective-permute-start.7 = (s32[1,128]{1,0:T(1,128)}, s32[1,128]{1,0:T(1,128)S(1)}, u32[]{:S(2)}, u32[]{:S(2)}) collective-permute-start(s32[1,128]{1,0:T(1,128)} %bitcast.21), channel_id=1, source_target_pairs={{0,4},{4,0},{8,12},{12,8},{16,20},{20,16},{24,28},{28,24},{1,5},{5... | collective-permute-start | bytes 1544 | tf_op jit(solution)/shard_map/ppermute | solution.py:516
  6.8 52.7 %collective-permute-start.1 = (bf16[4752,128]{1,0:T(8,128)(2,1)}, bf16[4752,128]{1,0:T(8,128)(2,1)S(1)}, u32[]{:S(2)}, u32[]{:S(2)}) collective-permute-start(bf16[4752,128]{1,0:T(8,128)(2,1)} %get-tuple-element.12), channel_id=1, source_target_pairs={{0,1},{1,0},{2,3},{3,2},{4,5},{5,4},{6,7},{7,6},{8,9},{9,8},{10,11... | collective-permute-start | bytes 3649544 | tf_op jit(solution)/shard_map/ppermute | solution.py:488
  6.9 52.6 %collective-permute-start.3 = (bf16[3168,128]{1,0:T(8,128)(2,1)}, bf16[3168,128]{1,0:T(8,128)(2,1)}, u32[]{:S(2)}, u32[]{:S(2)}) collective-permute-start(bf16[3168,128]{1,0:T(8,128)(2,1)} %get-tuple-element.13), channel_id=1, source_target_pairs={{0,3},{1,2},{2,1},{3,0},{4,7},{5,6},{6,5},{7,4},{8,11},{9,10},{10,... | collective-permute-start | bytes 2433032 | tf_op jit(solution)/shard_map/ppermute | solution.py:488
  8.5 62.9 %collective-permute-start.10 = (bf16[3168,128]{1,0:T(8,128)(2,1)}, bf16[3168,128]{1,0:T(8,128)(2,1)S(1)}, u32[]{:S(2)}, u32[]{:S(2)}) collective-permute-start(bf16[3168,128]{1,0:T(8,128)(2,1)} %get-tuple-element.15), channel_id=1, source_target_pairs={{0,2},{1,3},{2,0},{3,1},{4,6},{5,7},{6,4},{7,5},{8,10},{9,11},{10,... | collective-permute-start | bytes 2433032 | tf_op jit(solution)/shard_map/ppermute | solution.py:488
  9.8 30.0 %collective-permute-start.8 = (f32[1,128]{1,0:T(1,128)S(1)}, f32[1,128]{1,0:T(1,128)S(1)}, u32[]{:S(2)}, u32[]{:S(2)}) collective-permute-start(f32[1,128]{1,0:T(1,128)S(1)} %fusion.2), channel_id=1, source_target_pairs={{0,8},{4,12},{8,0},{12,4},{16,24},{20,28},{24,16},{28,20},{1,9},{5... | collective-permute-start | bytes 1544 | tf_op jit(solution)/shard_map/ppermute | solution.py:518
  38.6 6.8 %copy-start.4 = (f32[8,128]{1,0:T(8,128)S(1)}, f32[8,128]{1,0:T(8,128)}, u32[]{:S(2)}) copy-start(f32[8,128]{1,0:T(8,128)} %stats.1.refs_8_) | copy-start | bytes 12292
  38.6 7.8 %copy-start.8 = (s32[36]{0:T(128)S(1)}, s32[36]{0:T(128)}, u32[]{:S(2)}) copy-start(s32[36]{0:T(128)} %constant.56.clone) | copy-start | bytes 436
  38.6 7.9 %copy-start.9 = (s32[36]{0:T(128)S(1)}, s32[36]{0:T(128)}, u32[]{:S(2)}) copy-start(s32[36]{0:T(128)} %constant.57.clone) | copy-start | bytes 436
  38.6 7.8 %copy-start.10 = (s32[36]{0:T(128)S(1)}, s32[36]{0:T(128)}, u32[]{:S(2)}) copy-start(s32[36]{0:T(128)} %constant.58.clone) | copy-start | bytes 436
  38.7 7.8 %copy-start.11 = (s32[36]{0:T(128)S(1)}, s32[36]{0:T(128)}, u32[]{:S(2)}) copy-start(s32[36]{0:T(128)} %constant.59.clone) | copy-start | bytes 436
  38.7 6.8 %collective-permute-start.4 = (f32[8,128]{1,0:T(8,128)}, f32[8,128]{1,0:T(8,128)S(1)}, u32[]{:S(2)}, u32[]{:S(2)}) collective-permute-start(f32[8,128]{1,0:T(8,128)} %stats.1.refs_8_), channel_id=1, source_target_pairs={{0,1},{1,0},{2,3},{3,2},{4,5},{5,4},{6,7},{7,6},{8,9},{9,8},{10,11... | collective-permute-start | bytes 12296 | tf_op jit(solution)/shard_map/ppermute | solution.py:488
  39.9 4.5 %collective-permute-start.9 = (f32[1,128]{1,0:T(1,128)S(1)}, f32[1,128]{1,0:T(1,128)S(1)}, u32[]{:S(2)}, u32[]{:S(2)}) collective-permute-start(f32[1,128]{1,0:T(1,128)S(1)} %add.52), channel_id=1, source_target_pairs={{0,16},{4,20},{8,24},{12,28},{16,0},{20,4},{24,8},{28,12},{1,17},{... | collective-permute-start | bytes 1544 | tf_op jit(solution)/shard_map/ppermute | solution.py:518
  44.4 15.1 %collective-permute-start.2 = (bf16[1584,128]{1,0:T(8,128)(2,1)S(1)}, bf16[1584,128]{1,0:T(8,128)(2,1)}, u32[]{:S(2)}, u32[]{:S(2)}) collective-permute-start(bf16[1584,128]{1,0:T(8,128)(2,1)S(1)} %cut.3), channel_id=1, source_target_pairs={{0,3},{1,2},{2,1},{3,0},{4,7},{5,6},{6,5},{7,4},{8,11},{9,10},{10,... | collective-permute-start | bytes 1216520 | tf_op jit(solution)/shard_map/ppermute | solution.py:488
  45.4 14.1 %copy-start.5 = (f32[8,128]{1,0:T(8,128)}, f32[8,128]{1,0:T(8,128)S(1)}, u32[]{:S(2)}) copy-start(f32[8,128]{1,0:T(8,128)S(1)} %collective-permute-done.4.refs_9_) | copy-start | bytes 12292
  45.5 9.7 %collective-permute-start.5 = (f32[8,128]{1,0:T(8,128)S(1)}, f32[8,128]{1,0:T(8,128)S(1)}, u32[]{:S(2)}, u32[]{:S(2)}) collective-permute-start(f32[8,128]{1,0:T(8,128)S(1)} %copy-done.4), channel_id=1, source_target_pairs={{0,2},{1,3},{2,0},{3,1},{4,6},{5,7},{6,4},{7,5},{8,10},{9,11},{10,... | collective-permute-start | bytes 12296 | tf_op jit(solution)/shard_map/ppermute | solution.py:488
  55.2 4.3 %copy-start.6 = (f32[8,128]{1,0:T(8,128)}, f32[8,128]{1,0:T(8,128)S(1)}, u32[]{:S(2)}) copy-start(f32[8,128]{1,0:T(8,128)S(1)} %collective-permute-done.5.refs_10_) | copy-start | bytes 12292
  55.2 3.0 %collective-permute-start.6 = (f32[8,128]{1,0:T(8,128)S(1)}, f32[8,128]{1,0:T(8,128)S(1)}, u32[]{:S(2)}, u32[]{:S(2)}) collective-permute-start(f32[8,128]{1,0:T(8,128)S(1)} %copy-done.4), channel_id=1, source_target_pairs={{0,3},{1,2},{2,1},{3,0},{4,7},{5,6},{6,5},{7,4},{8,11},{9,10},{10,... | collective-permute-start | bytes 12296 | tf_op jit(solution)/shard_map/ppermute | solution.py:488
  58.2 1.3 %copy-start.7 = (f32[8,128]{1,0:T(8,128)}, f32[8,128]{1,0:T(8,128)S(1)}, u32[]{:S(2)}) copy-start(f32[8,128]{1,0:T(8,128)S(1)} %collective-permute-done.6.refs_11_) | copy-start | bytes 12292
  58.2 17.7 %collective-permute-start = (bf16[1584,128]{1,0:T(8,128)(2,1)}, bf16[1584,128]{1,0:T(8,128)(2,1)S(1)}, u32[]{:S(2)}, u32[]{:S(2)}) collective-permute-start(bf16[1584,128]{1,0:T(8,128)(2,1)} %get-tuple-element.11), channel_id=1, source_target_pairs={{0,2},{1,3},{2,0},{3,1},{4,6},{5,7},{6,4},{7,5},{8,10},{9,11},{10,... | collective-permute-start | bytes 1216520 | tf_op jit(solution)/shard_map/ppermute | solution.py:488
  71.3 4.6 %copy-start = (f32[8,128]{1,0:T(8,128)S(1)}, f32[8,128]{1,0:T(8,128)}, u32[]{:S(2)}) copy-start(f32[8,128]{1,0:T(8,128)} %get-tuple-element.14.refs_5_.refs_3_) | copy-start | bytes 12292
  71.3 4.6 %copy-start.2 = (s32[128]{0:T(128)S(1)}, s32[128]{0:T(128)}, u32[]{:S(2)}) copy-start(s32[128]{0:T(128)} %param.10) | copy-start | bytes 1540
  76.5 3.2 %collective-permute-start.11 = (f32[1,128]{1,0:T(1,128)S(1)}, f32[1,128]{1,0:T(1,128)S(1)}, u32[]{:S(2)}, u32[]{:S(2)}) collective-permute-start(f32[1,128]{1,0:T(1,128)S(1)} %tail_sum.1), channel_id=1, source_target_pairs={{0,1},{1,0},{2,3},{3,2},{4,5},{5,4},{6,7},{7,6},{8,9},{9,8},{10,11... | collective-permute-start | bytes 1544 | tf_op jit(solution)/shard_map/ppermute | solution.py:488
  76.5 3.6 %collective-permute-start.12 = (f32[1,128]{1,0:T(1,128)S(1)}, f32[1,128]{1,0:T(1,128)S(1)}, u32[]{:S(2)}, u32[]{:S(2)}) collective-permute-start(f32[1,128]{1,0:T(1,128)S(1)} %tail_sum.1), channel_id=1, source_target_pairs={{0,2},{1,3},{2,0},{3,1},{4,6},{5,7},{6,4},{7,5},{8,10},{9,11},{10,... | collective-permute-start | bytes 1544 | tf_op jit(solution)/shard_map/ppermute | solution.py:488
  77.7 3.0 %collective-permute-start.13 = (f32[1,128]{1,0:T(1,128)S(1)}, f32[1,128]{1,0:T(1,128)S(1)}, u32[]{:S(2)}, u32[]{:S(2)}) collective-permute-start(f32[1,128]{1,0:T(1,128)S(1)} %tail_sum.1), channel_id=1, source_target_pairs={{0,3},{1,2},{2,1},{3,0},{4,7},{5,6},{6,5},{7,4},{8,11},{9,10},{10,... | collective-permute-start | bytes 1544 | tf_op jit(solution)/shard_map/ppermute | solution.py:488
